TPU v7x, 128 devices: a whole 4x4x4 slice. The times are simulated.
128 devices in a mesh: row: 16 (over y, x_lo, core), col: 8 (over z, x_hi).
Axes of the slice: x: 4 (x_hi: 2, x_lo: 2; x = x_hi * 2 + x_lo), y: 4, z: 4, core: 2. Of those that a mesh axis runs over, the one named last changes fastest.
Arguments:
- schur_rows: float32 [1024, 1024], P('row', 'col'), may hold values from -0.40335507 to 0.40335507
- inverses: float32 [1024, 64, 2048], P('row', None, 'col'), may hold values from -0.75 to 0.75
- coupling: float32 [1024, 2048], P('row'), may hold values from -6 to 6
- selected: int32 [2048], P('col'), may hold values from 0 to 2047, each once
- schur_basis: bfloat16 [49152, 1024], P('row', 'col'), may hold values from -0.1875 to 0.1875
Outputs:
- eigenvectors: bfloat16 [49152, 2048], P('row', 'col')
- solved_slab: float32 [1024, 2048], P('row', 'col')
Inputs may be any that keep to these rules, and one draw needn't show every extreme that they name: `selected`: each of the 2048 indices appears exactly once.
All inputs are finite; a program needn't handle non-finite values.
Results may differ from a plain program's by a relative error of at most 0.0049.
Values may be sent and summed in bfloat16 or wider, within the bound.
No kernel may reach another device: no remote copies, remote signals or barrier semaphores. Data moves between devices by JAX's collectives and lax.ppermute only.
A program may use at most 64 MiB of HBM per device.

v0:
```python
import jax
import jax.numpy as jnp
from jax import lax
from jax.sharding import PartitionSpec as P


def from_root(value, axis, source):
    kept = jnp.where(lax.axis_index(axis) == source, value, 0).astype(value.dtype)
    return lax.psum(kept, axis)


def per_device(schur_rows, inverses, coupling, selected, schur_basis):
    tile_rows = inverses.shape[0]
    column_count = selected.shape[0]
    tile_count = lax.axis_size("row")
    my_row = lax.axis_index("row")
    full_rows = lax.all_gather(schur_rows, "col", axis=1, tiled=True)
    right_side = -jnp.take(coupling, selected, axis=1)

    def apply_inverse(pending):
        return jnp.sum(inverses * pending[None, :, :], axis=1)

    def advance(counter, state_now):
        pending, solved, buffer = state_now
        sender = tile_count - 1 - counter
        is_sender = my_row == sender

        def compute():
            return apply_inverse(pending)

        def nothing():
            return jnp.zeros_like(pending)

        candidate = lax.cond(is_sender, compute, nothing)
        received = from_root(candidate, "row", sender)
        solved = jnp.where(is_sender, received, solved)
        columns = lax.dynamic_slice_in_dim(full_rows, sender * tile_rows, tile_rows, 1)
        pending = pending - jnp.dot(columns, received, precision=lax.Precision.HIGHEST)
        return (pending, solved, buffer)

    buffer_start = jnp.zeros((1,), jnp.float32)
    solved_start = jnp.zeros((tile_rows, column_count), jnp.float32)
    pending, solved, buffer = lax.fori_loop(
        0, tile_count, advance, (right_side, solved_start, buffer_start)
    )
    factors = lax.all_gather(solved.astype(jnp.bfloat16), "row", axis=0, tiled=True)
    eigen_rows = jnp.dot(
        lax.all_gather(schur_basis, "col", axis=1, tiled=True),
        factors,
        preferred_element_type=jnp.float32,
    )
    return (eigen_rows.astype(jnp.bfloat16), solved)


def solution(mesh):
    in_specs = (P("row", "col"), P("row", None, "col"), P("row", None), P("col"), P("row", "col"))
    out_specs = (P("row", "col"), P("row", "col"))
    return jax.shard_map(
        per_device, mesh=mesh, in_specs=in_specs, out_specs=out_specs, check_vma=False
    )
```

profile of v0, /device:TPU:0, one launch (start us, length us, event | category | flops | bytes accessed | tf_op | source)
XLA Modules:
  0.0 1935.2 jit_solution(7254180944652337424)
XLA Ops:
  8.0 0.7 compare_and_fusion
  8.7 0.7 compare_select_fusion
  9.4 36.4 %all_gather.9 = f32[64,1024]{1,0:T(8,128)S(1)} all-gather(f32[64,128]{1,0:T(8,128)} %param.9), channel_id=1, replica_groups=mesh['row'=16,'col'=8] {'col'}, dimensions={1}, use_global_device_ids=true | all-gather | bytes 294912 | tf_op jit(solution)/shard_map/all_gather | solution.py:17
  45.7 1.4 copy.7
  47.1 0.7 gather_fusion
  47.8 0.1 negate_bitcast_fusion
  48.0 0.1 copy.8
  48.0 1779.4 %while.18 = (s32[]{:T(128)}, f32[64,256]{1,0:T(8,128)S(1)}, f32[64,256]{1,0:T(8,128)S(1)}, f32[64,1024]{1,0:T(8,128)S(1)}, s32[]{:T(128)}, /*index=5*/f32[64,64,...) while((s32[]{:T(128)}, f32[64,256]{1,0:T(8,128)S(1)}, ...), condition=%wide.region_5.6_spmd.clone, body=%wide.region_0.5_spmd.clone.sunk | while | flops 14745614 | bytes 5275974 | solution.py:43
  48.2 0.6 broadcast_select_fusion.2
  48.8 111.8 %all-reduce.2.cloned.1.call-done = f32[64,256]{1,0:T(8,128)} async-done(((f32[64,256]{1,0:T(8,128)}), f32[64,256]{1,0:T(8,128)}) %all-reduce.2.cloned.1.call-update) | async-done | bytes 65552 | tf_op jit(solution)/shard_map/while/body/eval_jaxpr/psum | solution.py:9
  160.6 1.1 convolution_subtract_fusion.2
  161.9 0.6 broadcast_select_fusion.2
  162.5 109.4 %all-reduce.2.cloned.1.call-done = f32[64,256]{1,0:T(8,128)} async-done(((f32[64,256]{1,0:T(8,128)}), f32[64,256]{1,0:T(8,128)}) %all-reduce.2.cloned.1.call-update) | async-done | bytes 65552 | tf_op jit(solution)/shard_map/while/body/eval_jaxpr/psum | solution.py:9
  271.9 1.1 convolution_subtract_fusion.2
  273.2 0.6 broadcast_select_fusion.2
  273.9 109.2 %all-reduce.2.cloned.1.call-done = f32[64,256]{1,0:T(8,128)} async-done(((f32[64,256]{1,0:T(8,128)}), f32[64,256]{1,0:T(8,128)}) %all-reduce.2.cloned.1.call-update) | async-done | bytes 65552 | tf_op jit(solution)/shard_map/while/body/eval_jaxpr/psum | solution.py:9
  383.1 1.1 convolution_subtract_fusion.2
  384.3 0.6 broadcast_select_fusion.2
  385.0 108.9 %all-reduce.2.cloned.1.call-done = f32[64,256]{1,0:T(8,128)} async-done(((f32[64,256]{1,0:T(8,128)}), f32[64,256]{1,0:T(8,128)}) %all-reduce.2.cloned.1.call-update) | async-done | bytes 65552 | tf_op jit(solution)/shard_map/while/body/eval_jaxpr/psum | solution.py:9
  493.9 1.1 convolution_subtract_fusion.2
  495.1 0.6 broadcast_select_fusion.2
  495.8 108.9 %all-reduce.2.cloned.1.call-done = f32[64,256]{1,0:T(8,128)} async-done(((f32[64,256]{1,0:T(8,128)}), f32[64,256]{1,0:T(8,128)}) %all-reduce.2.cloned.1.call-update) | async-done | bytes 65552 | tf_op jit(solution)/shard_map/while/body/eval_jaxpr/psum | solution.py:9
  604.7 1.1 convolution_subtract_fusion.2
  605.9 0.6 broadcast_select_fusion.2
  606.6 108.9 %all-reduce.2.cloned.1.call-done = f32[64,256]{1,0:T(8,128)} async-done(((f32[64,256]{1,0:T(8,128)}), f32[64,256]{1,0:T(8,128)}) %all-reduce.2.cloned.1.call-update) | async-done | bytes 65552 | tf_op jit(solution)/shard_map/while/body/eval_jaxpr/psum | solution.py:9
  715.5 1.1 convolution_subtract_fusion.2
  716.7 0.6 broadcast_select_fusion.2
  717.4 109.2 %all-reduce.2.cloned.1.call-done = f32[64,256]{1,0:T(8,128)} async-done(((f32[64,256]{1,0:T(8,128)}), f32[64,256]{1,0:T(8,128)}) %all-reduce.2.cloned.1.call-update) | async-done | bytes 65552 | tf_op jit(solution)/shard_map/while/body/eval_jaxpr/psum | solution.py:9
  826.6 1.1 convolution_subtract_fusion.2
  827.8 0.6 broadcast_select_fusion.2
  828.5 109.2 %all-reduce.2.cloned.1.call-done = f32[64,256]{1,0:T(8,128)} async-done(((f32[64,256]{1,0:T(8,128)}), f32[64,256]{1,0:T(8,128)}) %all-reduce.2.cloned.1.call-update) | async-done | bytes 65552 | tf_op jit(solution)/shard_map/while/body/eval_jaxpr/psum | solution.py:9
  937.7 1.1 convolution_subtract_fusion.2
  938.9 0.6 broadcast_select_fusion.2
  939.6 109.2 %all-reduce.2.cloned.1.call-done = f32[64,256]{1,0:T(8,128)} async-done(((f32[64,256]{1,0:T(8,128)}), f32[64,256]{1,0:T(8,128)}) %all-reduce.2.cloned.1.call-update) | async-done | bytes 65552 | tf_op jit(solution)/shard_map/while/body/eval_jaxpr/psum | solution.py:9
  1048.8 1.1 convolution_subtract_fusion.2
  1050.1 0.6 broadcast_select_fusion.2
  1050.7 108.9 %all-reduce.2.cloned.1.call-done = f32[64,256]{1,0:T(8,128)} async-done(((f32[64,256]{1,0:T(8,128)}), f32[64,256]{1,0:T(8,128)}) %all-reduce.2.cloned.1.call-update) | async-done | bytes 65552 | tf_op jit(solution)/shard_map/while/body/eval_jaxpr/psum | solution.py:9
  1159.6 1.1 convolution_subtract_fusion.2
  1160.9 0.6 broadcast_select_fusion.2
  1161.5 109.4 %all-reduce.2.cloned.1.call-done = f32[64,256]{1,0:T(8,128)} async-done(((f32[64,256]{1,0:T(8,128)}), f32[64,256]{1,0:T(8,128)}) %all-reduce.2.cloned.1.call-update) | async-done | bytes 65552 | tf_op jit(solution)/shard_map/while/body/eval_jaxpr/psum | solution.py:9
  1270.9 1.1 convolution_subtract_fusion.2
  1272.2 0.6 broadcast_select_fusion.2
  1272.9 108.9 %all-reduce.2.cloned.1.call-done = f32[64,256]{1,0:T(8,128)} async-done(((f32[64,256]{1,0:T(8,128)}), f32[64,256]{1,0:T(8,128)}) %all-reduce.2.cloned.1.call-update) | async-done | bytes 65552 | tf_op jit(solution)/shard_map/while/body/eval_jaxpr/psum | solution.py:9
  1381.7 1.1 convolution_subtract_fusion.2
  1383.0 0.6 broadcast_select_fusion.2
  1383.7 109.2 %all-reduce.2.cloned.1.call-done = f32[64,256]{1,0:T(8,128)} async-done(((f32[64,256]{1,0:T(8,128)}), f32[64,256]{1,0:T(8,128)}) %all-reduce.2.cloned.1.call-update) | async-done | bytes 65552 | tf_op jit(solution)/shard_map/while/body/eval_jaxpr/psum | solution.py:9
  1492.9 1.1 convolution_subtract_fusion.2
  1494.1 0.6 broadcast_select_fusion.2
  1494.8 108.9 %all-reduce.2.cloned.1.call-done = f32[64,256]{1,0:T(8,128)} async-done(((f32[64,256]{1,0:T(8,128)}), f32[64,256]{1,0:T(8,128)}) %all-reduce.2.cloned.1.call-update) | async-done | bytes 65552 | tf_op jit(solution)/shard_map/while/body/eval_jaxpr/psum | solution.py:9
  1603.7 1.1 convolution_subtract_fusion.2
  1604.9 0.6 broadcast_select_fusion.2
  1605.6 108.9 %all-reduce.2.cloned.1.call-done = f32[64,256]{1,0:T(8,128)} async-done(((f32[64,256]{1,0:T(8,128)}), f32[64,256]{1,0:T(8,128)}) %all-reduce.2.cloned.1.call-update) | async-done | bytes 65552 | tf_op jit(solution)/shard_map/while/body/eval_jaxpr/psum | solution.py:9
  1714.5 1.1 convolution_subtract_fusion.2
  1715.7 2.8 conditional.3
  1715.7 2.8 multiply_reduce_fusion
  1718.5 0.6 broadcast_select_fusion.2
  1719.2 106.2 %all-reduce.2.cloned.1.call-done = f32[64,256]{1,0:T(8,128)} async-done(((f32[64,256]{1,0:T(8,128)}), f32[64,256]{1,0:T(8,128)}) %all-reduce.2.cloned.1.call-update) | async-done | bytes 65552 | tf_op jit(solution)/shard_map/while/body/eval_jaxpr/psum | solution.py:9
  1825.4 0.9 select_select_fusion.2
  1826.3 1.1 convolution_subtract_fusion.2
  1827.5 0.5 all-gather.2.cloned.1.call-update
  1828.0 19.4 %all_gather.10 = bf16[1024,256]{1,0:T(8,128)(2,1)S(1)} all-gather(bf16[64,256]{1,0:T(8,128)(2,1)S(1)} %convert_element_type.27), channel_id=1, replica_groups=mesh['row'=16,'col'=8] {'row'}, dimensions={0}, use_global_device_ids=true | all-gather | bytes 557056 | tf_op jit(solution)/shard_map/all_gather | solution.py:46
  1847.4 74.5 %all-gather.2.cloned.1.call-done = bf16[3072,1024]{1,0:T(8,128)(2,1)} async-done(((bf16[3072,128]{1,0:T(8,128)(2,1)}), bf16[3072,1024]{1,0:T(8,128)(2,1)}) %all-gather.2.cloned.1.call-update) | async-done | bytes 6291472 | tf_op jit(solution)/shard_map/all_gather | solution.py:48
  1921.9 4.6 fusion.2
  1926.5 1.6 copy.9
  (83 shorter events, 1.8 us)
Async XLA Ops:
  48.1 112.6 %all-reduce.2.cloned.1.call-start = ((), (), s32[]{:S(2)}) async-start(), calls=%async_computation.1 | async-start | bytes 131072 | tf_op jit(solution)/shard_map/while/body/eval_jaxpr/psum | solution.py:9
  161.8 110.2 %all-reduce.2.cloned.1.call-start = ((), (), s32[]{:S(2)}) async-start(), calls=%async_computation.1 | async-start | bytes 131072 | tf_op jit(solution)/shard_map/while/body/eval_jaxpr/psum | solution.py:9
  273.1 110.0 %all-reduce.2.cloned.1.call-start = ((), (), s32[]{:S(2)}) async-start(), calls=%async_computation.1 | async-start | bytes 131072 | tf_op jit(solution)/shard_map/while/body/eval_jaxpr/psum | solution.py:9
  384.2 109.6 %all-reduce.2.cloned.1.call-start = ((), (), s32[]{:S(2)}) async-start(), calls=%async_computation.1 | async-start | bytes 131072 | tf_op jit(solution)/shard_map/while/body/eval_jaxpr/psum | solution.py:9
  495.0 109.7 %all-reduce.2.cloned.1.call-start = ((), (), s32[]{:S(2)}) async-start(), calls=%async_computation.1 | async-start | bytes 131072 | tf_op jit(solution)/shard_map/while/body/eval_jaxpr/psum | solution.py:9
  605.8 109.6 %all-reduce.2.cloned.1.call-start = ((), (), s32[]{:S(2)}) async-start(), calls=%async_computation.1 | async-start | bytes 131072 | tf_op jit(solution)/shard_map/while/body/eval_jaxpr/psum | solution.py:9
  716.6 110.0 %all-reduce.2.cloned.1.call-start = ((), (), s32[]{:S(2)}) async-start(), calls=%async_computation.1 | async-start | bytes 131072 | tf_op jit(solution)/shard_map/while/body/eval_jaxpr/psum | solution.py:9
  827.7 110.0 %all-reduce.2.cloned.1.call-start = ((), (), s32[]{:S(2)}) async-start(), calls=%async_computation.1 | async-start | bytes 131072 | tf_op jit(solution)/shard_map/while/body/eval_jaxpr/psum | solution.py:9
  938.8 110.0 %all-reduce.2.cloned.1.call-start = ((), (), s32[]{:S(2)}) async-start(), calls=%async_computation.1 | async-start | bytes 131072 | tf_op jit(solution)/shard_map/while/body/eval_jaxpr/psum | solution.py:9
  1050.0 109.6 %all-reduce.2.cloned.1.call-start = ((), (), s32[]{:S(2)}) async-start(), calls=%async_computation.1 | async-start | bytes 131072 | tf_op jit(solution)/shard_map/while/body/eval_jaxpr/psum | solution.py:9
  1160.8 110.2 %all-reduce.2.cloned.1.call-start = ((), (), s32[]{:S(2)}) async-start(), calls=%async_computation.1 | async-start | bytes 131072 | tf_op jit(solution)/shard_map/while/body/eval_jaxpr/psum | solution.py:9
  1272.1 109.6 %all-reduce.2.cloned.1.call-start = ((), (), s32[]{:S(2)}) async-start(), calls=%async_computation.1 | async-start | bytes 131072 | tf_op jit(solution)/shard_map/while/body/eval_jaxpr/psum | solution.py:9
  1382.9 110.0 %all-reduce.2.cloned.1.call-start = ((), (), s32[]{:S(2)}) async-start(), calls=%async_computation.1 | async-start | bytes 131072 | tf_op jit(solution)/shard_map/while/body/eval_jaxpr/psum | solution.py:9
  1494.0 109.6 %all-reduce.2.cloned.1.call-start = ((), (), s32[]{:S(2)}) async-start(), calls=%async_computation.1 | async-start | bytes 131072 | tf_op jit(solution)/shard_map/while/body/eval_jaxpr/psum | solution.py:9
  1604.8 109.6 %all-reduce.2.cloned.1.call-start = ((), (), s32[]{:S(2)}) async-start(), calls=%async_computation.1 | async-start | bytes 131072 | tf_op jit(solution)/shard_map/while/body/eval_jaxpr/psum | solution.py:9
  1715.6 109.8 %all-reduce.2.cloned.1.call-start = ((), (), s32[]{:S(2)}) async-start(), calls=%async_computation.1 | async-start | bytes 131072 | tf_op jit(solution)/shard_map/while/body/eval_jaxpr/psum | solution.py:9
  1827.4 99.1 %copy-start = (f32[64,256]{1,0:T(8,128)}, f32[64,256]{1,0:T(8,128)S(1)}, u32[]{:S(2)}) copy-start(f32[64,256]{1,0:T(8,128)S(1)} %get-tuple-element.201) | copy-start | bytes 196612
  1827.4 94.5 %all-gather.2.cloned.1.call-start = ((), (), s32[]{:S(2)}) async-start(), calls=%async_computation | async-start | bytes 7077888 | tf_op jit(solution)/shard_map/all_gather | solution.py:48
Sparse Core Ops, SparseCore 0:
  51.9 108.6 all-reduce.1
  165.6 106.2 all-reduce.1
  276.9 106.0 all-reduce.1
  387.7 106.0 all-reduce.1
  498.5 106.0 all-reduce.1
  609.4 106.0 all-reduce.1
  720.5 106.0 all-reduce.1
  831.6 106.0 all-reduce.1
  942.7 106.0 all-reduce.1
  1053.5 106.0 all-reduce.1
  1164.6 106.2 all-reduce.1
  1275.6 106.0 all-reduce.1
  1386.7 106.0 all-reduce.1
  1497.5 106.0 all-reduce.1
  1608.3 106.0 all-reduce.1
  1719.3 106.0 all-reduce.1
Sparse Core Ops, SparseCore 1:
  1830.1 91.8 all-gather.1
where the time goes:
time: 1940 us
  waiting for transfers between devices  1820 us (94%)
  blocking collectives  55.8 us (3%)
  matrix products  22.4 us (1%)
    psum x16, waiting for transfers between devices, from_root(): return lax.psum(kept, axis)  1740 us
    all_gather x1, waiting for transfers between devices, per_device(): lax.all_gather(schur_basis, 'col', axis=1, tiled=True)  74.5 us
  transfers between devices with their start and end apart: 17, of which 17 were waited for; matrix products, arithmetic and copies ran while one was open for 0% of the time, Pallas kernels for 0%

commit v1 on v0

v1 whole, which is shorter than its diff:
```python
import functools

import jax
import jax.numpy as jnp
from jax import lax
from jax.experimental import pallas as pl
from jax.experimental.pallas import tpu as pltpu
from jax.sharding import PartitionSpec as P


NB = 64
LANES = 128
PAIR = 2 * NB
CHIPS = 8
HIGHEST = lax.Precision.HIGHEST
F32 = jnp.float32
BF16 = jnp.bfloat16


SWAP = [(i, i ^ 1) for i in range(2 * CHIPS)]
XLO = [(i, i ^ 2) for i in range(2 * CHIPS)]
XHI = [(i, i ^ 1) for i in range(CHIPS)]

VMEM = pl.BlockSpec(memory_space=pltpu.VMEM)
HBM = pl.BlockSpec(memory_space=pltpu.MemorySpace.HBM)


def shift(values, by):
    return [(i, (i + by) % values) for i in range(values)]


def moves(step):
    chip = CHIPS - 1 - step
    result = []
    for least in (1, 2, 3):
        chips = [(chip + k, chip - least - k) for k in range(CHIPS if least > 1 else 1)]
        chips = [(a, b) for a, b in chips if a < CHIPS and b >= 0]
        result.append([(2 * a + core, 2 * b + core) for a, b in chips for core in (0, 1)])
    return result


def wrap(value, size):
    return lax.rem(value + 2 * size, size)


def core_lanes(core):
    return pl.ds(pl.multiple_of(core * LANES, LANES), LANES)


def setup_kernel(coupling, selected, schur_rows, inv, inv_mine, inv_send, small, rhs_mine, sem):
    core = lax.rem(lax.axis_index("row"), 2)
    send = pltpu.make_async_copy(inv.at[:, :, core_lanes(1 - core)], inv_send, sem.at[0])
    mine = pltpu.make_async_copy(inv.at[:, :, core_lanes(core)], inv_mine, sem.at[1])
    send.start()
    mine.start()
    candidates, columns = coupling.shape[1], selected.shape[1]
    piece = 256
    total = jnp.zeros((3 * NB, columns), F32)
    for first in range(0, candidates, piece):
        part = coupling[:, first : first + piece]
        high = part.astype(BF16)
        rest = part - high.astype(F32)
        middle = rest.astype(BF16)
        low = (rest - middle.astype(F32)).astype(BF16)
        index = lax.broadcasted_iota(jnp.int32, (piece, columns), 0) + first
        chosen = jnp.where(index == selected[...], 1.0, 0.0).astype(BF16)
        total += jnp.dot(jnp.concatenate([high, middle, low], axis=0), chosen, preferred_element_type=F32)
    rhs = -(total[:NB] + total[NB : 2 * NB] + total[2 * NB :])
    left, right = rhs[:, :LANES], rhs[:, LANES:]
    rhs_mine[...] = jnp.where(core == 0, left, right)
    small[:NB, :] = schur_rows[...]
    small[NB:, :] = jnp.where(core == 0, right, left)
    send.wait()
    mine.wait()


def setup(coupling, selected, schur_rows, inverses):
    half = pltpu.VMEM((NB, NB, LANES), F32)
    return pl.pallas_call(
        setup_kernel,
        out_shape=(half, half, pltpu.VMEM((PAIR, LANES), F32), pltpu.VMEM((NB, LANES), F32)),
        in_specs=[VMEM, VMEM, VMEM, HBM],
        out_specs=(VMEM,) * 4,
        scratch_shapes=[pltpu.SemaphoreType.DMA((2,))],
        compiler_params=pltpu.CompilerParams(vmem_limit_bytes=16 << 20),
        name="setup",
    )(coupling, selected[None, :], schur_rows, pltpu.with_memory_space_constraint(inverses, pltpu.HBM))


def apply_inverse(inv, pending):
    parts = [jnp.sum(inv[pl.ds(8 * g, 8)] * pending[None], axis=1) for g in range(NB // 8)]
    return jnp.concatenate(parts, axis=0)


def step_kernel(step, names, *refs):
    ref = dict(zip(names, refs))
    if step == 0:
        get_inv = pltpu.make_async_copy(ref["inv_from"], ref["inv_other"], refs[-1])
        get_inv.start()
    row, col = lax.axis_index("row"), lax.axis_index("col")
    me, core = row // 2, lax.rem(row, 2)
    chip = CHIPS - 1 - step
    active = me == chip
    inv_mine, inv_other, pend, x = ref["inv_mine"], ref["inv_other"], ref["pend"], ref["x"]
    tiles = ref["tiles"] if step else ref["tiles_out"]

    def tile(source):
        ahead = wrap(col // 2 - source // 2, CHIPS // 2)
        across = lax.rem(col + source, 2)
        return tiles[2 * ahead + across]

    def product(source, value):
        return jnp.dot(tile(source), value, precision=HIGHEST, preferred_element_type=F32)

    if step == 0:
        for index, name in enumerate(("t0", "t1", "t2", "t3")):
            tiles[pl.ds(2 * index, 2)] = ref[name][...]
        pend[pl.ds(pl.multiple_of(core * NB, NB), NB), :] = ref["rhs_mine"][...]
        pend[pl.ds(pl.multiple_of((1 - core) * NB, NB), NB), :] = ref["small"][NB:, :]
        get_inv.wait()
    else:
        pend[...] = ref["pend_in"][...]

    @pl.when(active)
    def _():
        if step:
            total = pend[...] - product(chip + 1, ref["near"][...])
            if step > 1:
                total -= product(chip + 2, ref["far2"][...])
            pend[...] = total

        def solve(odd, even):
            x_odd = apply_inverse(odd, pend[NB:, :])
            x[NB:, :] = x_odd
            padded = jnp.concatenate([jnp.zeros_like(x_odd), x_odd], axis=0)
            within = jnp.dot(tile(me)[:NB, :], padded, precision=HIGHEST, preferred_element_type=F32)
            x[:NB, :] = apply_inverse(even, pend[:NB, :] - within)

        @pl.when(core == 1)
        def _():
            solve(inv_mine, inv_other)

        @pl.when(core == 0)
        def _():
            solve(inv_other, inv_mine)

    @pl.when(jnp.logical_not(active))
    def _():
        x[...] = ref["x_in"][...] if step else jnp.zeros_like(x)
        if step > 1:
            from2, from3 = 2 * chip + 2 - me, 2 * chip + 1 - me

            @pl.when(jnp.logical_and(me < chip, from2 < CHIPS))
            def _():
                pend[...] -= product(from2, ref["far2"][...])

            if "far3" in ref:

                @pl.when(jnp.logical_and(me < chip, from3 < CHIPS))
                def _():
                    pend[...] -= product(from3, ref["far3"][...])

    if step == CHIPS - 1:
        ref["factor"][...] = x[...].astype(BF16)
        ref["mine"][...] = x[pl.ds(pl.multiple_of(core * NB, NB), NB), :]
        ref["theirs"][...] = x[pl.ds(pl.multiple_of((1 - core) * NB, NB), NB), :]


def solve_step(step, operands):
    block = jax.ShapeDtypeStruct((PAIR, LANES), F32)
    outs = {"pend": block, "x": block}
    if step == 0:
        outs["tiles_out"] = pltpu.VMEM((CHIPS, PAIR, LANES), F32)
        outs["inv_other"] = pltpu.VMEM((NB, NB, LANES), F32)
    if step == CHIPS - 1:
        outs["factor"] = jax.ShapeDtypeStruct((PAIR, LANES), BF16)
        outs["mine"] = outs["theirs"] = jax.ShapeDtypeStruct((NB, LANES), F32)
    names = list(operands) + list(outs)
    call = pl.pallas_call(
        functools.partial(step_kernel, step, names),
        out_shape=tuple(outs.values()),
        in_specs=[HBM if name == "inv_from" else VMEM for name in operands],
        out_specs=(VMEM,) * len(outs),
        scratch_shapes=[] if step else [pltpu.SemaphoreType.DMA],
        compiler_params=pltpu.CompilerParams(vmem_limit_bytes=16 << 20),
        cost_estimate=pl.CostEstimate(flops=8_000_000, bytes_accessed=5_000_000, transcendentals=0),
        name="solve_step",
    )
    result = call(*operands.values())
    return dict(zip(outs, result))


BLOCK = 512


def stack_kernel(a, b, c, d, out):
    for index, part in enumerate((a, b, c, d)):
        out[index] = part[...]


def stack4(*parts):
    return pl.pallas_call(
        stack_kernel,
        out_shape=jax.ShapeDtypeStruct((4,) + parts[0].shape, parts[0].dtype),
        in_specs=[VMEM] * 4,
        out_specs=VMEM,
        compiler_params=pltpu.CompilerParams(vmem_limit_bytes=8 << 20),
        name="stack4",
    )(*parts)


def product_kernel(same, same_swap, cross, cross_swap, own, h, zp1, zp2, zm1, zm2, z2, z2x, out, x_all):
    row, col = lax.axis_index("row"), lax.axis_index("col")
    core, xlo, y = lax.rem(row, 2), lax.rem(row // 2, 2), row // 4

    @pl.when(pl.program_id(0) == 0)
    def _():
        for back in range(4):
            level = wrap(y - back, 4)
            x_all[2 * level + xlo, :, core_lanes(core)] = same[back]
            x_all[2 * level + xlo, :, core_lanes(1 - core)] = same_swap[back]
            x_all[2 * level + 1 - xlo, :, core_lanes(core)] = cross[back]
            x_all[2 * level + 1 - xlo, :, core_lanes(1 - core)] = cross_swap[back]

    def pair(left, right, by):
        source = wrap(col + by, CHIPS)
        other = source + 1 - 2 * lax.rem(source, 2)
        lhs = jnp.concatenate([left[...], right[...]], axis=1)
        rhs = jnp.concatenate([x_all[source], x_all[other]], axis=0)
        return jnp.dot(lhs, rhs, preferred_element_type=F32)

    total = pair(own, h, 0) + pair(zp1, zp2, -2) + pair(zm1, zm2, 2) + pair(z2, z2x, 4)
    out[...] = total.astype(out.dtype)


def back_transform(factors, shards):
    rows = shards[0].shape[0]
    block = pl.BlockSpec((BLOCK, LANES), lambda i: (i, 0))
    resident = pl.BlockSpec((4, PAIR, LANES), lambda i: (0, 0, 0))
    return pl.pallas_call(
        product_kernel,
        grid=(rows // BLOCK,),
        out_shape=jax.ShapeDtypeStruct((rows, 2 * LANES), BF16),
        in_specs=[resident] * 4 + [block] * 8,
        out_specs=pl.BlockSpec((BLOCK, 2 * LANES), lambda i: (i, 0)),
        scratch_shapes=[pltpu.VMEM((CHIPS, PAIR, 2 * LANES), BF16)],
        compiler_params=pltpu.CompilerParams(vmem_limit_bytes=16 << 20),
        cost_estimate=pl.CostEstimate(flops=2 * rows * 1024 * 256, bytes_accessed=8_000_000, transcendentals=0),
        name="back_transform",
    )(*factors, *shards)


def per_device(schur_rows, inverses, coupling, selected, schur_basis):
    is_even = lax.axis_index("row") % 2 == 0

    def col_shift(value, by):
        return lax.ppermute(value, "col", shift(CHIPS, by))

    def row_move(value, pairs):
        return lax.ppermute(value, "row", pairs)

    def across(value):
        return lax.ppermute(value, "col", XHI)

    def tile_move(value, name, moved):
        pairs = []
        for row in range(2 * CHIPS):
            for col in range(CHIPS):
                last = col if name == "tx" else col | 1
                if last >= row // 2:
                    pairs.append((row * CHIPS + col, row * CHIPS + moved(col)))
        return lax.ppermute(value, ("row", "col"), pairs)

    inv_mine, inv_send, small, rhs_mine = setup(coupling, selected, schur_rows, inverses)
    inv_other = row_move(inv_send, SWAP)
    small = row_move(small, SWAP)
    t_other = small[:NB]
    t_pair = jnp.where(is_even, jnp.concatenate([schur_rows, t_other]), jnp.concatenate([t_other, schur_rows]))
    t0 = jnp.stack([t_pair, tile_move(t_pair, "tx", lambda c: c ^ 1)])
    t1, t2, t3 = [tile_move(t0, f"tz{j}", lambda c, j=j: (c + 2 * j) % CHIPS) for j in (1, 2, 3)]

    zp1, zm1 = col_shift(schur_basis, 2), col_shift(schur_basis, -2)
    z2, h = col_shift(schur_basis, 4), across(schur_basis)

    received = {"small": small, "t0": t0, "t1": t1, "t2": t2, "t3": t3, "inv_from": inv_other}
    state = solve_step(0, {"rhs_mine": rhs_mine, "inv_mine": inv_mine, **received})
    kept = {"inv_mine": inv_mine, "inv_other": state["inv_other"], "tiles": state["tiles_out"]}
    late = {}
    for step in range(1, CHIPS):
        near, far2, far3 = moves(step - 1)
        operands = {"pend_in": state["pend"], "x_in": state["x"], "near": row_move(state["x"], near)}
        operands.update(late)
        late = {name: row_move(state["x"], pairs) for name, pairs in (("far2", far2), ("far3", far3)) if pairs}
        state = solve_step(step, {**operands, **kept})
        if step == 3:
            h, _ = lax.optimization_barrier((h, state["x"]))
            zp2, zm2 = col_shift(h, 2), col_shift(h, -2)
        if step == 4:
            z2, _ = lax.optimization_barrier((z2, state["x"]))
            z2x = across(z2)

    factor = state["factor"]
    same = stack4(factor, *[row_move(factor, shift(2 * CHIPS, 4 * j)) for j in (1, 2, 3)])
    cross = row_move(same, XLO)
    same_swap = row_move(same, SWAP)
    cross_swap = row_move(cross, SWAP)
    eigen_rows = back_transform((same, same_swap, cross, cross_swap), (schur_basis, h, zp1, zp2, zm1, zm2, z2, z2x))

    mine, theirs = state["mine"], row_move(state["theirs"], SWAP)
    solved = jnp.where(is_even, jnp.concatenate([mine, theirs], axis=1), jnp.concatenate([theirs, mine], axis=1))
    return (eigen_rows, solved)


def solution(mesh):
    in_specs = (P("row", "col"), P("row", None, "col"), P("row", None), P("col"), P("row", "col"))
    out_specs = (P("row", "col"), P("row", "col"))
    return jax.shard_map(per_device, mesh=mesh, in_specs=in_specs, out_specs=out_specs, check_vma=False)
```

time: 1940 us -> 130 us (0.07)
  waiting for transfers between devices: 1820 us -> 60.4 us
  blocking collectives: 55.8 us -> 0 us
  starting transfers between devices: 0.7 us -> 51.5 us
  matrix products: 22.4 us -> 0 us
    psum x16 -> x0, waiting for transfers between devices: 1740 us -> none  [from_root(): return lax.psum(kept, axis)]
    all_gather x1 -> x0, waiting for transfers between devices: 74.5 us -> none  [per_device(): lax.all_gather(schur_basis, 'col', axis=1, tiled=True)]
    ppermute x0 -> x38, waiting for transfers between devices: none -> 60.4 us  [the longest x27 41.4 us: row_move(): return lax.ppermute(value, 'row', pairs)]
    all_gather x2 -> x0, blocking collectives: 55.8 us -> none  [the longest x1 36.4 us: per_device(): full_rows = lax.all_gather(schur_rows, 'col', axis=1, tiled=True)]
    ppermute x0 -> x38, starting transfers between devices: none -> 51.5 us  [the longest x27 20.7 us: row_move(): return lax.ppermute(value, 'row', pairs)]
    dot_general x17 -> x0, matrix products: 22.4 us -> none  [the longest x16 17.8 us: advance(): jnp.dot(columns, received, precision=lax.Precision.HIGHEST)]
  transfers between devices with their start and end apart: 17 -> 38, of which waited for: 17 -> 13; matrix products, arithmetic and copies ran while one was open for 0% -> 1% of each run, Pallas kernels for 0% -> 3%
where the time goes in v1:
time: 130 us; the launch traced here: 128 us
  waiting for transfers between devices  60.4 us (46%)
  starting transfers between devices  51.5 us (40%)
  Pallas kernels  12.3 us (9%)
  local copies, waits for them, and re-layouts  2.48 us (2%)
    ppermute x27, waiting for transfers between devices, row_move(): return lax.ppermute(value, 'row', pairs)  41.4 us
    ppermute x27, starting transfers between devices, row_move(): return lax.ppermute(value, 'row', pairs)  20.7 us
    ppermute x4, waiting for transfers between devices, tile_move(): return lax.ppermute(value, ('row', 'col'), pairs)  18.9 us
    ppermute x4, starting transfers between devices, tile_move(): return lax.ppermute(value, ('row', 'col'), pairs)  14.9 us
    ppermute x5, starting transfers between devices, col_shift(): return lax.ppermute(value, 'col', shift(CHIPS, by))  10.2 us
    ppermute x2, starting transfers between devices, across(): return lax.ppermute(value, 'col', XHI)  5.75 us
    pallas_call x8, Pallas kernels, solve_step(): result = call(*operands.values())  4.43 us
    pallas_call x1, Pallas kernels, back_transform(): pl.pallas_call(product_kernel, grid=(rows // BLOCK,), out_shape=jax.Shape...  4.07 us
  transfers between devices with their start and end apart: 38, of which 13 were waited for; matrix products, arithmetic and copies ran while one was open for 1% of the time, Pallas kernels for 3%

profile of v1, /device:TPU:0, one launch (start us, length us, event | category | flops | bytes accessed | tf_op | source)
XLA Modules:
  0.0 128.5 jit_solution(5769454514272985120)
XLA Ops:
  0.6 1.0 copy-done.1
  1.7 0.8 copy-done.2
  2.4 0.7 copy-done.4
  3.1 3.8 %setup.1 = (f32[64,64,128]{2,1,0:T(8,128)S(1)}, f32[64,64,128]{2,1,0:T(8,128)}, f32[128,128]{1,0:T(8,128)S(1)}, f32[64,128]{1,0:T(8,128)S(1)}) custom-call(f32[64,2048]{1,0:T(8,128)S(1)} %copy-done.1, s32[1,256]{1,0:T(1,128)S(1)} %bitcast.6, f32[64,128]{1,0:T(8,128)S(1)} %copy-done.2, f32[64,64,256]{2,1,0:T(8,128)} %inv.1), custom_call_target="tpu_custom_call" | custom-call | tf_op jit(solution)/shard_map/setup/pallas_call | solution.py:79
  7.0 0.1 collective-permute-start.5
  7.1 0.5 collective-permute-start
  7.6 4.0 %collective-permute-done.refs_2_ = f32[128,128]{1,0:T(8,128)S(1)} collective-permute-done((f32[128,128]{1,0:T(8,128)S(1)}, f32[128,128]{1,0:T(8,128)S(1)}, u32[]{:S(2)}, u32[]{:S(2)}) %collective-permute-start) | collective-permute-done | bytes 65568 | tf_op jit(solution)/shard_map/ppermute | solution.py:260
  11.6 5.0 %collective-permute-start.1 = (f32[128,128]{1,0:T(8,128)S(1)}, f32[128,128]{1,0:T(8,128)S(1)}, u32[]{:S(2)}, u32[]{:S(2)}) collective-permute-start(f32[128,128]{1,0:T(8,128)S(1)} %maximum_select_fusion.1), channel_id=1, source_target_pairs={{0,1},{1,0},{2,3},{3,2},{4,5},{5,4},{6,7},{7,6},{8,9},{9,8},{10,11... | collective-permute-start | bytes 196616 | tf_op jit(solution)/shard_map/ppermute | solution.py:272
  16.6 2.6 %collective-permute-done.1 = f32[128,128]{1,0:T(8,128)S(1)} collective-permute-done((f32[128,128]{1,0:T(8,128)S(1)}, f32[128,128]{1,0:T(8,128)S(1)}, u32[]{:S(2)}, u32[]{:S(2)}) %collective-permute-start.1) | collective-permute-done | bytes 65568 | tf_op jit(solution)/shard_map/ppermute | solution.py:272
  19.3 3.9 %collective-permute-start.2 = (f32[2,128,128]{2,1,0:T(8,128)S(1)}, f32[2,128,128]{2,1,0:T(8,128)S(1)}, u32[]{:S(2)}, u32[]{:S(2)}) collective-permute-start(f32[2,128,128]{2,1,0:T(8,128)S(1)} %pad_maximum_fusion.refs_3_), channel_id=1, source_target_pairs={{0,2},{1,3},{2,4},{3,5},{4,6},{5,7},{6,0},{7,1},{8,10},{9,11},{10,... | collective-permute-start | bytes 393224 | tf_op jit(solution)/shard_map/ppermute | solution.py:272
  23.2 3.7 %collective-permute-start.35 = (bf16[3072,128]{1,0:T(8,128)(2,1)S(1)}, bf16[3072,128]{1,0:T(8,128)(2,1)S(1)}, u32[]{:S(2)}, u32[]{:S(2)}) collective-permute-start(bf16[3072,128]{1,0:T(8,128)(2,1)S(1)} %copy-done), channel_id=1, source_target_pairs={{0,4},{1,5},{2,6},{3,7},{4,0},{5,1},{6,2},{7,3},{8,12},{9,13},{10,... | collective-permute-start | bytes 2359304 | tf_op jit(solution)/shard_map/ppermute | solution.py:257
  26.9 3.0 %collective-permute-start.30 = (bf16[3072,128]{1,0:T(8,128)(2,1)S(1)}, bf16[3072,128]{1,0:T(8,128)(2,1)S(1)}, u32[]{:S(2)}, u32[]{:S(2)}) collective-permute-start(bf16[3072,128]{1,0:T(8,128)(2,1)S(1)} %copy-done), channel_id=1, source_target_pairs={{0,1},{1,0},{2,3},{3,2},{4,5},{5,4},{6,7},{7,6},{8,9},{9,8},{10,11... | collective-permute-start | bytes 2359304 | tf_op jit(solution)/shard_map/ppermute | solution.py:263
  29.9 2.0 %collective-permute-start.3 = (f32[2,128,128]{2,1,0:T(8,128)S(1)}, f32[2,128,128]{2,1,0:T(8,128)S(1)}, u32[]{:S(2)}, u32[]{:S(2)}) collective-permute-start(f32[2,128,128]{2,1,0:T(8,128)S(1)} %pad_maximum_fusion.refs_3_), channel_id=1, source_target_pairs={{0,4},{1,5},{2,6},{3,7},{4,0},{5,1},{6,2},{7,3},{8,12},{9,13},{10,... | collective-permute-start | bytes 393224 | tf_op jit(solution)/shard_map/ppermute | solution.py:272
  31.9 0.0 collective-permute-done.2.refs_4_
  31.9 3.9 %collective-permute-start.4 = (f32[2,128,128]{2,1,0:T(8,128)S(1)}, f32[2,128,128]{2,1,0:T(8,128)S(1)}, u32[]{:S(2)}, u32[]{:S(2)}) collective-permute-start(f32[2,128,128]{2,1,0:T(8,128)S(1)} %pad_maximum_fusion.refs_3_), channel_id=1, source_target_pairs={{0,6},{1,7},{2,0},{3,1},{4,2},{5,3},{6,4},{7,5},{8,14},{9,15},{10,... | collective-permute-start | bytes 393224 | tf_op jit(solution)/shard_map/ppermute | solution.py:272
  35.8 13.0 %collective-permute-done.3.refs_5_ = f32[2,128,128]{2,1,0:T(8,128)S(1)} collective-permute-done((f32[2,128,128]{2,1,0:T(8,128)S(1)}, f32[2,128,128]{2,1,0:T(8,128)S(1)}, u32[]{:S(2)}, u32[]{:S(2)}) %collective-permute-start.3) | collective-permute-done | bytes 131104 | tf_op jit(solution)/shard_map/ppermute | solution.py:272
  48.8 3.3 %collective-permute-done.4.refs_6_ = f32[2,128,128]{2,1,0:T(8,128)S(1)} collective-permute-done((f32[2,128,128]{2,1,0:T(8,128)S(1)}, f32[2,128,128]{2,1,0:T(8,128)S(1)}, u32[]{:S(2)}, u32[]{:S(2)}) %collective-permute-start.4) | collective-permute-done | bytes 131104 | tf_op jit(solution)/shard_map/ppermute | solution.py:272
  52.1 0.0 collective-permute-done.5.refs_7_
  52.1 1.6 %solve_step.8 = (f32[128,128]{1,0:T(8,128)S(1)}, f32[128,128]{1,0:T(8,128)S(1)}, f32[8,128,128]{2,1,0:T(8,128)S(1)}, f32[64,64,128]{2,1,0:T(8,128)S(1)}) custom-call(f32[64,128]{1,0:T(8,128)S(1)} %get-tuple-element.27.refs_0_, f32[64,64,128]{2,1,0:T(8,128)S(1)} %get-tuple-element.28.refs_1_.refs_3_.refs_5_.refs_4_, ...), custom_call_target="tpu_custom_call" | custom-call | flops 8000000 | bytes 5000000 | tf_op jit(solution)/shard_map/solve_step/pallas_call | solution.py:189
  53.7 0.7 collective-permute-start.6
  54.4 0.7 collective-permute-start.8
  55.1 0.7 collective-permute-start.9
  55.8 0.7 collective-permute-start.7
  56.5 0.0 collective-permute-done.8.refs_3_
  56.5 0.7 collective-permute-start.11
  57.1 0.0 collective-permute-done.9.refs_4_
  57.2 0.7 collective-permute-start.12
  57.9 0.7 collective-permute-start.10
  58.6 0.7 collective-permute-start.14
  59.3 1.3 %collective-permute-start.15 = (f32[128,128]{1,0:T(8,128)S(1)}, f32[128,128]{1,0:T(8,128)S(1)}, u32[]{:S(2)}, u32[]{:S(2)}) collective-permute-start(f32[128,128]{1,0:T(8,128)S(1)} %get-tuple-element.38.refs_1_), channel_id=1, source_target_pairs={{80,32},{88,40},{96,16},{104,24},{112,0},{120,8},{81,33},{89,41},{... | collective-permute-start | bytes 196616 | tf_op jit(solution)/shard_map/ppermute | solution.py:260
  60.6 0.7 collective-permute-start.13
  61.3 1.3 %collective-permute-start.17 = (f32[128,128]{1,0:T(8,128)S(1)}, f32[128,128]{1,0:T(8,128)S(1)}, u32[]{:S(2)}, u32[]{:S(2)}) collective-permute-start(f32[128,128]{1,0:T(8,128)S(1)} %get-tuple-element.40.refs_1_), channel_id=1, source_target_pairs={{64,32},{72,40},{80,16},{88,24},{96,0},{104,8},{65,33},{73,41},{81... | collective-permute-start | bytes 196616 | tf_op jit(solution)/shard_map/ppermute | solution.py:260
  62.6 6.3 %collective-permute-done.15.refs_4_ = f32[128,128]{1,0:T(8,128)S(1)} collective-permute-done((f32[128,128]{1,0:T(8,128)S(1)}, f32[128,128]{1,0:T(8,128)S(1)}, u32[]{:S(2)}, u32[]{:S(2)}) %collective-permute-start.15) | collective-permute-done | bytes 65568 | tf_op jit(solution)/shard_map/ppermute | solution.py:260
  68.9 1.3 collective-permute-start.18
  70.2 0.2 solve_step.12
  70.4 0.7 collective-permute-start.16
  71.1 1.3 %collective-permute-start.20 = (f32[128,128]{1,0:T(8,128)S(1)}, f32[128,128]{1,0:T(8,128)S(1)}, u32[]{:S(2)}, u32[]{:S(2)}) collective-permute-start(f32[128,128]{1,0:T(8,128)S(1)} %get-tuple-element.42.refs_1_), channel_id=1, source_target_pairs={{48,16},{56,24},{64,0},{72,8},{49,17},{57,25},{65,1},{73,9},{50,18... | collective-permute-start | bytes 196616 | tf_op jit(solution)/shard_map/ppermute | solution.py:260
  72.4 5.0 %collective-permute-done.18.refs_4_ = f32[128,128]{1,0:T(8,128)S(1)} collective-permute-done((f32[128,128]{1,0:T(8,128)S(1)}, f32[128,128]{1,0:T(8,128)S(1)}, u32[]{:S(2)}, u32[]{:S(2)}) %collective-permute-start.18) | collective-permute-done | bytes 65568 | tf_op jit(solution)/shard_map/ppermute | solution.py:260
  77.4 1.8 %collective-permute-start.31 = (bf16[3072,128]{1,0:T(8,128)(2,1)S(1)}, bf16[3072,128]{1,0:T(8,128)(2,1)S(1)}, u32[]{:S(2)}, u32[]{:S(2)}) collective-permute-start(bf16[3072,128]{1,0:T(8,128)(2,1)S(1)} %copy-done), channel_id=1, source_target_pairs={{0,2},{1,3},{2,4},{3,5},{4,6},{5,7},{6,0},{7,1},{8,10},{9,11},{10,... | collective-permute-start | bytes 2359304 | tf_op jit(solution)/shard_map/ppermute | solution.py:257
  79.2 1.3 collective-permute-start.21
  80.5 0.4 solve_step.13
  80.9 0.7 collective-permute-start.19
  81.6 4.7 %collective-permute-done.21.refs_4_ = f32[128,128]{1,0:T(8,128)S(1)} collective-permute-done((f32[128,128]{1,0:T(8,128)S(1)}, f32[128,128]{1,0:T(8,128)S(1)}, u32[]{:S(2)}, u32[]{:S(2)}) %collective-permute-start.21) | collective-permute-done | bytes 65568 | tf_op jit(solution)/shard_map/ppermute | solution.py:260
  86.3 1.5 %collective-permute-start.23 = (f32[128,128]{1,0:T(8,128)S(1)}, f32[128,128]{1,0:T(8,128)S(1)}, u32[]{:S(2)}, u32[]{:S(2)}) collective-permute-start(f32[128,128]{1,0:T(8,128)S(1)} %get-tuple-element.44.refs_1_), channel_id=1, source_target_pairs={{32,0},{40,8},{33,1},{41,9},{34,2},{42,10},{35,3},{43,11},{36,4},{... | collective-permute-start | bytes 196616 | tf_op jit(solution)/shard_map/ppermute | solution.py:260
  87.8 1.5 %collective-permute-start.33 = (bf16[3072,128]{1,0:T(8,128)(2,1)S(1)}, bf16[3072,128]{1,0:T(8,128)(2,1)S(1)}, u32[]{:S(2)}, u32[]{:S(2)}) collective-permute-start(bf16[3072,128]{1,0:T(8,128)(2,1)S(1)} %copy-done), channel_id=1, source_target_pairs={{0,6},{1,7},{2,0},{3,1},{4,2},{5,3},{6,4},{7,5},{8,14},{9,15},{10,... | collective-permute-start | bytes 2359304 | tf_op jit(solution)/shard_map/ppermute | solution.py:257
  89.4 0.4 solve_step.14
  89.8 2.7 %collective-permute-done.23.refs_3_ = f32[128,128]{1,0:T(8,128)S(1)} collective-permute-done((f32[128,128]{1,0:T(8,128)S(1)}, f32[128,128]{1,0:T(8,128)S(1)}, u32[]{:S(2)}, u32[]{:S(2)}) %collective-permute-start.23) | collective-permute-done | bytes 65568 | tf_op jit(solution)/shard_map/ppermute | solution.py:260
  92.5 1.3 collective-permute-start.22
  93.8 4.9 %collective-permute-done.22.refs_2_ = f32[128,128]{1,0:T(8,128)S(1)} collective-permute-done((f32[128,128]{1,0:T(8,128)S(1)}, f32[128,128]{1,0:T(8,128)S(1)}, u32[]{:S(2)}, u32[]{:S(2)}) %collective-permute-start.22) | collective-permute-done | bytes 65568 | tf_op jit(solution)/shard_map/ppermute | solution.py:260
  98.6 1.6 %solve_step.15 = (f32[128,128]{1,0:T(8,128)}, f32[128,128]{1,0:T(8,128)}, bf16[128,128]{1,0:T(8,128)(2,1)S(1)}, f32[64,128]{1,0:T(8,128)S(1)}, f32[64,128]{1,0:T(8,128)S(1)}) custom-call(f32[128,128]{1,0:T(8,128)S(1)} %get-tuple-element.45.refs_0_, f32[128,128]{1,0:T(8,128)S(1)} %get-tuple-element.46.refs_1_, ...), custom_call_target="tpu_custom_call" | custom-call | flops 8000000 | bytes 5000000 | tf_op jit(solution)/shard_map/solve_step/pallas_call | solution.py:189
  100.3 0.1 collective-permute-start.25
  100.3 3.2 %collective-permute-start.26 = (bf16[128,128]{1,0:T(8,128)(2,1)S(1)}, bf16[128,128]{1,0:T(8,128)(2,1)S(1)}, u32[]{:S(2)}, u32[]{:S(2)}) collective-permute-start(bf16[128,128]{1,0:T(8,128)(2,1)S(1)} %get-tuple-element.47.a), channel_id=1, source_target_pairs={{0,96},{8,104},{16,112},{24,120},{32,0},{40,8},{48,16},{56,24},{64... | collective-permute-start | bytes 98312 | tf_op jit(solution)/shard_map/ppermute | solution.py:260
  103.6 1.8 %collective-permute-done.24.b = bf16[128,128]{1,0:T(8,128)(2,1)S(1)} collective-permute-done((bf16[128,128]{1,0:T(8,128)(2,1)S(1)}, bf16[128,128]{1,0:T(8,128)(2,1)S(1)}, u32[]{:S(2)}, u32[]{:S(2)}) %collective-permute-start.24) | collective-permute-done | bytes 32800 | tf_op jit(solution)/shard_map/ppermute | solution.py:260
  105.4 1.9 %collective-permute-start.32 = (bf16[3072,128]{1,0:T(8,128)(2,1)S(1)}, bf16[3072,128]{1,0:T(8,128)(2,1)S(1)}, u32[]{:S(2)}, u32[]{:S(2)}) collective-permute-start(bf16[3072,128]{1,0:T(8,128)(2,1)S(1)} %collective-permute-done.30.h), channel_id=1, source_target_pairs={{0,2},{1,3},{2,4},{3,5},{4,6},{5,7},{6,0},{7,1},{8,10},{9,11},{10,... | collective-permute-start | bytes 2359304 | tf_op jit(solution)/shard_map/ppermute | solution.py:257
  107.3 1.3 %collective-permute-start.34 = (bf16[3072,128]{1,0:T(8,128)(2,1)S(1)}, bf16[3072,128]{1,0:T(8,128)(2,1)S(1)}, u32[]{:S(2)}, u32[]{:S(2)}) collective-permute-start(bf16[3072,128]{1,0:T(8,128)(2,1)S(1)} %collective-permute-done.30.h), channel_id=1, source_target_pairs={{0,6},{1,7},{2,0},{3,1},{4,2},{5,3},{6,4},{7,5},{8,14},{9,15},{10,... | collective-permute-start | bytes 2359304 | tf_op jit(solution)/shard_map/ppermute | solution.py:257
  108.6 2.7 %collective-permute-start.36 = (bf16[3072,128]{1,0:T(8,128)(2,1)S(1)}, bf16[3072,128]{1,0:T(8,128)(2,1)S(1)}, u32[]{:S(2)}, u32[]{:S(2)}) collective-permute-start(bf16[3072,128]{1,0:T(8,128)(2,1)S(1)} %collective-permute-done.35.z2), channel_id=1, source_target_pairs={{0,1},{1,0},{2,3},{3,2},{4,5},{5,4},{6,7},{7,6},{8,9},{9,8},{10,11... | collective-permute-start | bytes 2359304 | tf_op jit(solution)/shard_map/ppermute | solution.py:263
  111.4 0.1 collective-permute-start.28
  111.5 0.1 collective-permute-start.37
  111.6 1.2 collective-permute-done.37
  112.8 0.2 collective-permute-start.27
  112.9 10.1 %collective-permute-done.28.cross = bf16[4,128,128]{2,1,0:T(8,128)(2,1)S(1)} collective-permute-done((bf16[4,128,128]{2,1,0:T(8,128)(2,1)S(1)}, bf16[4,128,128]{2,1,0:T(8,128)(2,1)S(1)}, u32[]{:S(2)}, u32[]{:S(2)}) %collective-permute-start.28) | collective-permute-done | bytes 131104 | tf_op jit(solution)/shard_map/ppermute | solution.py:260
  123.0 0.6 maximum_select_fusion.2
  123.7 0.7 collective-permute-done.29.cross_swap
  124.4 4.1 %back_transform.1 = bf16[3072,256]{1,0:T(8,128)(2,1)} custom-call(bf16[4,128,128]{2,1,0:T(8,128)(2,1)S(1)} %stack4.1.same, bf16[4,128,128]{2,1,0:T(8,128)(2,1)S(1)} %collective-permute-done.27.same_swap, bf16[4,128,128]{2,1,0:T(8,128)(2,1)S(1)} %collective-permute-done.28.cross, bf16[4,128,128]{2,1,0:T(8,128)(2,1)S(1)} %collective-permute-done.29.cross_swap, ...), custom_call_target="tpu_custom_call" | custom-call | flops 1610612736 | bytes 8000000 | tf_op jit(solution)/shard_map/back_transform/pallas_call | solution.py:240
  (38 shorter events, 0.2 us)
Async XLA Ops:
  0.6 1.0 copy-start.1
  1.7 0.8 copy-start.2
  2.4 0.7 copy-start.4
  3.1 8.4 %copy-start.3 = (f32[64,128]{1,0:T(8,128)S(1)}, f32[64,128]{1,0:T(8,128)}, u32[]{:S(2)}) copy-start(f32[64,128]{1,0:T(8,128)} %schur_rows.1) | copy-start | bytes 98308
  3.1 20.1 %copy-start = (bf16[3072,128]{1,0:T(8,128)(2,1)S(1)}, bf16[3072,128]{1,0:T(8,128)(2,1)}, u32[]{:S(2)}) copy-start(bf16[3072,128]{1,0:T(8,128)(2,1)} %own.1) | copy-start | bytes 2359300
  7.0 45.1 %collective-permute-start.5 = (f32[64,64,128]{2,1,0:T(8,128)}, f32[64,64,128]{2,1,0:T(8,128)}, u32[]{:S(2)}, u32[]{:S(2)}) collective-permute-start(f32[64,64,128]{2,1,0:T(8,128)} %get-tuple-element.30), channel_id=1, source_target_pairs={{0,8},{8,0},{16,24},{24,16},{32,40},{40,32},{48,56},{56,48},{64,72... | collective-permute-start | bytes 6291464 | tf_op jit(solution)/shard_map/ppermute | solution.py:260
  7.1 4.5 %collective-permute-start = (f32[128,128]{1,0:T(8,128)S(1)}, f32[128,128]{1,0:T(8,128)S(1)}, u32[]{:S(2)}, u32[]{:S(2)}) collective-permute-start(f32[128,128]{1,0:T(8,128)S(1)} %get-tuple-element.29), channel_id=1, source_target_pairs={{0,8},{8,0},{16,24},{24,16},{32,40},{40,32},{48,56},{56,48},{64,72... | collective-permute-start | bytes 196616 | tf_op jit(solution)/shard_map/ppermute | solution.py:260
  11.6 7.7 %collective-permute-start.1 = (f32[128,128]{1,0:T(8,128)S(1)}, f32[128,128]{1,0:T(8,128)S(1)}, u32[]{:S(2)}, u32[]{:S(2)}) collective-permute-start(f32[128,128]{1,0:T(8,128)S(1)} %maximum_select_fusion.1), channel_id=1, source_target_pairs={{0,1},{1,0},{2,3},{3,2},{4,5},{5,4},{6,7},{7,6},{8,9},{9,8},{10,11... | collective-permute-start | bytes 196616 | tf_op jit(solution)/shard_map/ppermute | solution.py:272
  19.3 12.6 %collective-permute-start.2 = (f32[2,128,128]{2,1,0:T(8,128)S(1)}, f32[2,128,128]{2,1,0:T(8,128)S(1)}, u32[]{:S(2)}, u32[]{:S(2)}) collective-permute-start(f32[2,128,128]{2,1,0:T(8,128)S(1)} %pad_maximum_fusion.refs_3_), channel_id=1, source_target_pairs={{0,2},{1,3},{2,4},{3,5},{4,6},{5,7},{6,0},{7,1},{8,10},{9,11},{10,... | collective-permute-start | bytes 393224 | tf_op jit(solution)/shard_map/ppermute | solution.py:272
  23.2 77.1 %collective-permute-start.35 = (bf16[3072,128]{1,0:T(8,128)(2,1)S(1)}, bf16[3072,128]{1,0:T(8,128)(2,1)S(1)}, u32[]{:S(2)}, u32[]{:S(2)}) collective-permute-start(bf16[3072,128]{1,0:T(8,128)(2,1)S(1)} %copy-done), channel_id=1, source_target_pairs={{0,4},{1,5},{2,6},{3,7},{4,0},{5,1},{6,2},{7,3},{8,12},{9,13},{10,... | collective-permute-start | bytes 2359304 | tf_op jit(solution)/shard_map/ppermute | solution.py:257
  26.9 73.5 %collective-permute-start.30 = (bf16[3072,128]{1,0:T(8,128)(2,1)S(1)}, bf16[3072,128]{1,0:T(8,128)(2,1)S(1)}, u32[]{:S(2)}, u32[]{:S(2)}) collective-permute-start(bf16[3072,128]{1,0:T(8,128)(2,1)S(1)} %copy-done), channel_id=1, source_target_pairs={{0,1},{1,0},{2,3},{3,2},{4,5},{5,4},{6,7},{7,6},{8,9},{9,8},{10,11... | collective-permute-start | bytes 2359304 | tf_op jit(solution)/shard_map/ppermute | solution.py:263
  29.9 18.9 %collective-permute-start.3 = (f32[2,128,128]{2,1,0:T(8,128)S(1)}, f32[2,128,128]{2,1,0:T(8,128)S(1)}, u32[]{:S(2)}, u32[]{:S(2)}) collective-permute-start(f32[2,128,128]{2,1,0:T(8,128)S(1)} %pad_maximum_fusion.refs_3_), channel_id=1, source_target_pairs={{0,4},{1,5},{2,6},{3,7},{4,0},{5,1},{6,2},{7,3},{8,12},{9,13},{10,... | collective-permute-start | bytes 393224 | tf_op jit(solution)/shard_map/ppermute | solution.py:272
  31.9 20.2 %collective-permute-start.4 = (f32[2,128,128]{2,1,0:T(8,128)S(1)}, f32[2,128,128]{2,1,0:T(8,128)S(1)}, u32[]{:S(2)}, u32[]{:S(2)}) collective-permute-start(f32[2,128,128]{2,1,0:T(8,128)S(1)} %pad_maximum_fusion.refs_3_), channel_id=1, source_target_pairs={{0,6},{1,7},{2,0},{3,1},{4,2},{5,3},{6,4},{7,5},{8,14},{9,15},{10,... | collective-permute-start | bytes 393224 | tf_op jit(solution)/shard_map/ppermute | solution.py:272
  53.7 2.0 %collective-permute-start.6 = (f32[128,128]{1,0:T(8,128)S(1)}, f32[128,128]{1,0:T(8,128)S(1)}, u32[]{:S(2)}, u32[]{:S(2)}) collective-permute-start(f32[128,128]{1,0:T(8,128)S(1)} %get-tuple-element.32.refs_1_), channel_id=1, source_target_pairs={{112,96},{120,104},{113,97},{121,105},{114,98},{122,106},{115,99},... | collective-permute-start | bytes 196616 | tf_op jit(solution)/shard_map/ppermute | solution.py:260
  54.4 2.1 %collective-permute-start.8 = (f32[128,128]{1,0:T(8,128)S(1)}, f32[128,128]{1,0:T(8,128)S(1)}, u32[]{:S(2)}, u32[]{:S(2)}) collective-permute-start(f32[128,128]{1,0:T(8,128)S(1)} %get-tuple-element.32.refs_1_), channel_id=1, source_target_pairs={{112,80},{120,88},{113,81},{121,89},{114,82},{122,90},{115,83},{12... | collective-permute-start | bytes 196616 | tf_op jit(solution)/shard_map/ppermute | solution.py:260
  55.1 2.1 %collective-permute-start.9 = (f32[128,128]{1,0:T(8,128)S(1)}, f32[128,128]{1,0:T(8,128)S(1)}, u32[]{:S(2)}, u32[]{:S(2)}) collective-permute-start(f32[128,128]{1,0:T(8,128)S(1)} %get-tuple-element.32.refs_1_), channel_id=1, source_target_pairs={{112,64},{120,72},{113,65},{121,73},{114,66},{122,74},{115,67},{12... | collective-permute-start | bytes 196616 | tf_op jit(solution)/shard_map/ppermute | solution.py:260
  55.8 2.0 %collective-permute-start.7 = (f32[128,128]{1,0:T(8,128)S(1)}, f32[128,128]{1,0:T(8,128)S(1)}, u32[]{:S(2)}, u32[]{:S(2)}) collective-permute-start(f32[128,128]{1,0:T(8,128)S(1)} %get-tuple-element.36.refs_1_), channel_id=1, source_target_pairs={{96,80},{104,88},{97,81},{105,89},{98,82},{106,90},{99,83},{107,91... | collective-permute-start | bytes 196616 | tf_op jit(solution)/shard_map/ppermute | solution.py:260
  56.5 2.1 %collective-permute-start.11 = (f32[128,128]{1,0:T(8,128)S(1)}, f32[128,128]{1,0:T(8,128)S(1)}, u32[]{:S(2)}, u32[]{:S(2)}) collective-permute-start(f32[128,128]{1,0:T(8,128)S(1)} %get-tuple-element.36.refs_1_), channel_id=1, source_target_pairs={{96,64},{104,72},{112,48},{120,56},{97,65},{105,73},{113,49},{121,... | collective-permute-start | bytes 196616 | tf_op jit(solution)/shard_map/ppermute | solution.py:260
  57.2 2.1 %collective-permute-start.12 = (f32[128,128]{1,0:T(8,128)S(1)}, f32[128,128]{1,0:T(8,128)S(1)}, u32[]{:S(2)}, u32[]{:S(2)}) collective-permute-start(f32[128,128]{1,0:T(8,128)S(1)} %get-tuple-element.36.refs_1_), channel_id=1, source_target_pairs={{96,48},{104,56},{112,32},{120,40},{97,49},{105,57},{113,33},{121,... | collective-permute-start | bytes 196616 | tf_op jit(solution)/shard_map/ppermute | solution.py:260
  57.9 2.7 %collective-permute-start.10 = (f32[128,128]{1,0:T(8,128)S(1)}, f32[128,128]{1,0:T(8,128)S(1)}, u32[]{:S(2)}, u32[]{:S(2)}) collective-permute-start(f32[128,128]{1,0:T(8,128)S(1)} %get-tuple-element.38.refs_1_), channel_id=1, source_target_pairs={{80,64},{88,72},{81,65},{89,73},{82,66},{90,74},{83,67},{91,75},{8... | collective-permute-start | bytes 196616 | tf_op jit(solution)/shard_map/ppermute | solution.py:260
  58.6 2.7 %collective-permute-start.14 = (f32[128,128]{1,0:T(8,128)S(1)}, f32[128,128]{1,0:T(8,128)S(1)}, u32[]{:S(2)}, u32[]{:S(2)}) collective-permute-start(f32[128,128]{1,0:T(8,128)S(1)} %get-tuple-element.38.refs_1_), channel_id=1, source_target_pairs={{80,48},{88,56},{96,32},{104,40},{112,16},{120,24},{81,49},{89,57}... | collective-permute-start | bytes 196616 | tf_op jit(solution)/shard_map/ppermute | solution.py:260
  59.3 9.6 %collective-permute-start.15 = (f32[128,128]{1,0:T(8,128)S(1)}, f32[128,128]{1,0:T(8,128)S(1)}, u32[]{:S(2)}, u32[]{:S(2)}) collective-permute-start(f32[128,128]{1,0:T(8,128)S(1)} %get-tuple-element.38.refs_1_), channel_id=1, source_target_pairs={{80,32},{88,40},{96,16},{104,24},{112,0},{120,8},{81,33},{89,41},{... | collective-permute-start | bytes 196616 | tf_op jit(solution)/shard_map/ppermute | solution.py:260
  60.6 9.6 %collective-permute-start.13 = (f32[128,128]{1,0:T(8,128)S(1)}, f32[128,128]{1,0:T(8,128)S(1)}, u32[]{:S(2)}, u32[]{:S(2)}) collective-permute-start(f32[128,128]{1,0:T(8,128)S(1)} %get-tuple-element.40.refs_1_), channel_id=1, source_target_pairs={{64,48},{72,56},{65,49},{73,57},{66,50},{74,58},{67,51},{75,59},{6... | collective-permute-start | bytes 196616 | tf_op jit(solution)/shard_map/ppermute | solution.py:260
  61.3 9.8 %collective-permute-start.17 = (f32[128,128]{1,0:T(8,128)S(1)}, f32[128,128]{1,0:T(8,128)S(1)}, u32[]{:S(2)}, u32[]{:S(2)}) collective-permute-start(f32[128,128]{1,0:T(8,128)S(1)} %get-tuple-element.40.refs_1_), channel_id=1, source_target_pairs={{64,32},{72,40},{80,16},{88,24},{96,0},{104,8},{65,33},{73,41},{81... | collective-permute-start | bytes 196616 | tf_op jit(solution)/shard_map/ppermute | solution.py:260
  68.9 8.6 %collective-permute-start.18 = (f32[128,128]{1,0:T(8,128)S(1)}, f32[128,128]{1,0:T(8,128)S(1)}, u32[]{:S(2)}, u32[]{:S(2)}) collective-permute-start(f32[128,128]{1,0:T(8,128)S(1)} %get-tuple-element.40.refs_1_), channel_id=1, source_target_pairs={{64,16},{72,24},{80,0},{88,8},{65,17},{73,25},{81,1},{89,9},{66,18... | collective-permute-start | bytes 196616 | tf_op jit(solution)/shard_map/ppermute | solution.py:260
  70.4 8.8 %collective-permute-start.16 = (f32[128,128]{1,0:T(8,128)S(1)}, f32[128,128]{1,0:T(8,128)S(1)}, u32[]{:S(2)}, u32[]{:S(2)}) collective-permute-start(f32[128,128]{1,0:T(8,128)S(1)} %get-tuple-element.42.refs_1_), channel_id=1, source_target_pairs={{48,32},{56,40},{49,33},{57,41},{50,34},{58,42},{51,35},{59,43},{5... | collective-permute-start | bytes 196616 | tf_op jit(solution)/shard_map/ppermute | solution.py:260
  71.1 9.8 %collective-permute-start.20 = (f32[128,128]{1,0:T(8,128)S(1)}, f32[128,128]{1,0:T(8,128)S(1)}, u32[]{:S(2)}, u32[]{:S(2)}) collective-permute-start(f32[128,128]{1,0:T(8,128)S(1)} %get-tuple-element.42.refs_1_), channel_id=1, source_target_pairs={{48,16},{56,24},{64,0},{72,8},{49,17},{57,25},{65,1},{73,9},{50,18... | collective-permute-start | bytes 196616 | tf_op jit(solution)/shard_map/ppermute | solution.py:260
  77.4 33.9 %collective-permute-start.31 = (bf16[3072,128]{1,0:T(8,128)(2,1)S(1)}, bf16[3072,128]{1,0:T(8,128)(2,1)S(1)}, u32[]{:S(2)}, u32[]{:S(2)}) collective-permute-start(bf16[3072,128]{1,0:T(8,128)(2,1)S(1)} %copy-done), channel_id=1, source_target_pairs={{0,2},{1,3},{2,4},{3,5},{4,6},{5,7},{6,0},{7,1},{8,10},{9,11},{10,... | collective-permute-start | bytes 2359304 | tf_op jit(solution)/shard_map/ppermute | solution.py:257
  79.2 7.2 %collective-permute-start.21 = (f32[128,128]{1,0:T(8,128)S(1)}, f32[128,128]{1,0:T(8,128)S(1)}, u32[]{:S(2)}, u32[]{:S(2)}) collective-permute-start(f32[128,128]{1,0:T(8,128)S(1)} %get-tuple-element.42.refs_1_), channel_id=1, source_target_pairs={{48,0},{56,8},{49,1},{57,9},{50,2},{58,10},{51,3},{59,11},{52,4},{... | collective-permute-start | bytes 196616 | tf_op jit(solution)/shard_map/ppermute | solution.py:260
  80.9 6.9 %collective-permute-start.19 = (f32[128,128]{1,0:T(8,128)S(1)}, f32[128,128]{1,0:T(8,128)S(1)}, u32[]{:S(2)}, u32[]{:S(2)}) collective-permute-start(f32[128,128]{1,0:T(8,128)S(1)} %get-tuple-element.44.refs_1_), channel_id=1, source_target_pairs={{32,16},{40,24},{33,17},{41,25},{34,18},{42,26},{35,19},{43,27},{3... | collective-permute-start | bytes 196616 | tf_op jit(solution)/shard_map/ppermute | solution.py:260
  86.3 6.1 %collective-permute-start.23 = (f32[128,128]{1,0:T(8,128)S(1)}, f32[128,128]{1,0:T(8,128)S(1)}, u32[]{:S(2)}, u32[]{:S(2)}) collective-permute-start(f32[128,128]{1,0:T(8,128)S(1)} %get-tuple-element.44.refs_1_), channel_id=1, source_target_pairs={{32,0},{40,8},{33,1},{41,9},{34,2},{42,10},{35,3},{43,11},{36,4},{... | collective-permute-start | bytes 196616 | tf_op jit(solution)/shard_map/ppermute | solution.py:260
  87.8 23.7 %collective-permute-start.33 = (bf16[3072,128]{1,0:T(8,128)(2,1)S(1)}, bf16[3072,128]{1,0:T(8,128)(2,1)S(1)}, u32[]{:S(2)}, u32[]{:S(2)}) collective-permute-start(bf16[3072,128]{1,0:T(8,128)(2,1)S(1)} %copy-done), channel_id=1, source_target_pairs={{0,6},{1,7},{2,0},{3,1},{4,2},{5,3},{6,4},{7,5},{8,14},{9,15},{10,... | collective-permute-start | bytes 2359304 | tf_op jit(solution)/shard_map/ppermute | solution.py:257
  92.5 6.1 %collective-permute-start.22 = (f32[128,128]{1,0:T(8,128)S(1)}, f32[128,128]{1,0:T(8,128)S(1)}, u32[]{:S(2)}, u32[]{:S(2)}) collective-permute-start(f32[128,128]{1,0:T(8,128)S(1)} %get-tuple-element.46.refs_1_), channel_id=1, source_target_pairs={{16,0},{24,8},{17,1},{25,9},{18,2},{26,10},{19,3},{27,11},{20,4},{... | collective-permute-start | bytes 196616 | tf_op jit(solution)/shard_map/ppermute | solution.py:260
  100.3 5.1 %collective-permute-start.24 = (bf16[128,128]{1,0:T(8,128)(2,1)S(1)}, bf16[128,128]{1,0:T(8,128)(2,1)S(1)}, u32[]{:S(2)}, u32[]{:S(2)}) collective-permute-start(bf16[128,128]{1,0:T(8,128)(2,1)S(1)} %get-tuple-element.47.a), channel_id=1, source_target_pairs={{0,32},{8,40},{16,48},{24,56},{32,64},{40,72},{48,80},{56,88},{64,... | collective-permute-start | bytes 98312 | tf_op jit(solution)/shard_map/ppermute | solution.py:260
  100.3 7.0 %collective-permute-start.25 = (bf16[128,128]{1,0:T(8,128)(2,1)S(1)}, bf16[128,128]{1,0:T(8,128)(2,1)S(1)}, u32[]{:S(2)}, u32[]{:S(2)}) collective-permute-start(bf16[128,128]{1,0:T(8,128)(2,1)S(1)} %get-tuple-element.47.a), channel_id=1, source_target_pairs={{0,64},{8,72},{16,80},{24,88},{32,96},{40,104},{48,112},{56,120},{... | collective-permute-start | bytes 98312 | tf_op jit(solution)/shard_map/ppermute | solution.py:260
  100.3 8.3 %collective-permute-start.26 = (bf16[128,128]{1,0:T(8,128)(2,1)S(1)}, bf16[128,128]{1,0:T(8,128)(2,1)S(1)}, u32[]{:S(2)}, u32[]{:S(2)}) collective-permute-start(bf16[128,128]{1,0:T(8,128)(2,1)S(1)} %get-tuple-element.47.a), channel_id=1, source_target_pairs={{0,96},{8,104},{16,112},{24,120},{32,0},{40,8},{48,16},{56,24},{64... | collective-permute-start | bytes 98312 | tf_op jit(solution)/shard_map/ppermute | solution.py:260
  105.4 19.0 %collective-permute-start.32 = (bf16[3072,128]{1,0:T(8,128)(2,1)S(1)}, bf16[3072,128]{1,0:T(8,128)(2,1)S(1)}, u32[]{:S(2)}, u32[]{:S(2)}) collective-permute-start(bf16[3072,128]{1,0:T(8,128)(2,1)S(1)} %collective-permute-done.30.h), channel_id=1, source_target_pairs={{0,2},{1,3},{2,4},{3,5},{4,6},{5,7},{6,0},{7,1},{8,10},{9,11},{10,... | collective-permute-start | bytes 2359304 | tf_op jit(solution)/shard_map/ppermute | solution.py:257
  107.3 17.1 %collective-permute-start.34 = (bf16[3072,128]{1,0:T(8,128)(2,1)S(1)}, bf16[3072,128]{1,0:T(8,128)(2,1)S(1)}, u32[]{:S(2)}, u32[]{:S(2)}) collective-permute-start(bf16[3072,128]{1,0:T(8,128)(2,1)S(1)} %collective-permute-done.30.h), channel_id=1, source_target_pairs={{0,6},{1,7},{2,0},{3,1},{4,2},{5,3},{6,4},{7,5},{8,14},{9,15},{10,... | collective-permute-start | bytes 2359304 | tf_op jit(solution)/shard_map/ppermute | solution.py:257
  108.6 15.8 %collective-permute-start.36 = (bf16[3072,128]{1,0:T(8,128)(2,1)S(1)}, bf16[3072,128]{1,0:T(8,128)(2,1)S(1)}, u32[]{:S(2)}, u32[]{:S(2)}) collective-permute-start(bf16[3072,128]{1,0:T(8,128)(2,1)S(1)} %collective-permute-done.35.z2), channel_id=1, source_target_pairs={{0,1},{1,0},{2,3},{3,2},{4,5},{5,4},{6,7},{7,6},{8,9},{9,8},{10,11... | collective-permute-start | bytes 2359304 | tf_op jit(solution)/shard_map/ppermute | solution.py:263
  111.4 11.7 %collective-permute-start.28 = (bf16[4,128,128]{2,1,0:T(8,128)(2,1)S(1)}, bf16[4,128,128]{2,1,0:T(8,128)(2,1)S(1)}, u32[]{:S(2)}, u32[]{:S(2)}) collective-permute-start(bf16[4,128,128]{2,1,0:T(8,128)(2,1)S(1)} %stack4.1.same), channel_id=1, source_target_pairs={{0,16},{8,24},{16,0},{24,8},{32,48},{40,56},{48,32},{56,40},{64,80... | collective-permute-start | bytes 393224 | tf_op jit(solution)/shard_map/ppermute | solution.py:260
  111.5 1.3 %collective-permute-start.37 = (f32[64,128]{1,0:T(8,128)S(1)}, f32[64,128]{1,0:T(8,128)S(1)}, u32[]{:S(2)}, u32[]{:S(2)}) collective-permute-start(f32[64,128]{1,0:T(8,128)S(1)} %get-tuple-element.51), channel_id=1, source_target_pairs={{0,8},{8,0},{16,24},{24,16},{32,40},{40,32},{48,56},{56,48},{64,72... | collective-permute-start | bytes 98312 | tf_op jit(solution)/shard_map/ppermute | solution.py:260
  112.8 10.9 %collective-permute-start.27 = (bf16[4,128,128]{2,1,0:T(8,128)(2,1)S(1)}, bf16[4,128,128]{2,1,0:T(8,128)(2,1)S(1)}, u32[]{:S(2)}, u32[]{:S(2)}) collective-permute-start(bf16[4,128,128]{2,1,0:T(8,128)(2,1)S(1)} %stack4.1.same), channel_id=1, source_target_pairs={{0,8},{8,0},{16,24},{24,16},{32,40},{40,32},{48,56},{56,48},{64,72... | collective-permute-start | bytes 393224 | tf_op jit(solution)/shard_map/ppermute | solution.py:260
  123.0 1.3 %collective-permute-start.29 = (bf16[4,128,128]{2,1,0:T(8,128)(2,1)S(1)}, bf16[4,128,128]{2,1,0:T(8,128)(2,1)S(1)}, u32[]{:S(2)}, u32[]{:S(2)}) collective-permute-start(bf16[4,128,128]{2,1,0:T(8,128)(2,1)S(1)} %collective-permute-done.28.cross), channel_id=1, source_target_pairs={{0,8},{8,0},{16,24},{24,16},{32,40},{40,32},{48,56},{56,48},{64,72... | collective-permute-start | bytes 393224 | tf_op jit(solution)/shard_map/ppermute | solution.py:260

commit v2 on v1

--- a/solution.py
+++ b/solution.py
@@ -47,12 +47,15 @@
     return pl.ds(pl.multiple_of(core * LANES, LANES), LANES)
 
 
-def setup_kernel(coupling, selected, schur_rows, inv, inv_mine, inv_send, small, rhs_mine, sem):
+def setup_kernel(coupling, selected, t0, t1, t2, t3, inv, inv_from, inv_mine, inv_other, send, rhs_mine, sem):
     core = lax.rem(lax.axis_index("row"), 2)
-    send = pltpu.make_async_copy(inv.at[:, :, core_lanes(1 - core)], inv_send, sem.at[0])
-    mine = pltpu.make_async_copy(inv.at[:, :, core_lanes(core)], inv_mine, sem.at[1])
-    send.start()
+    mine = pltpu.make_async_copy(inv.at[:, :, core_lanes(core)], inv_mine, sem.at[0])
+    other = pltpu.make_async_copy(inv_from.at[:, :, core_lanes(core)], inv_other, sem.at[1])
     mine.start()
+    other.start()
+    for index, tile in enumerate((t0, t1, t2, t3)):
+        for half in range(2):
+            send[pl.ds((2 * index + half) * NB, NB), :] = tile[half]
     candidates, columns = coupling.shape[1], selected.shape[1]
     piece = 256
     total = jnp.zeros((3 * NB, columns), F32)
@@ -68,23 +71,22 @@
     rhs = -(total[:NB] + total[NB : 2 * NB] + total[2 * NB :])
     left, right = rhs[:, :LANES], rhs[:, LANES:]
     rhs_mine[...] = jnp.where(core == 0, left, right)
-    small[:NB, :] = schur_rows[...]
-    small[NB:, :] = jnp.where(core == 0, right, left)
-    send.wait()
+    send[pl.ds(CHIPS * NB, NB), :] = jnp.where(core == 0, right, left)
     mine.wait()
-
-
-def setup(coupling, selected, schur_rows, inverses):
+    other.wait()
+
+
+def setup(coupling, selected, parts, inverses, inv_from):
     half = pltpu.VMEM((NB, NB, LANES), F32)
     return pl.pallas_call(
         setup_kernel,
-        out_shape=(half, half, pltpu.VMEM((PAIR, LANES), F32), pltpu.VMEM((NB, LANES), F32)),
-        in_specs=[VMEM, VMEM, VMEM, HBM],
+        out_shape=(half, half, pltpu.VMEM(((CHIPS + 1) * NB, LANES), F32), pltpu.VMEM((NB, LANES), F32)),
+        in_specs=[VMEM] * 6 + [HBM] * 2,
         out_specs=(VMEM,) * 4,
         scratch_shapes=[pltpu.SemaphoreType.DMA((2,))],
         compiler_params=pltpu.CompilerParams(vmem_limit_bytes=16 << 20),
         name="setup",
-    )(coupling, selected[None, :], schur_rows, pltpu.with_memory_space_constraint(inverses, pltpu.HBM))
+    )(coupling, selected[None, :], *parts, pltpu.with_memory_space_constraint(inverses, pltpu.HBM), inv_from)
 
 
 def apply_inverse(inv, pending):
@@ -94,9 +96,6 @@
 
 def step_kernel(step, names, *refs):
     ref = dict(zip(names, refs))
-    if step == 0:
-        get_inv = pltpu.make_async_copy(ref["inv_from"], ref["inv_other"], refs[-1])
-        get_inv.start()
     row, col = lax.axis_index("row"), lax.axis_index("col")
     me, core = row // 2, lax.rem(row, 2)
     chip = CHIPS - 1 - step
@@ -113,11 +112,13 @@
         return jnp.dot(tile(source), value, precision=HIGHEST, preferred_element_type=F32)
 
     if step == 0:
-        for index, name in enumerate(("t0", "t1", "t2", "t3")):
-            tiles[pl.ds(2 * index, 2)] = ref[name][...]
-        pend[pl.ds(pl.multiple_of(core * NB, NB), NB), :] = ref["rhs_mine"][...]
-        pend[pl.ds(pl.multiple_of((1 - core) * NB, NB), NB), :] = ref["small"][NB:, :]
-        get_inv.wait()
+        mine = pl.ds(pl.multiple_of(core * NB, NB), NB)
+        theirs = pl.ds(pl.multiple_of((1 - core) * NB, NB), NB)
+        for index in range(CHIPS):
+            tiles[index, mine, :] = ref["sent"][pl.ds(index * NB, NB), :]
+            tiles[index, theirs, :] = ref["swapped"][pl.ds(index * NB, NB), :]
+        pend[mine, :] = ref["rhs_mine"][...]
+        pend[theirs, :] = ref["swapped"][pl.ds(CHIPS * NB, NB), :]
     else:
         pend[...] = ref["pend_in"][...]
 
@@ -167,11 +168,10 @@
 
 
 def solve_step(step, operands):
-    block = jax.ShapeDtypeStruct((PAIR, LANES), F32)
+    block = pltpu.VMEM((PAIR, LANES), F32)
     outs = {"pend": block, "x": block}
     if step == 0:
         outs["tiles_out"] = pltpu.VMEM((CHIPS, PAIR, LANES), F32)
-        outs["inv_other"] = pltpu.VMEM((NB, NB, LANES), F32)
     if step == CHIPS - 1:
         outs["factor"] = jax.ShapeDtypeStruct((PAIR, LANES), BF16)
         outs["mine"] = outs["theirs"] = jax.ShapeDtypeStruct((NB, LANES), F32)
@@ -179,9 +179,8 @@
     call = pl.pallas_call(
         functools.partial(step_kernel, step, names),
         out_shape=tuple(outs.values()),
-        in_specs=[HBM if name == "inv_from" else VMEM for name in operands],
+        in_specs=[VMEM] * len(operands),
         out_specs=(VMEM,) * len(outs),
-        scratch_shapes=[] if step else [pltpu.SemaphoreType.DMA],
         compiler_params=pltpu.CompilerParams(vmem_limit_bytes=16 << 20),
         cost_estimate=pl.CostEstimate(flops=8_000_000, bytes_accessed=5_000_000, transcendentals=0),
         name="solve_step",
@@ -209,7 +208,7 @@
     )(*parts)
 
 
-def product_kernel(same, same_swap, cross, cross_swap, own, h, zp1, zp2, zm1, zm2, z2, z2x, out, x_all):
+def product_kernel(same, same_swap, cross, cross_swap, own, h, zp1, zp2, zm1, zm2, ra, rb, rc, rd, out, x_all):
     row, col = lax.axis_index("row"), lax.axis_index("col")
     core, xlo, y = lax.rem(row, 2), lax.rem(row // 2, 2), row // 4
 
@@ -225,23 +224,30 @@
     def pair(left, right, by):
         source = wrap(col + by, CHIPS)
         other = source + 1 - 2 * lax.rem(source, 2)
-        lhs = jnp.concatenate([left[...], right[...]], axis=1)
+        lhs = jnp.concatenate([left, right], axis=1)
         rhs = jnp.concatenate([x_all[source], x_all[other]], axis=0)
         return jnp.dot(lhs, rhs, preferred_element_type=F32)
 
-    total = pair(own, h, 0) + pair(zp1, zp2, -2) + pair(zm1, zm2, 2) + pair(z2, z2x, 4)
+    first = pl.program_id(0) < pl.num_programs(0) // 2
+    far_own = jnp.where(first, ra[...], rb[...])
+    far_h = jnp.where(first, rc[...], rd[...])
+    total = pair(own[...], h[...], 0) + pair(zp1[...], zp2[...], -2) + pair(zm1[...], zm2[...], 2)
+    total += pair(far_own, far_h, 4)
     out[...] = total.astype(out.dtype)
 
 
 def back_transform(factors, shards):
     rows = shards[0].shape[0]
+    half = rows // BLOCK // 2
     block = pl.BlockSpec((BLOCK, LANES), lambda i: (i, 0))
+    low = pl.BlockSpec((BLOCK, LANES), lambda i: (jnp.minimum(i, half - 1), 0))
+    high = pl.BlockSpec((BLOCK, LANES), lambda i: (jnp.maximum(i - half, 0), 0))
     resident = pl.BlockSpec((4, PAIR, LANES), lambda i: (0, 0, 0))
     return pl.pallas_call(
         product_kernel,
         grid=(rows // BLOCK,),
         out_shape=jax.ShapeDtypeStruct((rows, 2 * LANES), BF16),
-        in_specs=[resident] * 4 + [block] * 8,
+        in_specs=[resident] * 4 + [block] * 6 + [low, high, low, high],
         out_specs=pl.BlockSpec((BLOCK, 2 * LANES), lambda i: (i, 0)),
         scratch_shapes=[pltpu.VMEM((CHIPS, PAIR, 2 * LANES), BF16)],
         compiler_params=pltpu.CompilerParams(vmem_limit_bytes=16 << 20),
@@ -271,20 +277,19 @@
                     pairs.append((row * CHIPS + col, row * CHIPS + moved(col)))
         return lax.ppermute(value, ("row", "col"), pairs)
 
-    inv_mine, inv_send, small, rhs_mine = setup(coupling, selected, schur_rows, inverses)
-    inv_other = row_move(inv_send, SWAP)
-    small = row_move(small, SWAP)
-    t_other = small[:NB]
-    t_pair = jnp.where(is_even, jnp.concatenate([schur_rows, t_other]), jnp.concatenate([t_other, schur_rows]))
-    t0 = jnp.stack([t_pair, tile_move(t_pair, "tx", lambda c: c ^ 1)])
-    t1, t2, t3 = [tile_move(t0, f"tz{j}", lambda c, j=j: (c + 2 * j) % CHIPS) for j in (1, 2, 3)]
+    t0 = jnp.stack([schur_rows, tile_move(schur_rows, "tx", lambda c: c ^ 1)])
+    parts = [t0] + [tile_move(t0, f"tz{j}", lambda c, j=j: (c + 2 * j) % CHIPS) for j in (1, 2, 3)]
+    inv_from = row_move(inverses, SWAP)
 
     zp1, zm1 = col_shift(schur_basis, 2), col_shift(schur_basis, -2)
-    z2, h = col_shift(schur_basis, 4), across(schur_basis)
-
-    received = {"small": small, "t0": t0, "t1": t1, "t2": t2, "t3": t3, "inv_from": inv_other}
-    state = solve_step(0, {"rhs_mine": rhs_mine, "inv_mine": inv_mine, **received})
-    kept = {"inv_mine": inv_mine, "inv_other": state["inv_other"], "tiles": state["tiles_out"]}
+    h = across(schur_basis)
+    split = schur_basis.shape[0] // 2
+
+    inv_mine, inv_other, sent, rhs_mine = setup(coupling, selected, parts, inverses, inv_from)
+    swapped = row_move(sent, SWAP)
+    kept = {"inv_mine": inv_mine, "inv_other": inv_other}
+    state = solve_step(0, {"rhs_mine": rhs_mine, "sent": sent, "swapped": swapped, **kept})
+    kept["tiles"] = state["tiles_out"]
     late = {}
     for step in range(1, CHIPS):
         near, far2, far3 = moves(step - 1)
@@ -292,19 +297,22 @@
         operands.update(late)
         late = {name: row_move(state["x"], pairs) for name, pairs in (("far2", far2), ("far3", far3)) if pairs}
         state = solve_step(step, {**operands, **kept})
-        if step == 3:
+        if step == 2:
             h, _ = lax.optimization_barrier((h, state["x"]))
             zp2, zm2 = col_shift(h, 2), col_shift(h, -2)
-        if step == 4:
-            z2, _ = lax.optimization_barrier((z2, state["x"]))
-            z2x = across(z2)
+        if step == 3:
+            zp1, zm1, _ = lax.optimization_barrier((zp1, zm1, state["x"]))
+            ra, rb = col_shift(zp1[:split], 2), col_shift(zm1[split:], -2)
+        if step == 6:
+            zp2, zm2, _ = lax.optimization_barrier((zp2, zm2, state["x"]))
+            rc, rd = col_shift(zp2[:split], 2), col_shift(zm2[split:], -2)
 
     factor = state["factor"]
     same = stack4(factor, *[row_move(factor, shift(2 * CHIPS, 4 * j)) for j in (1, 2, 3)])
     cross = row_move(same, XLO)
     same_swap = row_move(same, SWAP)
     cross_swap = row_move(cross, SWAP)
-    eigen_rows = back_transform((same, same_swap, cross, cross_swap), (schur_basis, h, zp1, zp2, zm1, zm2, z2, z2x))
+    eigen_rows = back_transform((same, same_swap, cross, cross_swap), (schur_basis, h, zp1, zp2, zm1, zm2, ra, rb, rc, rd))
 
     mine, theirs = state["mine"], row_move(state["theirs"], SWAP)
     solved = jnp.where(is_even, jnp.concatenate([mine, theirs], axis=1), jnp.concatenate([theirs, mine], axis=1))

time: 130 us -> 145 us (1.12)
  waiting for transfers between devices: 60.4 us -> 71.7 us
  local copies, waits for them, and re-layouts: 2.48 us -> 8.38 us
  starting transfers between devices: 51.5 us -> 48.1 us
  Pallas kernels: 12.3 us -> 10.7 us
  other arithmetic: 0.66 us -> 2.24 us
    ppermute x27, waiting for transfers between devices: 41.4 us -> 51.6 us  [row_move(): return lax.ppermute(value, 'row', pairs)]
    unnamed x10 -> x18, local copies, waits for them, and re-layouts: 2.48 us -> 5.99 us
    ppermute x2 -> x1, starting transfers between devices: 5.75 us -> 3.21 us  [across(): return lax.ppermute(value, 'col', XHI)]
    slice x0 -> x4, local copies, waits for them, and re-layouts: none -> 2.38 us  [the longest x2 1.57 us: per_device(): rc, rd = (col_shift(zp2[:split], 2), col_shift(zm2[split:], -2))]
    pallas_call x1, Pallas kernels: 3.84 us -> 1.61 us  [setup(): pl.pallas_call(setup_kernel, out_shape=(half, half, pltpu.VMEM(((CHIPS +...]
    pallas_call x1, Pallas kernels: 4.07 us -> 6.01 us  [back_transform(): pl.pallas_call(product_kernel, grid=(rows // BLOCK,), out_shape=jax.Shape...]
    ppermute x5 -> x8, starting transfers between devices: 10.2 us -> 10.6 us  [col_shift(): return lax.ppermute(value, 'col', shift(CHIPS, by))]
  transfers between devices with their start and end apart: 38 -> 40, of which waited for: 13 -> 15; matrix products, arithmetic and copies ran while one was open for 1% -> 3% of each run, Pallas kernels for 3% -> 3%
where the time goes in v2:
time: 145 us; the launch traced here: 142 us
  waiting for transfers between devices  71.7 us (49%)
  starting transfers between devices  48.1 us (33%)
  Pallas kernels  10.7 us (7%)
  local copies, waits for them, and re-layouts  8.38 us (6%)
  other arithmetic  2.24 us (2%)
    ppermute x27, waiting for transfers between devices, row_move(): return lax.ppermute(value, 'row', pairs)  51.6 us
    ppermute x4, waiting for transfers between devices, tile_move(): return lax.ppermute(value, ('row', 'col'), pairs)  20.1 us
    ppermute x27, starting transfers between devices, row_move(): return lax.ppermute(value, 'row', pairs)  19.7 us
    ppermute x4, starting transfers between devices, tile_move(): return lax.ppermute(value, ('row', 'col'), pairs)  14.6 us
    ppermute x8, starting transfers between devices, col_shift(): return lax.ppermute(value, 'col', shift(CHIPS, by))  10.6 us
    pallas_call x1, Pallas kernels, back_transform(): pl.pallas_call(product_kernel, grid=(rows // BLOCK,), out_shape=jax.Shape...  6.01 us
    unnamed x18, local copies, waits for them, and re-layouts  5.99 us
    ppermute x1, starting transfers between devices, across(): return lax.ppermute(value, 'col', XHI)  3.21 us
  transfers between devices with their start and end apart: 40, of which 15 were waited for; matrix products, arithmetic and copies ran while one was open for 3% of the time, Pallas kernels for 3%

profile of v2, /device:TPU:0, one launch (start us, length us, event | category | flops | bytes accessed | tf_op | source)
XLA Modules:
  0.0 142.2 jit_solution(4040912865984671904)
XLA Ops:
  0.7 3.2 %collective-permute-start.30 = (bf16[3072,128]{1,0:T(8,128)(2,1)}, bf16[3072,128]{1,0:T(8,128)(2,1)S(1)}, u32[]{:S(2)}, u32[]{:S(2)}) collective-permute-start(bf16[3072,128]{1,0:T(8,128)(2,1)} %own.1), channel_id=1, source_target_pairs={{0,1},{1,0},{2,3},{3,2},{4,5},{5,4},{6,7},{7,6},{8,9},{9,8},{10,11... | collective-permute-start | bytes 2359304 | tf_op jit(solution)/shard_map/ppermute | solution.py:269
  3.9 2.3 %collective-permute-start = (f32[64,128]{1,0:T(8,128)}, f32[64,128]{1,0:T(8,128)S(1)}, u32[]{:S(2)}, u32[]{:S(2)}) collective-permute-start(f32[64,128]{1,0:T(8,128)} %param.5), channel_id=1, source_target_pairs={{0,1},{1,0},{2,3},{3,2},{4,5},{5,4},{6,7},{7,6},{8,9},{9,8},{10,11... | collective-permute-start | bytes 98312 | tf_op jit(solution)/shard_map/ppermute | solution.py:278
  6.2 16.8 %collective-permute-done = f32[64,128]{1,0:T(8,128)S(1)} collective-permute-done((f32[64,128]{1,0:T(8,128)}, f32[64,128]{1,0:T(8,128)S(1)}, u32[]{:S(2)}, u32[]{:S(2)}) %collective-permute-start) | collective-permute-done | bytes 32800 | tf_op jit(solution)/shard_map/ppermute | solution.py:278
  23.1 0.8 pad_maximum_fusion.t0
  23.8 3.9 %collective-permute-start.1 = (f32[2,64,128]{2,1,0:T(8,128)S(1)}, f32[2,64,128]{2,1,0:T(8,128)S(1)}, u32[]{:S(2)}, u32[]{:S(2)}) collective-permute-start(f32[2,64,128]{2,1,0:T(8,128)S(1)} %pad_maximum_fusion.t0), channel_id=1, source_target_pairs={{0,2},{1,3},{2,4},{3,5},{4,6},{5,7},{6,0},{7,1},{8,10},{9,11},{10,... | collective-permute-start | bytes 196616 | tf_op jit(solution)/shard_map/ppermute | solution.py:278
  27.8 5.5 %collective-permute-start.2 = (f32[2,64,128]{2,1,0:T(8,128)S(1)}, f32[2,64,128]{2,1,0:T(8,128)S(1)}, u32[]{:S(2)}, u32[]{:S(2)}) collective-permute-start(f32[2,64,128]{2,1,0:T(8,128)S(1)} %pad_maximum_fusion.t0), channel_id=1, source_target_pairs={{0,4},{1,5},{2,6},{3,7},{4,0},{5,1},{6,2},{7,3},{8,12},{9,13},{10,... | collective-permute-start | bytes 196616 | tf_op jit(solution)/shard_map/ppermute | solution.py:278
  33.3 2.9 %collective-permute-start.3 = (f32[2,64,128]{2,1,0:T(8,128)S(1)}, f32[2,64,128]{2,1,0:T(8,128)S(1)}, u32[]{:S(2)}, u32[]{:S(2)}) collective-permute-start(f32[2,64,128]{2,1,0:T(8,128)S(1)} %pad_maximum_fusion.t0), channel_id=1, source_target_pairs={{0,6},{1,7},{2,0},{3,1},{4,2},{5,3},{6,4},{7,5},{8,14},{9,15},{10,... | collective-permute-start | bytes 196616 | tf_op jit(solution)/shard_map/ppermute | solution.py:278
  36.2 3.2 %collective-permute-done.3.t3 = f32[2,64,128]{2,1,0:T(8,128)S(1)} collective-permute-done((f32[2,64,128]{2,1,0:T(8,128)S(1)}, f32[2,64,128]{2,1,0:T(8,128)S(1)}, u32[]{:S(2)}, u32[]{:S(2)}) %collective-permute-start.3) | collective-permute-done | bytes 65568 | tf_op jit(solution)/shard_map/ppermute | solution.py:278
  39.4 1.0 copy-done.4
  40.5 0.7 copy-done.8
  41.2 1.6 %setup.1 = (f32[64,64,128]{2,1,0:T(8,128)S(1)}, f32[64,64,128]{2,1,0:T(8,128)S(1)}, f32[576,128]{1,0:T(8,128)S(1)}, f32[64,128]{1,0:T(8,128)S(1)}) custom-call(f32[64,2048]{1,0:T(8,128)S(1)} %copy-done.4, s32[1,256]{1,0:T(1,128)S(1)} %bitcast.3, f32[2,64,128]{2,1,0:T(8,128)S(1)} %pad_maximum_fusion.t0, f32[2,64,128]{2,1,0:T(8,128)S(1)} %collective-permute-done.1.t1, ...), custom_call_target="tpu_custom_call" | custom-call | tf_op jit(solution)/shard_map/setup/pallas_call | solution.py:81
  42.9 1.6 %collective-permute-done.5.refs_2_ = f32[576,128]{1,0:T(8,128)S(1)} collective-permute-done((f32[576,128]{1,0:T(8,128)S(1)}, f32[576,128]{1,0:T(8,128)S(1)}, u32[]{:S(2)}, u32[]{:S(2)}) %collective-permute-start.5) | collective-permute-done | bytes 294944 | tf_op jit(solution)/shard_map/ppermute | solution.py:266
  44.5 0.8 collective-permute-start.6
  45.3 0.3 copy-done
  45.6 3.2 %collective-permute-start.32 = (bf16[3072,128]{1,0:T(8,128)(2,1)S(1)}, bf16[3072,128]{1,0:T(8,128)(2,1)S(1)}, u32[]{:S(2)}, u32[]{:S(2)}) collective-permute-start(bf16[3072,128]{1,0:T(8,128)(2,1)S(1)} %copy-done), channel_id=1, source_target_pairs={{0,6},{1,7},{2,0},{3,1},{4,2},{5,3},{6,4},{7,5},{8,14},{9,15},{10,... | collective-permute-start | bytes 2359304 | tf_op jit(solution)/shard_map/ppermute | solution.py:263
  48.8 0.7 collective-permute-start.8
  49.5 0.7 collective-permute-start.9
  50.2 0.7 collective-permute-start.7
  50.9 0.7 collective-permute-start.11
  51.7 3.2 %collective-permute-start.34 = (bf16[3072,128]{1,0:T(8,128)(2,1)S(1)}, bf16[3072,128]{1,0:T(8,128)(2,1)S(1)}, u32[]{:S(2)}, u32[]{:S(2)}) collective-permute-start(bf16[3072,128]{1,0:T(8,128)(2,1)S(1)} %collective-permute-done.30.h), channel_id=1, source_target_pairs={{0,6},{1,7},{2,0},{3,1},{4,2},{5,3},{6,4},{7,5},{8,14},{9,15},{10,... | collective-permute-start | bytes 2359304 | tf_op jit(solution)/shard_map/ppermute | solution.py:263
  55.0 0.7 collective-permute-start.12
  55.6 0.7 collective-permute-start.10
  56.3 0.7 collective-permute-start.14
  57.0 1.3 collective-permute-start.15
  58.3 11.0 %collective-permute-done.15.refs_4_ = f32[128,128]{1,0:T(8,128)S(1)} collective-permute-done((f32[128,128]{1,0:T(8,128)S(1)}, f32[128,128]{1,0:T(8,128)S(1)}, u32[]{:S(2)}, u32[]{:S(2)}) %collective-permute-start.15) | collective-permute-done | bytes 65568 | tf_op jit(solution)/shard_map/ppermute | solution.py:266
  69.3 0.7 collective-permute-start.13
  70.0 1.3 collective-permute-start.17
  71.3 6.4 %collective-permute-done.17.refs_3_ = f32[128,128]{1,0:T(8,128)S(1)} collective-permute-done((f32[128,128]{1,0:T(8,128)S(1)}, f32[128,128]{1,0:T(8,128)S(1)}, u32[]{:S(2)}, u32[]{:S(2)}) %collective-permute-start.17) | collective-permute-done | bytes 65568 | tf_op jit(solution)/shard_map/ppermute | solution.py:266
  77.6 1.3 collective-permute-start.18
  78.9 0.2 solve_step.12
  79.2 7.0 %collective-permute-done.18.refs_4_ = f32[128,128]{1,0:T(8,128)S(1)} collective-permute-done((f32[128,128]{1,0:T(8,128)S(1)}, f32[128,128]{1,0:T(8,128)S(1)}, u32[]{:S(2)}, u32[]{:S(2)}) %collective-permute-start.18) | collective-permute-done | bytes 65568 | tf_op jit(solution)/shard_map/ppermute | solution.py:266
  86.2 0.7 collective-permute-start.16
  86.9 1.3 collective-permute-start.20
  88.2 0.6 solve_step.13
  88.8 1.3 collective-permute-start.21
  90.1 0.7 collective-permute-start.19
  90.8 3.7 %collective-permute-done.20.refs_3_ = f32[128,128]{1,0:T(8,128)S(1)} collective-permute-done((f32[128,128]{1,0:T(8,128)S(1)}, f32[128,128]{1,0:T(8,128)S(1)}, u32[]{:S(2)}, u32[]{:S(2)}) %collective-permute-start.20) | collective-permute-done | bytes 65568 | tf_op jit(solution)/shard_map/ppermute | solution.py:266
  94.5 0.4 collective-permute-start.35
  94.9 5.1 %collective-permute-done.21.refs_4_ = f32[128,128]{1,0:T(8,128)S(1)} collective-permute-done((f32[128,128]{1,0:T(8,128)S(1)}, f32[128,128]{1,0:T(8,128)S(1)}, u32[]{:S(2)}, u32[]{:S(2)}) %collective-permute-start.21) | collective-permute-done | bytes 65568 | tf_op jit(solution)/shard_map/ppermute | solution.py:266
  99.9 1.3 collective-permute-start.23
  101.2 0.4 solve_step.14
  101.7 1.3 collective-permute-start.22
  103.0 0.8 slice.13
  103.8 2.3 %collective-permute-done.23.refs_3_ = f32[128,128]{1,0:T(8,128)S(1)} collective-permute-done((f32[128,128]{1,0:T(8,128)S(1)}, f32[128,128]{1,0:T(8,128)S(1)}, u32[]{:S(2)}, u32[]{:S(2)}) %collective-permute-start.23) | collective-permute-done | bytes 65568 | tf_op jit(solution)/shard_map/ppermute | solution.py:266
  106.1 0.4 collective-permute-start.36
  106.5 1.3 collective-permute-done.22.refs_2_
  107.8 1.6 %solve_step.15 = (f32[128,128]{1,0:T(8,128)}, f32[128,128]{1,0:T(8,128)}, bf16[128,128]{1,0:T(8,128)(2,1)S(1)}, f32[64,128]{1,0:T(8,128)S(1)}, f32[64,128]{1,0:T(8,128)S(1)}) custom-call(f32[128,128]{1,0:T(8,128)S(1)} %get-tuple-element.46.refs_0_, f32[128,128]{1,0:T(8,128)S(1)} %get-tuple-element.47.refs_1_, ...), custom_call_target="tpu_custom_call" | custom-call | flops 8000000 | bytes 5000000 | tf_op jit(solution)/shard_map/solve_step/pallas_call | solution.py:188
  109.5 0.8 slice.14
  110.3 0.3 collective-permute-start.37
  110.6 0.8 slice.15
  111.3 3.0 %collective-permute-start.38 = (bf16[1536,128]{1,0:T(8,128)(2,1)}, bf16[1536,128]{1,0:T(8,128)(2,1)}, u32[]{:S(2)}, u32[]{:S(2)}) collective-permute-start(bf16[1536,128]{1,0:T(8,128)(2,1)} %slice.15), channel_id=1, source_target_pairs={{0,6},{1,7},{2,0},{3,1},{4,2},{5,3},{6,4},{7,5},{8,14},{9,15},{10,... | collective-permute-start | bytes 1179656 | tf_op jit(solution)/shard_map/ppermute | solution.py:263
  114.3 0.3 collective-permute-done.24.b
  114.6 5.4 %collective-permute-done.25.c = bf16[128,128]{1,0:T(8,128)(2,1)S(1)} collective-permute-done((bf16[128,128]{1,0:T(8,128)(2,1)S(1)}, bf16[128,128]{1,0:T(8,128)(2,1)S(1)}, u32[]{:S(2)}, u32[]{:S(2)}) %collective-permute-start.25) | collective-permute-done | bytes 32800 | tf_op jit(solution)/shard_map/ppermute | solution.py:266
  120.0 2.9 %collective-permute-start.26 = (bf16[128,128]{1,0:T(8,128)(2,1)S(1)}, bf16[128,128]{1,0:T(8,128)(2,1)S(1)}, u32[]{:S(2)}, u32[]{:S(2)}) collective-permute-start(bf16[128,128]{1,0:T(8,128)(2,1)S(1)} %get-tuple-element.48.a), channel_id=1, source_target_pairs={{0,96},{8,104},{16,112},{24,120},{32,0},{40,8},{48,16},{56,24},{64... | collective-permute-start | bytes 98312 | tf_op jit(solution)/shard_map/ppermute | solution.py:266
  123.0 1.6 %collective-permute-done.26.d = bf16[128,128]{1,0:T(8,128)(2,1)S(1)} collective-permute-done((bf16[128,128]{1,0:T(8,128)(2,1)S(1)}, bf16[128,128]{1,0:T(8,128)(2,1)S(1)}, u32[]{:S(2)}, u32[]{:S(2)}) %collective-permute-start.26) | collective-permute-done | bytes 32800 | tf_op jit(solution)/shard_map/ppermute | solution.py:266
  124.6 1.3 collective-permute-done.39
  125.9 0.7 copy-done.5
  126.6 0.2 collective-permute-start.27
  126.8 4.7 %collective-permute-done.28.cross = bf16[4,128,128]{2,1,0:T(8,128)(2,1)S(1)} collective-permute-done((bf16[4,128,128]{2,1,0:T(8,128)(2,1)S(1)}, bf16[4,128,128]{2,1,0:T(8,128)(2,1)S(1)}, u32[]{:S(2)}, u32[]{:S(2)}) %collective-permute-start.28) | collective-permute-done | bytes 131104 | tf_op jit(solution)/shard_map/ppermute | solution.py:266
  131.5 1.5 %maximum_select_fusion = f32[64,256]{1,0:T(8,128)} fusion(f32[64,128]{1,0:T(8,128)} %collective-permute-done.39, f32[64,128]{1,0:T(8,128)} %copy-done.7, pred[]{:T(512)S(6)} %eq.5), kind=kLoop, calls=%fused_computation.1 | loop fusion | flops 49152 | bytes 131073 | tf_op jit(solution)/shard_map/jit(_where)/select_n | solution.py:318
  133.0 1.1 copy-done.1
  134.1 1.1 copy-done.3
  135.2 1.0 copy-done.6
  136.2 6.0 %back_transform.1 = bf16[3072,256]{1,0:T(8,128)(2,1)} custom-call(bf16[4,128,128]{2,1,0:T(8,128)(2,1)S(1)} %stack4.1.same, bf16[4,128,128]{2,1,0:T(8,128)(2,1)S(1)} %collective-permute-done.27.same_swap, bf16[4,128,128]{2,1,0:T(8,128)(2,1)S(1)} %collective-permute-done.28.cross, bf16[4,128,128]{2,1,0:T(8,128)(2,1)} %collective-permute-done.29.cross_swap, ...), custom_call_target="tpu_custom_call" | custom-call | flops 1610612736 | bytes 8000000 | tf_op jit(solution)/shard_map/back_transform/pallas_call | solution.py:246
  (51 shorter events, 0.5 us)
Async XLA Ops:
  0.6 38.8 %collective-permute-start.4 = (f32[64,64,256]{2,1,0:T(8,128)}, f32[64,64,256]{2,1,0:T(8,128)S(1)}, u32[]{:S(2)}, u32[]{:S(2)}) collective-permute-start(f32[64,64,256]{2,1,0:T(8,128)} %inv.1), channel_id=1, source_target_pairs={{0,8},{8,0},{16,24},{24,16},{32,40},{40,32},{48,56},{56,48},{64,72... | collective-permute-start | bytes 12582920 | tf_op jit(solution)/shard_map/ppermute | solution.py:266
  0.7 50.9 %collective-permute-start.30 = (bf16[3072,128]{1,0:T(8,128)(2,1)}, bf16[3072,128]{1,0:T(8,128)(2,1)S(1)}, u32[]{:S(2)}, u32[]{:S(2)}) collective-permute-start(bf16[3072,128]{1,0:T(8,128)(2,1)} %own.1), channel_id=1, source_target_pairs={{0,1},{1,0},{2,3},{3,2},{4,5},{5,4},{6,7},{7,6},{8,9},{9,8},{10,11... | collective-permute-start | bytes 2359304 | tf_op jit(solution)/shard_map/ppermute | solution.py:269
  3.9 19.1 %collective-permute-start = (f32[64,128]{1,0:T(8,128)}, f32[64,128]{1,0:T(8,128)S(1)}, u32[]{:S(2)}, u32[]{:S(2)}) collective-permute-start(f32[64,128]{1,0:T(8,128)} %param.5), channel_id=1, source_target_pairs={{0,1},{1,0},{2,3},{3,2},{4,5},{5,4},{6,7},{7,6},{8,9},{9,8},{10,11... | collective-permute-start | bytes 98312 | tf_op jit(solution)/shard_map/ppermute | solution.py:278
  23.8 12.4 %collective-permute-start.1 = (f32[2,64,128]{2,1,0:T(8,128)S(1)}, f32[2,64,128]{2,1,0:T(8,128)S(1)}, u32[]{:S(2)}, u32[]{:S(2)}) collective-permute-start(f32[2,64,128]{2,1,0:T(8,128)S(1)} %pad_maximum_fusion.t0), channel_id=1, source_target_pairs={{0,2},{1,3},{2,4},{3,5},{4,6},{5,7},{6,0},{7,1},{8,10},{9,11},{10,... | collective-permute-start | bytes 196616 | tf_op jit(solution)/shard_map/ppermute | solution.py:278
  27.8 8.4 %collective-permute-start.2 = (f32[2,64,128]{2,1,0:T(8,128)S(1)}, f32[2,64,128]{2,1,0:T(8,128)S(1)}, u32[]{:S(2)}, u32[]{:S(2)}) collective-permute-start(f32[2,64,128]{2,1,0:T(8,128)S(1)} %pad_maximum_fusion.t0), channel_id=1, source_target_pairs={{0,4},{1,5},{2,6},{3,7},{4,0},{5,1},{6,2},{7,3},{8,12},{9,13},{10,... | collective-permute-start | bytes 196616 | tf_op jit(solution)/shard_map/ppermute | solution.py:278
  33.3 6.2 %collective-permute-start.3 = (f32[2,64,128]{2,1,0:T(8,128)S(1)}, f32[2,64,128]{2,1,0:T(8,128)S(1)}, u32[]{:S(2)}, u32[]{:S(2)}) collective-permute-start(f32[2,64,128]{2,1,0:T(8,128)S(1)} %pad_maximum_fusion.t0), channel_id=1, source_target_pairs={{0,6},{1,7},{2,0},{3,1},{4,2},{5,3},{6,4},{7,5},{8,14},{9,15},{10,... | collective-permute-start | bytes 196616 | tf_op jit(solution)/shard_map/ppermute | solution.py:278
  39.4 1.0 copy-start.4
  40.5 0.7 copy-start.8
  42.8 1.7 %collective-permute-start.5 = (f32[576,128]{1,0:T(8,128)S(1)}, f32[576,128]{1,0:T(8,128)S(1)}, u32[]{:S(2)}, u32[]{:S(2)}) collective-permute-start(f32[576,128]{1,0:T(8,128)S(1)} %get-tuple-element.30.refs_1_), channel_id=1, source_target_pairs={{0,8},{8,0},{16,24},{24,16},{32,40},{40,32},{48,56},{56,48},{64,72... | collective-permute-start | bytes 884744 | tf_op jit(solution)/shard_map/ppermute | solution.py:266
  44.4 1.1 copy-start
  44.5 5.0 %collective-permute-start.6 = (f32[128,128]{1,0:T(8,128)S(1)}, f32[128,128]{1,0:T(8,128)S(1)}, u32[]{:S(2)}, u32[]{:S(2)}) collective-permute-start(f32[128,128]{1,0:T(8,128)S(1)} %get-tuple-element.34.refs_1_), channel_id=1, source_target_pairs={{112,96},{120,104},{113,97},{121,105},{114,98},{122,106},{115,99},... | collective-permute-start | bytes 196616 | tf_op jit(solution)/shard_map/ppermute | solution.py:266
  45.6 43.2 %collective-permute-start.31 = (bf16[3072,128]{1,0:T(8,128)(2,1)S(1)}, bf16[3072,128]{1,0:T(8,128)(2,1)S(1)}, u32[]{:S(2)}, u32[]{:S(2)}) collective-permute-start(bf16[3072,128]{1,0:T(8,128)(2,1)S(1)} %copy-done), channel_id=1, source_target_pairs={{0,2},{1,3},{2,4},{3,5},{4,6},{5,7},{6,0},{7,1},{8,10},{9,11},{10,... | collective-permute-start | bytes 2359304 | tf_op jit(solution)/shard_map/ppermute | solution.py:263
  45.6 44.5 %collective-permute-start.32 = (bf16[3072,128]{1,0:T(8,128)(2,1)S(1)}, bf16[3072,128]{1,0:T(8,128)(2,1)S(1)}, u32[]{:S(2)}, u32[]{:S(2)}) collective-permute-start(bf16[3072,128]{1,0:T(8,128)(2,1)S(1)} %copy-done), channel_id=1, source_target_pairs={{0,6},{1,7},{2,0},{3,1},{4,2},{5,3},{6,4},{7,5},{8,14},{9,15},{10,... | collective-permute-start | bytes 2359304 | tf_op jit(solution)/shard_map/ppermute | solution.py:263
  48.8 1.4 collective-permute-start.8
  49.5 1.4 collective-permute-start.9
  50.2 1.4 collective-permute-start.7
  50.9 4.1 %collective-permute-start.11 = (f32[128,128]{1,0:T(8,128)S(1)}, f32[128,128]{1,0:T(8,128)S(1)}, u32[]{:S(2)}, u32[]{:S(2)}) collective-permute-start(f32[128,128]{1,0:T(8,128)S(1)} %get-tuple-element.37.refs_1_), channel_id=1, source_target_pairs={{96,64},{104,72},{112,48},{120,56},{97,65},{105,73},{113,49},{121,... | collective-permute-start | bytes 196616 | tf_op jit(solution)/shard_map/ppermute | solution.py:266
  51.6 6.7 %copy-start.2 = (bf16[3072,128]{1,0:T(8,128)(2,1)}, bf16[3072,128]{1,0:T(8,128)(2,1)S(1)}, u32[]{:S(2)}) copy-start(bf16[3072,128]{1,0:T(8,128)(2,1)S(1)} %collective-permute-done.30.h) | copy-start | bytes 2359300
  51.6 57.8 %collective-permute-start.33 = (bf16[3072,128]{1,0:T(8,128)(2,1)S(1)}, bf16[3072,128]{1,0:T(8,128)(2,1)S(1)}, u32[]{:S(2)}, u32[]{:S(2)}) collective-permute-start(bf16[3072,128]{1,0:T(8,128)(2,1)S(1)} %collective-permute-done.30.h), channel_id=1, source_target_pairs={{0,2},{1,3},{2,4},{3,5},{4,6},{5,7},{6,0},{7,1},{8,10},{9,11},{10,... | collective-permute-start | bytes 2359304 | tf_op jit(solution)/shard_map/ppermute | solution.py:263
  51.7 57.8 %collective-permute-start.34 = (bf16[3072,128]{1,0:T(8,128)(2,1)S(1)}, bf16[3072,128]{1,0:T(8,128)(2,1)S(1)}, u32[]{:S(2)}, u32[]{:S(2)}) collective-permute-start(bf16[3072,128]{1,0:T(8,128)(2,1)S(1)} %collective-permute-done.30.h), channel_id=1, source_target_pairs={{0,6},{1,7},{2,0},{3,1},{4,2},{5,3},{6,4},{7,5},{8,14},{9,15},{10,... | collective-permute-start | bytes 2359304 | tf_op jit(solution)/shard_map/ppermute | solution.py:263
  55.0 0.7 collective-permute-start.12
  55.6 0.7 collective-permute-start.10
  56.3 0.7 collective-permute-start.14
  57.0 12.3 %collective-permute-start.15 = (f32[128,128]{1,0:T(8,128)S(1)}, f32[128,128]{1,0:T(8,128)S(1)}, u32[]{:S(2)}, u32[]{:S(2)}) collective-permute-start(f32[128,128]{1,0:T(8,128)S(1)} %get-tuple-element.39.refs_1_), channel_id=1, source_target_pairs={{80,32},{88,40},{96,16},{104,24},{112,0},{120,8},{81,33},{89,41},{... | collective-permute-start | bytes 196616 | tf_op jit(solution)/shard_map/ppermute | solution.py:266
  69.3 0.7 collective-permute-start.13
  70.0 7.7 %collective-permute-start.17 = (f32[128,128]{1,0:T(8,128)S(1)}, f32[128,128]{1,0:T(8,128)S(1)}, u32[]{:S(2)}, u32[]{:S(2)}) collective-permute-start(f32[128,128]{1,0:T(8,128)S(1)} %get-tuple-element.41.refs_1_), channel_id=1, source_target_pairs={{64,32},{72,40},{80,16},{88,24},{96,0},{104,8},{65,33},{73,41},{81... | collective-permute-start | bytes 196616 | tf_op jit(solution)/shard_map/ppermute | solution.py:266
  77.6 8.6 %collective-permute-start.18 = (f32[128,128]{1,0:T(8,128)S(1)}, f32[128,128]{1,0:T(8,128)S(1)}, u32[]{:S(2)}, u32[]{:S(2)}) collective-permute-start(f32[128,128]{1,0:T(8,128)S(1)} %get-tuple-element.41.refs_1_), channel_id=1, source_target_pairs={{64,16},{72,24},{80,0},{88,8},{65,17},{73,25},{81,1},{89,9},{66,18... | collective-permute-start | bytes 196616 | tf_op jit(solution)/shard_map/ppermute | solution.py:266
  86.2 0.7 collective-permute-start.16
  86.9 7.7 %collective-permute-start.20 = (f32[128,128]{1,0:T(8,128)S(1)}, f32[128,128]{1,0:T(8,128)S(1)}, u32[]{:S(2)}, u32[]{:S(2)}) collective-permute-start(f32[128,128]{1,0:T(8,128)S(1)} %get-tuple-element.43.refs_1_), channel_id=1, source_target_pairs={{48,16},{56,24},{64,0},{72,8},{49,17},{57,25},{65,1},{73,9},{50,18... | collective-permute-start | bytes 196616 | tf_op jit(solution)/shard_map/ppermute | solution.py:266
  88.8 11.1 %collective-permute-start.21 = (f32[128,128]{1,0:T(8,128)S(1)}, f32[128,128]{1,0:T(8,128)S(1)}, u32[]{:S(2)}, u32[]{:S(2)}) collective-permute-start(f32[128,128]{1,0:T(8,128)S(1)} %get-tuple-element.43.refs_1_), channel_id=1, source_target_pairs={{48,0},{56,8},{49,1},{57,9},{50,2},{58,10},{51,3},{59,11},{52,4},{... | collective-permute-start | bytes 196616 | tf_op jit(solution)/shard_map/ppermute | solution.py:266
  90.1 11.1 %collective-permute-start.19 = (f32[128,128]{1,0:T(8,128)S(1)}, f32[128,128]{1,0:T(8,128)S(1)}, u32[]{:S(2)}, u32[]{:S(2)}) collective-permute-start(f32[128,128]{1,0:T(8,128)S(1)} %get-tuple-element.45.refs_1_), channel_id=1, source_target_pairs={{32,16},{40,24},{33,17},{41,25},{34,18},{42,26},{35,19},{43,27},{3... | collective-permute-start | bytes 196616 | tf_op jit(solution)/shard_map/ppermute | solution.py:266
  94.5 31.4 %collective-permute-start.35 = (bf16[1536,128]{1,0:T(8,128)(2,1)S(1)}, bf16[1536,128]{1,0:T(8,128)(2,1)S(1)}, u32[]{:S(2)}, u32[]{:S(2)}) collective-permute-start(bf16[1536,128]{1,0:T(8,128)(2,1)S(1)} %slice.12), channel_id=1, source_target_pairs={{0,2},{1,3},{2,4},{3,5},{4,6},{5,7},{6,0},{7,1},{8,10},{9,11},{10,... | collective-permute-start | bytes 1179656 | tf_op jit(solution)/shard_map/ppermute | solution.py:263
  99.9 6.1 %collective-permute-start.23 = (f32[128,128]{1,0:T(8,128)S(1)}, f32[128,128]{1,0:T(8,128)S(1)}, u32[]{:S(2)}, u32[]{:S(2)}) collective-permute-start(f32[128,128]{1,0:T(8,128)S(1)} %get-tuple-element.45.refs_1_), channel_id=1, source_target_pairs={{32,0},{40,8},{33,1},{41,9},{34,2},{42,10},{35,3},{43,11},{36,4},{... | collective-permute-start | bytes 196616 | tf_op jit(solution)/shard_map/ppermute | solution.py:266
  101.7 6.2 %collective-permute-start.22 = (f32[128,128]{1,0:T(8,128)S(1)}, f32[128,128]{1,0:T(8,128)S(1)}, u32[]{:S(2)}, u32[]{:S(2)}) collective-permute-start(f32[128,128]{1,0:T(8,128)S(1)} %get-tuple-element.47.refs_1_), channel_id=1, source_target_pairs={{16,0},{24,8},{17,1},{25,9},{18,2},{26,10},{19,3},{27,11},{20,4},{... | collective-permute-start | bytes 196616 | tf_op jit(solution)/shard_map/ppermute | solution.py:266
  106.1 26.9 %collective-permute-start.36 = (bf16[1536,128]{1,0:T(8,128)(2,1)}, bf16[1536,128]{1,0:T(8,128)(2,1)}, u32[]{:S(2)}, u32[]{:S(2)}) collective-permute-start(bf16[1536,128]{1,0:T(8,128)(2,1)} %slice.13), channel_id=1, source_target_pairs={{0,6},{1,7},{2,0},{3,1},{4,2},{5,3},{6,4},{7,5},{8,14},{9,15},{10,... | collective-permute-start | bytes 1179656 | tf_op jit(solution)/shard_map/ppermute | solution.py:263
  109.5 22.0 %copy-start.7 = (f32[64,128]{1,0:T(8,128)}, f32[64,128]{1,0:T(8,128)S(1)}, u32[]{:S(2)}) copy-start(f32[64,128]{1,0:T(8,128)S(1)} %get-tuple-element.54) | copy-start | bytes 98308
  109.5 5.1 %collective-permute-start.24 = (bf16[128,128]{1,0:T(8,128)(2,1)S(1)}, bf16[128,128]{1,0:T(8,128)(2,1)S(1)}, u32[]{:S(2)}, u32[]{:S(2)}) collective-permute-start(bf16[128,128]{1,0:T(8,128)(2,1)S(1)} %get-tuple-element.48.a), channel_id=1, source_target_pairs={{0,32},{8,40},{16,48},{24,56},{32,64},{40,72},{48,80},{56,88},{64,... | collective-permute-start | bytes 98312 | tf_op jit(solution)/shard_map/ppermute | solution.py:266
  110.3 22.7 %collective-permute-start.37 = (bf16[1536,128]{1,0:T(8,128)(2,1)}, bf16[1536,128]{1,0:T(8,128)(2,1)}, u32[]{:S(2)}, u32[]{:S(2)}) collective-permute-start(bf16[1536,128]{1,0:T(8,128)(2,1)} %slice.14), channel_id=1, source_target_pairs={{0,2},{1,3},{2,4},{3,5},{4,6},{5,7},{6,0},{7,1},{8,10},{9,11},{10,... | collective-permute-start | bytes 1179656 | tf_op jit(solution)/shard_map/ppermute | solution.py:263
  111.3 21.6 %collective-permute-start.38 = (bf16[1536,128]{1,0:T(8,128)(2,1)}, bf16[1536,128]{1,0:T(8,128)(2,1)}, u32[]{:S(2)}, u32[]{:S(2)}) collective-permute-start(bf16[1536,128]{1,0:T(8,128)(2,1)} %slice.15), channel_id=1, source_target_pairs={{0,6},{1,7},{2,0},{3,1},{4,2},{5,3},{6,4},{7,5},{8,14},{9,15},{10,... | collective-permute-start | bytes 1179656 | tf_op jit(solution)/shard_map/ppermute | solution.py:263
  114.6 5.4 %collective-permute-start.25 = (bf16[128,128]{1,0:T(8,128)(2,1)S(1)}, bf16[128,128]{1,0:T(8,128)(2,1)S(1)}, u32[]{:S(2)}, u32[]{:S(2)}) collective-permute-start(bf16[128,128]{1,0:T(8,128)(2,1)S(1)} %get-tuple-element.48.a), channel_id=1, source_target_pairs={{0,64},{8,72},{16,80},{24,88},{32,96},{40,104},{48,112},{56,120},{... | collective-permute-start | bytes 98312 | tf_op jit(solution)/shard_map/ppermute | solution.py:266
  120.0 4.5 %collective-permute-start.26 = (bf16[128,128]{1,0:T(8,128)(2,1)S(1)}, bf16[128,128]{1,0:T(8,128)(2,1)S(1)}, u32[]{:S(2)}, u32[]{:S(2)}) collective-permute-start(bf16[128,128]{1,0:T(8,128)(2,1)S(1)} %get-tuple-element.48.a), channel_id=1, source_target_pairs={{0,96},{8,104},{16,112},{24,120},{32,0},{40,8},{48,16},{56,24},{64... | collective-permute-start | bytes 98312 | tf_op jit(solution)/shard_map/ppermute | solution.py:266
  124.6 1.3 collective-permute-start.39
  125.9 5.6 %collective-permute-start.28 = (bf16[4,128,128]{2,1,0:T(8,128)(2,1)S(1)}, bf16[4,128,128]{2,1,0:T(8,128)(2,1)S(1)}, u32[]{:S(2)}, u32[]{:S(2)}) collective-permute-start(bf16[4,128,128]{2,1,0:T(8,128)(2,1)S(1)} %stack4.1.same), channel_id=1, source_target_pairs={{0,16},{8,24},{16,0},{24,8},{32,48},{40,56},{48,32},{56,40},{64,80... | collective-permute-start | bytes 393224 | tf_op jit(solution)/shard_map/ppermute | solution.py:266
  125.9 0.7 copy-start.5
  126.6 6.3 %collective-permute-start.27 = (bf16[4,128,128]{2,1,0:T(8,128)(2,1)S(1)}, bf16[4,128,128]{2,1,0:T(8,128)(2,1)S(1)}, u32[]{:S(2)}, u32[]{:S(2)}) collective-permute-start(bf16[4,128,128]{2,1,0:T(8,128)(2,1)S(1)} %stack4.1.same), channel_id=1, source_target_pairs={{0,8},{8,0},{16,24},{24,16},{32,40},{40,32},{48,56},{56,48},{64,72... | collective-permute-start | bytes 393224 | tf_op jit(solution)/shard_map/ppermute | solution.py:266
  131.5 1.5 %collective-permute-start.29 = (bf16[4,128,128]{2,1,0:T(8,128)(2,1)S(1)}, bf16[4,128,128]{2,1,0:T(8,128)(2,1)}, u32[]{:S(2)}, u32[]{:S(2)}) collective-permute-start(bf16[4,128,128]{2,1,0:T(8,128)(2,1)S(1)} %collective-permute-done.28.cross), channel_id=1, source_target_pairs={{0,8},{8,0},{16,24},{24,16},{32,40},{40,32},{48,56},{56,48},{64,72... | collective-permute-start | bytes 393224 | tf_op jit(solution)/shard_map/ppermute | solution.py:266
  133.0 1.1 copy-start.1
  134.1 1.1 copy-start.3
  135.2 1.0 copy-start.6

commit v3 on v2

--- a/solution.py
+++ b/solution.py
@@ -17,16 +17,12 @@
 BF16 = jnp.bfloat16
 
 
-SWAP = [(i, i ^ 1) for i in range(2 * CHIPS)]
-XLO = [(i, i ^ 2) for i in range(2 * CHIPS)]
-XHI = [(i, i ^ 1) for i in range(CHIPS)]
-
 VMEM = pl.BlockSpec(memory_space=pltpu.VMEM)
 HBM = pl.BlockSpec(memory_space=pltpu.MemorySpace.HBM)
 
 
-def shift(values, by):
-    return [(i, (i + by) % values) for i in range(values)]
+def flip(values, mask):
+    return [(i, i ^ mask) for i in range(values)]
 
 
 def moves(step):
@@ -39,23 +35,25 @@
     return result
 
 
-def wrap(value, size):
-    return lax.rem(value + 2 * size, size)
-
-
 def core_lanes(core):
     return pl.ds(pl.multiple_of(core * LANES, LANES), LANES)
 
 
-def setup_kernel(coupling, selected, t0, t1, t2, t3, inv, inv_from, inv_mine, inv_other, send, rhs_mine, sem):
+def setup_kernel(candidates_from, selected_from, t0, t1, t2, t3, inv, inv_from, inv_mine, inv_other, send, rhs_mine, coupling, selected, sem):
     core = lax.rem(lax.axis_index("row"), 2)
-    mine = pltpu.make_async_copy(inv.at[:, :, core_lanes(core)], inv_mine, sem.at[0])
-    other = pltpu.make_async_copy(inv_from.at[:, :, core_lanes(core)], inv_other, sem.at[1])
-    mine.start()
-    other.start()
+    copies = [
+        pltpu.make_async_copy(candidates_from, coupling, sem.at[0]),
+        pltpu.make_async_copy(selected_from, selected, sem.at[1]),
+        pltpu.make_async_copy(inv.at[:, :, core_lanes(core)], inv_mine, sem.at[2]),
+        pltpu.make_async_copy(inv_from.at[:, :, core_lanes(core)], inv_other, sem.at[3]),
+    ]
+    for copy in copies:
+        copy.start()
     for index, tile in enumerate((t0, t1, t2, t3)):
         for half in range(2):
             send[pl.ds((2 * index + half) * NB, NB), :] = tile[half]
+    copies[0].wait()
+    copies[1].wait()
     candidates, columns = coupling.shape[1], selected.shape[1]
     piece = 256
     total = jnp.zeros((3 * NB, columns), F32)
@@ -72,8 +70,8 @@
     left, right = rhs[:, :LANES], rhs[:, LANES:]
     rhs_mine[...] = jnp.where(core == 0, left, right)
     send[pl.ds(CHIPS * NB, NB), :] = jnp.where(core == 0, right, left)
-    mine.wait()
-    other.wait()
+    copies[2].wait()
+    copies[3].wait()
 
 
 def setup(coupling, selected, parts, inverses, inv_from):
@@ -81,12 +79,20 @@
     return pl.pallas_call(
         setup_kernel,
         out_shape=(half, half, pltpu.VMEM(((CHIPS + 1) * NB, LANES), F32), pltpu.VMEM((NB, LANES), F32)),
-        in_specs=[VMEM] * 6 + [HBM] * 2,
+        in_specs=[HBM] * 2 + [VMEM] * 4 + [HBM] * 2,
         out_specs=(VMEM,) * 4,
-        scratch_shapes=[pltpu.SemaphoreType.DMA((2,))],
+        scratch_shapes=[
+            pltpu.VMEM(coupling.shape, F32),
+            pltpu.VMEM((1, selected.shape[0]), jnp.int32),
+            pltpu.SemaphoreType.DMA((4,)),
+        ],
         compiler_params=pltpu.CompilerParams(vmem_limit_bytes=16 << 20),
         name="setup",
-    )(coupling, selected[None, :], *parts, pltpu.with_memory_space_constraint(inverses, pltpu.HBM), inv_from)
+    )(hbm(coupling), hbm(selected[None, :]), *parts, hbm(inverses), inv_from)
+
+
+def hbm(value):
+    return pltpu.with_memory_space_constraint(value, pltpu.HBM)
 
 
 def apply_inverse(inv, pending):
@@ -104,9 +110,7 @@
     tiles = ref["tiles"] if step else ref["tiles_out"]
 
     def tile(source):
-        ahead = wrap(col // 2 - source // 2, CHIPS // 2)
-        across = lax.rem(col + source, 2)
-        return tiles[2 * ahead + across]
+        return tiles[lax.bitwise_xor(col, source)]
 
     def product(source, value):
         return jnp.dot(tile(source), value, precision=HIGHEST, preferred_element_type=F32)
@@ -173,8 +177,8 @@
     if step == 0:
         outs["tiles_out"] = pltpu.VMEM((CHIPS, PAIR, LANES), F32)
     if step == CHIPS - 1:
-        outs["factor"] = jax.ShapeDtypeStruct((PAIR, LANES), BF16)
-        outs["mine"] = outs["theirs"] = jax.ShapeDtypeStruct((NB, LANES), F32)
+        outs["factor"] = pltpu.VMEM((PAIR, LANES), BF16)
+        outs["mine"] = outs["theirs"] = pltpu.VMEM((NB, LANES), F32)
     names = list(operands) + list(outs)
     call = pl.pallas_call(
         functools.partial(step_kernel, step, names),
@@ -208,85 +212,73 @@
     )(*parts)
 
 
-def product_kernel(same, same_swap, cross, cross_swap, own, h, zp1, zp2, zm1, zm2, ra, rb, rc, rd, out, x_all):
+def product_kernel(same, same_swap, cross, cross_swap, mine, theirs, v0, v1, v2, v3, a4, b4, a5, b5, v6, v7, out, slab, x_all):
     row, col = lax.axis_index("row"), lax.axis_index("col")
     core, xlo, y = lax.rem(row, 2), lax.rem(row // 2, 2), row // 4
 
     @pl.when(pl.program_id(0) == 0)
     def _():
-        for back in range(4):
-            level = wrap(y - back, 4)
-            x_all[2 * level + xlo, :, core_lanes(core)] = same[back]
-            x_all[2 * level + xlo, :, core_lanes(1 - core)] = same_swap[back]
-            x_all[2 * level + 1 - xlo, :, core_lanes(core)] = cross[back]
-            x_all[2 * level + 1 - xlo, :, core_lanes(1 - core)] = cross_swap[back]
-
-    def pair(left, right, by):
-        source = wrap(col + by, CHIPS)
-        other = source + 1 - 2 * lax.rem(source, 2)
-        lhs = jnp.concatenate([left, right], axis=1)
-        rhs = jnp.concatenate([x_all[source], x_all[other]], axis=0)
-        return jnp.dot(lhs, rhs, preferred_element_type=F32)
+        for mask in range(4):
+            source = 2 * lax.bitwise_xor(y, mask) + xlo
+            for index, left, right in ((source, same, same_swap), (lax.bitwise_xor(source, 1), cross, cross_swap)):
+                slot = pl.ds(pl.multiple_of(lax.bitwise_xor(col, index) * PAIR, PAIR), PAIR)
+                x_all[slot, core_lanes(core)] = left[mask]
+                x_all[slot, core_lanes(1 - core)] = right[mask]
+        slab[:, core_lanes(core)] = mine[...]
+        slab[:, core_lanes(1 - core)] = theirs[...]
 
     first = pl.program_id(0) < pl.num_programs(0) // 2
-    far_own = jnp.where(first, ra[...], rb[...])
-    far_h = jnp.where(first, rc[...], rd[...])
-    total = pair(own[...], h[...], 0) + pair(zp1[...], zp2[...], -2) + pair(zm1[...], zm2[...], 2)
-    total += pair(far_own, far_h, 4)
-    out[...] = total.astype(out.dtype)
-
-
-def back_transform(factors, shards):
+    half = pl.num_programs(0) // 2
+    rows = pl.ds(pl.multiple_of(pl.program_id(0) * BLOCK, BLOCK), BLOCK)
+    part = pl.ds(pl.multiple_of(lax.rem(pl.program_id(0), half) * BLOCK, BLOCK), BLOCK)
+    v4 = jnp.where(first, a4[part, :], b4[part, :])
+    v5 = jnp.where(first, a5[part, :], b5[part, :])
+    lhs = jnp.concatenate([v0[rows, :], v1[rows, :], v2[rows, :], v3[rows, :], v4, v5, v6[rows, :], v7[rows, :]], axis=1)
+    out[...] = jnp.dot(lhs, x_all[...], preferred_element_type=F32).astype(out.dtype)
+
+
+def back_transform(factors, slabs, shards):
     rows = shards[0].shape[0]
     half = rows // BLOCK // 2
     block = pl.BlockSpec((BLOCK, LANES), lambda i: (i, 0))
     low = pl.BlockSpec((BLOCK, LANES), lambda i: (jnp.minimum(i, half - 1), 0))
     high = pl.BlockSpec((BLOCK, LANES), lambda i: (jnp.maximum(i - half, 0), 0))
-    resident = pl.BlockSpec((4, PAIR, LANES), lambda i: (0, 0, 0))
     return pl.pallas_call(
         product_kernel,
         grid=(rows // BLOCK,),
-        out_shape=jax.ShapeDtypeStruct((rows, 2 * LANES), BF16),
-        in_specs=[resident] * 4 + [block] * 6 + [low, high, low, high],
-        out_specs=pl.BlockSpec((BLOCK, 2 * LANES), lambda i: (i, 0)),
-        scratch_shapes=[pltpu.VMEM((CHIPS, PAIR, 2 * LANES), BF16)],
-        compiler_params=pltpu.CompilerParams(vmem_limit_bytes=16 << 20),
+        out_shape=(
+            jax.ShapeDtypeStruct((rows, 2 * LANES), BF16),
+            jax.ShapeDtypeStruct((NB, 2 * LANES), F32),
+        ),
+        in_specs=[VMEM] * 16,
+        out_specs=(pl.BlockSpec((BLOCK, 2 * LANES), lambda i: (i, 0)), VMEM),
+        scratch_shapes=[pltpu.VMEM((CHIPS * PAIR, 2 * LANES), BF16)],
+        compiler_params=pltpu.CompilerParams(vmem_limit_bytes=24 << 20),
         cost_estimate=pl.CostEstimate(flops=2 * rows * 1024 * 256, bytes_accessed=8_000_000, transcendentals=0),
         name="back_transform",
-    )(*factors, *shards)
+    )(*factors, *slabs, *shards)
 
 
 def per_device(schur_rows, inverses, coupling, selected, schur_basis):
-    is_even = lax.axis_index("row") % 2 == 0
-
-    def col_shift(value, by):
-        return lax.ppermute(value, "col", shift(CHIPS, by))
+    def col_flip(value, mask):
+        return lax.ppermute(value, "col", flip(CHIPS, mask))
 
     def row_move(value, pairs):
         return lax.ppermute(value, "row", pairs)
 
-    def across(value):
-        return lax.ppermute(value, "col", XHI)
-
-    def tile_move(value, name, moved):
-        pairs = []
-        for row in range(2 * CHIPS):
-            for col in range(CHIPS):
-                last = col if name == "tx" else col | 1
-                if last >= row // 2:
-                    pairs.append((row * CHIPS + col, row * CHIPS + moved(col)))
-        return lax.ppermute(value, ("row", "col"), pairs)
-
-    t0 = jnp.stack([schur_rows, tile_move(schur_rows, "tx", lambda c: c ^ 1)])
-    parts = [t0] + [tile_move(t0, f"tz{j}", lambda c, j=j: (c + 2 * j) % CHIPS) for j in (1, 2, 3)]
-    inv_from = row_move(inverses, SWAP)
-
-    zp1, zm1 = col_shift(schur_basis, 2), col_shift(schur_basis, -2)
-    h = across(schur_basis)
+    def row_flip(value, mask):
+        return row_move(value, flip(2 * CHIPS, mask))
+
+    t0 = jnp.stack([schur_rows, col_flip(schur_rows, 1)])
+    parts = [t0] + [col_flip(t0, mask) for mask in (2, 4, 6)]
+    inv_from = row_flip(inverses, 1)
+
+    v = {0: schur_basis, 1: col_flip(schur_basis, 1)}
+    v[2], v[6] = col_flip(schur_basis, 2), col_flip(schur_basis, 6)
     split = schur_basis.shape[0] // 2
 
     inv_mine, inv_other, sent, rhs_mine = setup(coupling, selected, parts, inverses, inv_from)
-    swapped = row_move(sent, SWAP)
+    swapped = row_flip(sent, 1)
     kept = {"inv_mine": inv_mine, "inv_other": inv_other}
     state = solve_step(0, {"rhs_mine": rhs_mine, "sent": sent, "swapped": swapped, **kept})
     kept["tiles"] = state["tiles_out"]
@@ -298,25 +290,21 @@
         late = {name: row_move(state["x"], pairs) for name, pairs in (("far2", far2), ("far3", far3)) if pairs}
         state = solve_step(step, {**operands, **kept})
         if step == 2:
-            h, _ = lax.optimization_barrier((h, state["x"]))
-            zp2, zm2 = col_shift(h, 2), col_shift(h, -2)
+            v[1], _ = lax.optimization_barrier((v[1], state["x"]))
+            v[3], v[7] = col_flip(v[1], 2), col_flip(v[1], 6)
         if step == 3:
-            zp1, zm1, _ = lax.optimization_barrier((zp1, zm1, state["x"]))
-            ra, rb = col_shift(zp1[:split], 2), col_shift(zm1[split:], -2)
+            v[2], v[6], _ = lax.optimization_barrier((v[2], v[6], state["x"]))
+            a4, b4 = col_flip(v[6][:split], 2), col_flip(v[2][split:], 6)
         if step == 6:
-            zp2, zm2, _ = lax.optimization_barrier((zp2, zm2, state["x"]))
-            rc, rd = col_shift(zp2[:split], 2), col_shift(zm2[split:], -2)
+            v[3], v[7], _ = lax.optimization_barrier((v[3], v[7], state["x"]))
+            a5, b5 = col_flip(v[7][:split], 2), col_flip(v[3][split:], 6)
 
     factor = state["factor"]
-    same = stack4(factor, *[row_move(factor, shift(2 * CHIPS, 4 * j)) for j in (1, 2, 3)])
-    cross = row_move(same, XLO)
-    same_swap = row_move(same, SWAP)
-    cross_swap = row_move(cross, SWAP)
-    eigen_rows = back_transform((same, same_swap, cross, cross_swap), (schur_basis, h, zp1, zp2, zm1, zm2, ra, rb, rc, rd))
-
-    mine, theirs = state["mine"], row_move(state["theirs"], SWAP)
-    solved = jnp.where(is_even, jnp.concatenate([mine, theirs], axis=1), jnp.concatenate([theirs, mine], axis=1))
-    return (eigen_rows, solved)
+    same = stack4(factor, *[row_flip(factor, 4 * mask) for mask in (1, 2, 3)])
+    cross = row_flip(same, 2)
+    factors = (same, row_flip(same, 1), cross, row_flip(cross, 1))
+    slabs = (state["mine"], row_flip(state["theirs"], 1))
+    return back_transform(factors, slabs, (v[0], v[1], v[2], v[3], a4, b4, a5, b5, v[6], v[7]))
 
 
 def solution(mesh):

time: 145 us -> 134 us (0.924); the launches traced: 142 us -> 133 us
  waiting for transfers between devices: 71.7 us -> 87.6 us
  starting transfers between devices: 48.1 us -> 34.3 us
  local copies, waits for them, and re-layouts: 8.38 us -> 0.38 us
  Pallas kernels: 10.7 us -> 8.96 us
  other arithmetic: 2.24 us -> 0.76 us
    ppermute x27, waiting for transfers between devices: 51.6 us -> 63.4 us  [row_move(): return lax.ppermute(value, 'row', pairs)]
    ppermute x13, starting transfers between devices: 28.4 us -> 17.6 us  [col_flip(): return lax.ppermute(value, 'col', flip(CHIPS, mask))]
    unnamed x18 -> x2, local copies, waits for them, and re-layouts: 5.99 us -> 0.27 us
    ppermute x13, waiting for transfers between devices: 20.1 us -> 24.2 us  [col_flip(): return lax.ppermute(value, 'col', flip(CHIPS, mask))]
    ppermute x27, starting transfers between devices: 19.7 us -> 16.8 us  [row_move(): return lax.ppermute(value, 'row', pairs)]
    slice x4, local copies, waits for them, and re-layouts: 2.38 us -> 0.11 us  [the longest x2 0.05 us: per_device(): a4, b4 = (col_flip(v[6][:split], 2), col_flip(v[2][split:], 6))]
    pallas_call x1, Pallas kernels: 6.01 us -> 4.07 us  [back_transform(): pl.pallas_call(product_kernel, grid=(rows // BLOCK,), out_shape=(jax.Shap...]
    select_n x1 -> x0, other arithmetic: 1.48 us -> none  [per_device(): jnp.where(is_even, jnp.concatenate([mine, theirs], axis=1), jnp.concatena...]
  transfers between devices with their start and end apart: 40 -> 40, of which waited for: 15 -> 17; matrix products, arithmetic and copies ran while one was open for 3% -> 1% of each run, Pallas kernels for 3% -> 4%
where the time goes in v3:
time: 134 us; the launch traced here: 133 us
  waiting for transfers between devices  87.6 us (65%)
  starting transfers between devices  34.3 us (26%)
  Pallas kernels  8.96 us (7%)
    ppermute x27, waiting for transfers between devices, row_move(): return lax.ppermute(value, 'row', pairs)  63.4 us
    ppermute x13, waiting for transfers between devices, col_flip(): return lax.ppermute(value, 'col', flip(CHIPS, mask))  24.2 us
    ppermute x13, starting transfers between devices, col_flip(): return lax.ppermute(value, 'col', flip(CHIPS, mask))  17.6 us
    ppermute x27, starting transfers between devices, row_move(): return lax.ppermute(value, 'row', pairs)  16.8 us
    pallas_call x1, Pallas kernels, back_transform(): pl.pallas_call(product_kernel, grid=(rows // BLOCK,), out_shape=(jax.Shap...  4.07 us
    pallas_call x8, Pallas kernels, solve_step(): result = call(*operands.values())  3.05 us
  transfers between devices with their start and end apart: 40, of which 17 were waited for; matrix products, arithmetic and copies ran while one was open for 1% of the time, Pallas kernels for 4%

profile of v3, /device:TPU:0, one launch (start us, length us, event | category | flops | bytes accessed | tf_op | source)
XLA Modules:
  0.0 133.0 jit_solution(5067549352128457274)
XLA Ops:
  0.6 0.1 collective-permute-start.4
  0.7 3.2 %collective-permute-start.31 = (bf16[3072,128]{1,0:T(8,128)(2,1)}, bf16[3072,128]{1,0:T(8,128)(2,1)S(1)}, u32[]{:S(2)}, u32[]{:S(2)}) collective-permute-start(bf16[3072,128]{1,0:T(8,128)(2,1)} %v0.1), channel_id=1, source_target_pairs={{0,1},{1,0},{2,3},{3,2},{4,5},{5,4},{6,7},{7,6},{8,9},{9,8},{10,11... | collective-permute-start | bytes 2359304 | tf_op jit(solution)/shard_map/ppermute | solution.py:264
  3.9 0.4 collective-permute-start
  4.3 18.7 %collective-permute-done = f32[64,128]{1,0:T(8,128)S(1)} collective-permute-done((f32[64,128]{1,0:T(8,128)}, f32[64,128]{1,0:T(8,128)S(1)}, u32[]{:S(2)}, u32[]{:S(2)}) %collective-permute-start) | collective-permute-done | bytes 32800 | tf_op jit(solution)/shard_map/ppermute | solution.py:264
  23.1 0.8 pad_maximum_fusion.t0
  23.8 2.0 %collective-permute-start.1 = (f32[2,64,128]{2,1,0:T(8,128)S(1)}, f32[2,64,128]{2,1,0:T(8,128)S(1)}, u32[]{:S(2)}, u32[]{:S(2)}) collective-permute-start(f32[2,64,128]{2,1,0:T(8,128)S(1)} %pad_maximum_fusion.t0), channel_id=1, source_target_pairs={{0,2},{1,3},{2,0},{3,1},{4,6},{5,7},{6,4},{7,5},{8,10},{9,11},{10,... | collective-permute-start | bytes 196616 | tf_op jit(solution)/shard_map/ppermute | solution.py:264
  25.9 3.6 %collective-permute-start.2 = (f32[2,64,128]{2,1,0:T(8,128)S(1)}, f32[2,64,128]{2,1,0:T(8,128)S(1)}, u32[]{:S(2)}, u32[]{:S(2)}) collective-permute-start(f32[2,64,128]{2,1,0:T(8,128)S(1)} %pad_maximum_fusion.t0), channel_id=1, source_target_pairs={{0,4},{1,5},{2,6},{3,7},{4,0},{5,1},{6,2},{7,3},{8,12},{9,13},{10,... | collective-permute-start | bytes 196616 | tf_op jit(solution)/shard_map/ppermute | solution.py:264
  29.5 0.0 collective-permute-start.3
  29.5 0.0 collective-permute-done.1.t1
  29.5 2.9 %collective-permute-done.2.t2 = f32[2,64,128]{2,1,0:T(8,128)S(1)} collective-permute-done((f32[2,64,128]{2,1,0:T(8,128)S(1)}, f32[2,64,128]{2,1,0:T(8,128)S(1)}, u32[]{:S(2)}, u32[]{:S(2)}) %collective-permute-start.2) | collective-permute-done | bytes 65568 | tf_op jit(solution)/shard_map/ppermute | solution.py:264
  32.4 2.5 %collective-permute-done.3.t3 = f32[2,64,128]{2,1,0:T(8,128)S(1)} collective-permute-done((f32[2,64,128]{2,1,0:T(8,128)S(1)}, f32[2,64,128]{2,1,0:T(8,128)S(1)}, u32[]{:S(2)}, u32[]{:S(2)}) %collective-permute-start.3) | collective-permute-done | bytes 65568 | tf_op jit(solution)/shard_map/ppermute | solution.py:264
  34.9 0.0 collective-permute-done.4.inv_from
  34.9 1.8 %setup.1 = (f32[64,64,128]{2,1,0:T(8,128)S(1)}, f32[64,64,128]{2,1,0:T(8,128)S(1)}, f32[576,128]{1,0:T(8,128)S(1)}, f32[64,128]{1,0:T(8,128)S(1)}) custom-call(f32[64,2048]{1,0:T(8,128)} %candidates_from.1, s32[1,256]{1,0:T(1,128)} %bitcast.5, f32[2,64,128]{2,1,0:T(8,128)S(1)} %pad_maximum_fusion.t0, f32[2,64,128]{2,1,0:T(8,128)S(1)} %collective-permute-done.1.t1, ...), custom_call_target="tpu_custom_call" | custom-call | tf_op jit(solution)/shard_map/setup/pallas_call | solution.py:79
  36.8 0.1 collective-permute-start.5
  36.9 1.6 %collective-permute-done.5.refs_2_ = f32[576,128]{1,0:T(8,128)S(1)} collective-permute-done((f32[576,128]{1,0:T(8,128)S(1)}, f32[576,128]{1,0:T(8,128)S(1)}, u32[]{:S(2)}, u32[]{:S(2)}) %collective-permute-start.5) | collective-permute-done | bytes 294944 | tf_op jit(solution)/shard_map/ppermute | solution.py:267
  38.4 0.1 solve_step.8
  38.5 0.8 collective-permute-start.6
  39.3 0.3 copy-done
  39.6 0.0 collective-permute-start.32
  39.6 0.9 collective-permute-start.33
  40.4 0.7 collective-permute-start.8
  41.1 0.7 collective-permute-start.9
  41.8 0.0 collective-permute-done.8.refs_3_
  41.8 0.7 collective-permute-start.7
  42.5 0.0 collective-permute-done.9.refs_4_
  42.5 0.7 collective-permute-start.11
  43.2 1.2 collective-permute-start.34
  44.5 2.6 %collective-permute-start.35 = (bf16[3072,128]{1,0:T(8,128)(2,1)S(1)}, bf16[3072,128]{1,0:T(8,128)(2,1)S(1)}, u32[]{:S(2)}, u32[]{:S(2)}) collective-permute-start(bf16[3072,128]{1,0:T(8,128)(2,1)S(1)} %collective-permute-done.31.v1), channel_id=1, source_target_pairs={{0,6},{1,7},{2,4},{3,5},{4,2},{5,3},{6,0},{7,1},{8,14},{9,15},{10,... | collective-permute-start | bytes 2359304 | tf_op jit(solution)/shard_map/ppermute | solution.py:264
  47.1 0.7 collective-permute-start.12
  47.8 0.7 collective-permute-start.10
  48.5 0.7 collective-permute-start.14
  49.2 1.3 collective-permute-start.15
  50.5 15.7 %collective-permute-done.15.refs_4_ = f32[128,128]{1,0:T(8,128)S(1)} collective-permute-done((f32[128,128]{1,0:T(8,128)S(1)}, f32[128,128]{1,0:T(8,128)S(1)}, u32[]{:S(2)}, u32[]{:S(2)}) %collective-permute-start.15) | collective-permute-done | bytes 65568 | tf_op jit(solution)/shard_map/ppermute | solution.py:267
  66.2 0.7 collective-permute-start.13
  66.9 1.3 collective-permute-start.17
  68.2 6.4 %collective-permute-done.17.refs_3_ = f32[128,128]{1,0:T(8,128)S(1)} collective-permute-done((f32[128,128]{1,0:T(8,128)S(1)}, f32[128,128]{1,0:T(8,128)S(1)}, u32[]{:S(2)}, u32[]{:S(2)}) %collective-permute-start.17) | collective-permute-done | bytes 65568 | tf_op jit(solution)/shard_map/ppermute | solution.py:267
  74.6 1.3 collective-permute-start.18
  75.9 0.2 solve_step.12
  76.1 7.0 %collective-permute-done.18.refs_4_ = f32[128,128]{1,0:T(8,128)S(1)} collective-permute-done((f32[128,128]{1,0:T(8,128)S(1)}, f32[128,128]{1,0:T(8,128)S(1)}, u32[]{:S(2)}, u32[]{:S(2)}) %collective-permute-start.18) | collective-permute-done | bytes 65568 | tf_op jit(solution)/shard_map/ppermute | solution.py:267
  83.1 0.7 collective-permute-start.16
  83.8 1.3 collective-permute-start.20
  85.1 0.6 solve_step.13
  85.7 1.3 collective-permute-start.21
  87.0 0.7 collective-permute-start.19
  87.7 3.7 %collective-permute-done.20.refs_3_ = f32[128,128]{1,0:T(8,128)S(1)} collective-permute-done((f32[128,128]{1,0:T(8,128)S(1)}, f32[128,128]{1,0:T(8,128)S(1)}, u32[]{:S(2)}, u32[]{:S(2)}) %collective-permute-start.20) | collective-permute-done | bytes 65568 | tf_op jit(solution)/shard_map/ppermute | solution.py:267
  91.5 0.1 collective-permute-start.36
  91.5 5.3 %collective-permute-done.21.refs_4_ = f32[128,128]{1,0:T(8,128)S(1)} collective-permute-done((f32[128,128]{1,0:T(8,128)S(1)}, f32[128,128]{1,0:T(8,128)S(1)}, u32[]{:S(2)}, u32[]{:S(2)}) %collective-permute-start.21) | collective-permute-done | bytes 65568 | tf_op jit(solution)/shard_map/ppermute | solution.py:267
  96.9 1.3 collective-permute-start.23
  98.2 0.4 solve_step.14
  98.6 1.3 collective-permute-start.22
  99.9 3.4 %collective-permute-done.23.refs_3_ = f32[128,128]{1,0:T(8,128)S(1)} collective-permute-done((f32[128,128]{1,0:T(8,128)S(1)}, f32[128,128]{1,0:T(8,128)S(1)}, u32[]{:S(2)}, u32[]{:S(2)}) %collective-permute-start.23) | collective-permute-done | bytes 65568 | tf_op jit(solution)/shard_map/ppermute | solution.py:267
  103.4 0.9 collective-permute-start.37
  104.3 0.5 collective-permute-done.22.refs_2_
  104.8 1.6 %solve_step.15 = (f32[128,128]{1,0:T(8,128)}, f32[128,128]{1,0:T(8,128)}, bf16[128,128]{1,0:T(8,128)(2,1)S(1)}, f32[64,128]{1,0:T(8,128)S(1)}, f32[64,128]{1,0:T(8,128)S(1)}) custom-call(f32[128,128]{1,0:T(8,128)S(1)} %get-tuple-element.46.refs_0_, f32[128,128]{1,0:T(8,128)S(1)} %get-tuple-element.47.refs_1_, ...), custom_call_target="tpu_custom_call" | custom-call | flops 8000000 | bytes 5000000 | tf_op jit(solution)/shard_map/solve_step/pallas_call | solution.py:192
  106.4 0.5 collective-permute-start.38
  107.0 2.1 %collective-permute-start.39 = (bf16[1536,128]{1,0:T(8,128)(2,1)S(1)}, bf16[1536,128]{1,0:T(8,128)(2,1)S(1)}, u32[]{:S(2)}, u32[]{:S(2)}) collective-permute-start(bf16[1536,128]{1,0:T(8,128)(2,1)S(1)} %slice.15), channel_id=1, source_target_pairs={{0,6},{1,7},{2,4},{3,5},{4,2},{5,3},{6,0},{7,1},{8,14},{9,15},{10,... | collective-permute-start | bytes 1179656 | tf_op jit(solution)/shard_map/ppermute | solution.py:264
  109.1 1.2 collective-permute-done.24.b
  110.3 5.4 %collective-permute-done.25.c = bf16[128,128]{1,0:T(8,128)(2,1)S(1)} collective-permute-done((bf16[128,128]{1,0:T(8,128)(2,1)S(1)}, bf16[128,128]{1,0:T(8,128)(2,1)S(1)}, u32[]{:S(2)}, u32[]{:S(2)}) %collective-permute-start.25) | collective-permute-done | bytes 32800 | tf_op jit(solution)/shard_map/ppermute | solution.py:267
  115.7 5.1 %collective-permute-done.26.d = bf16[128,128]{1,0:T(8,128)(2,1)S(1)} collective-permute-done((bf16[128,128]{1,0:T(8,128)(2,1)S(1)}, bf16[128,128]{1,0:T(8,128)(2,1)S(1)}, u32[]{:S(2)}, u32[]{:S(2)}) %collective-permute-start.26) | collective-permute-done | bytes 32800 | tf_op jit(solution)/shard_map/ppermute | solution.py:267
  120.9 1.2 collective-permute-done.30.theirs
  122.1 0.2 collective-permute-start.27
  122.2 5.4 %collective-permute-done.28.cross = bf16[4,128,128]{2,1,0:T(8,128)(2,1)S(1)} collective-permute-done((bf16[4,128,128]{2,1,0:T(8,128)(2,1)S(1)}, bf16[4,128,128]{2,1,0:T(8,128)(2,1)S(1)}, u32[]{:S(2)}, u32[]{:S(2)}) %collective-permute-start.28) | collective-permute-done | bytes 131104 | tf_op jit(solution)/shard_map/ppermute | solution.py:267
  127.6 1.3 %collective-permute-done.29.cross_swap = bf16[4,128,128]{2,1,0:T(8,128)(2,1)S(1)} collective-permute-done((bf16[4,128,128]{2,1,0:T(8,128)(2,1)S(1)}, bf16[4,128,128]{2,1,0:T(8,128)(2,1)S(1)}, u32[]{:S(2)}, u32[]{:S(2)}) %collective-permute-start.29) | collective-permute-done | bytes 131104 | tf_op jit(solution)/shard_map/ppermute | solution.py:267
  129.0 4.1 %back_transform.1 = (bf16[3072,256]{1,0:T(8,128)(2,1)}, f32[64,256]{1,0:T(8,128)}) custom-call(bf16[4,128,128]{2,1,0:T(8,128)(2,1)S(1)} %stack4.1.same, bf16[4,128,128]{2,1,0:T(8,128)(2,1)S(1)} %collective-permute-done.27.same_swap, bf16[4,128,128]{2,1,0:T(8,128)(2,1)S(1)} %collective-permute-done.28.cross, ...), custom_call_target="tpu_custom_call" | custom-call | flops 1610612736 | bytes 8000000 | tf_op jit(solution)/shard_map/back_transform/pallas_call | solution.py:246
  (34 shorter events, 0.3 us)
Async XLA Ops:
  0.6 34.3 %collective-permute-start.4 = (f32[64,64,256]{2,1,0:T(8,128)}, f32[64,64,256]{2,1,0:T(8,128)S(1)}, u32[]{:S(2)}, u32[]{:S(2)}) collective-permute-start(f32[64,64,256]{2,1,0:T(8,128)} %inv.1), channel_id=1, source_target_pairs={{0,8},{8,0},{16,24},{24,16},{32,40},{40,32},{48,56},{56,48},{64,72... | collective-permute-start | bytes 12582920 | tf_op jit(solution)/shard_map/ppermute | solution.py:267
  0.7 42.5 %collective-permute-start.31 = (bf16[3072,128]{1,0:T(8,128)(2,1)}, bf16[3072,128]{1,0:T(8,128)(2,1)S(1)}, u32[]{:S(2)}, u32[]{:S(2)}) collective-permute-start(bf16[3072,128]{1,0:T(8,128)(2,1)} %v0.1), channel_id=1, source_target_pairs={{0,1},{1,0},{2,3},{3,2},{4,5},{5,4},{6,7},{7,6},{8,9},{9,8},{10,11... | collective-permute-start | bytes 2359304 | tf_op jit(solution)/shard_map/ppermute | solution.py:264
  3.9 19.1 %collective-permute-start = (f32[64,128]{1,0:T(8,128)}, f32[64,128]{1,0:T(8,128)S(1)}, u32[]{:S(2)}, u32[]{:S(2)}) collective-permute-start(f32[64,128]{1,0:T(8,128)} %param.5), channel_id=1, source_target_pairs={{0,1},{1,0},{2,3},{3,2},{4,5},{5,4},{6,7},{7,6},{8,9},{9,8},{10,11... | collective-permute-start | bytes 98312 | tf_op jit(solution)/shard_map/ppermute | solution.py:264
  23.8 5.6 %collective-permute-start.1 = (f32[2,64,128]{2,1,0:T(8,128)S(1)}, f32[2,64,128]{2,1,0:T(8,128)S(1)}, u32[]{:S(2)}, u32[]{:S(2)}) collective-permute-start(f32[2,64,128]{2,1,0:T(8,128)S(1)} %pad_maximum_fusion.t0), channel_id=1, source_target_pairs={{0,2},{1,3},{2,0},{3,1},{4,6},{5,7},{6,4},{7,5},{8,10},{9,11},{10,... | collective-permute-start | bytes 196616 | tf_op jit(solution)/shard_map/ppermute | solution.py:264
  25.9 6.5 %collective-permute-start.2 = (f32[2,64,128]{2,1,0:T(8,128)S(1)}, f32[2,64,128]{2,1,0:T(8,128)S(1)}, u32[]{:S(2)}, u32[]{:S(2)}) collective-permute-start(f32[2,64,128]{2,1,0:T(8,128)S(1)} %pad_maximum_fusion.t0), channel_id=1, source_target_pairs={{0,4},{1,5},{2,6},{3,7},{4,0},{5,1},{6,2},{7,3},{8,12},{9,13},{10,... | collective-permute-start | bytes 196616 | tf_op jit(solution)/shard_map/ppermute | solution.py:264
  29.5 5.5 %collective-permute-start.3 = (f32[2,64,128]{2,1,0:T(8,128)S(1)}, f32[2,64,128]{2,1,0:T(8,128)S(1)}, u32[]{:S(2)}, u32[]{:S(2)}) collective-permute-start(f32[2,64,128]{2,1,0:T(8,128)S(1)} %pad_maximum_fusion.t0), channel_id=1, source_target_pairs={{0,6},{1,7},{2,4},{3,5},{4,2},{5,3},{6,0},{7,1},{8,14},{9,15},{10,... | collective-permute-start | bytes 196616 | tf_op jit(solution)/shard_map/ppermute | solution.py:264
  36.8 1.7 %collective-permute-start.5 = (f32[576,128]{1,0:T(8,128)S(1)}, f32[576,128]{1,0:T(8,128)S(1)}, u32[]{:S(2)}, u32[]{:S(2)}) collective-permute-start(f32[576,128]{1,0:T(8,128)S(1)} %get-tuple-element.30.refs_1_), channel_id=1, source_target_pairs={{0,8},{8,0},{16,24},{24,16},{32,40},{40,32},{48,56},{56,48},{64,72... | collective-permute-start | bytes 884744 | tf_op jit(solution)/shard_map/ppermute | solution.py:267
  38.4 1.1 copy-start
  38.5 2.6 %collective-permute-start.6 = (f32[128,128]{1,0:T(8,128)S(1)}, f32[128,128]{1,0:T(8,128)S(1)}, u32[]{:S(2)}, u32[]{:S(2)}) collective-permute-start(f32[128,128]{1,0:T(8,128)S(1)} %get-tuple-element.34.refs_1_), channel_id=1, source_target_pairs={{112,96},{120,104},{113,97},{121,105},{114,98},{122,106},{115,99},... | collective-permute-start | bytes 196616 | tf_op jit(solution)/shard_map/ppermute | solution.py:267
  39.6 46.1 %collective-permute-start.32 = (bf16[3072,128]{1,0:T(8,128)(2,1)S(1)}, bf16[3072,128]{1,0:T(8,128)(2,1)S(1)}, u32[]{:S(2)}, u32[]{:S(2)}) collective-permute-start(bf16[3072,128]{1,0:T(8,128)(2,1)S(1)} %copy-done), channel_id=1, source_target_pairs={{0,2},{1,3},{2,0},{3,1},{4,6},{5,7},{6,4},{7,5},{8,10},{9,11},{10,... | collective-permute-start | bytes 2359304 | tf_op jit(solution)/shard_map/ppermute | solution.py:264
  39.6 47.5 %collective-permute-start.33 = (bf16[3072,128]{1,0:T(8,128)(2,1)S(1)}, bf16[3072,128]{1,0:T(8,128)(2,1)S(1)}, u32[]{:S(2)}, u32[]{:S(2)}) collective-permute-start(bf16[3072,128]{1,0:T(8,128)(2,1)S(1)} %copy-done), channel_id=1, source_target_pairs={{0,6},{1,7},{2,4},{3,5},{4,2},{5,3},{6,0},{7,1},{8,14},{9,15},{10,... | collective-permute-start | bytes 2359304 | tf_op jit(solution)/shard_map/ppermute | solution.py:264
  40.4 1.4 %collective-permute-start.8 = (f32[128,128]{1,0:T(8,128)S(1)}, f32[128,128]{1,0:T(8,128)S(1)}, u32[]{:S(2)}, u32[]{:S(2)}) collective-permute-start(f32[128,128]{1,0:T(8,128)S(1)} %get-tuple-element.34.refs_1_), channel_id=1, source_target_pairs={{112,80},{120,88},{113,81},{121,89},{114,82},{122,90},{115,83},{12... | collective-permute-start | bytes 196616 | tf_op jit(solution)/shard_map/ppermute | solution.py:267
  41.1 1.4 %collective-permute-start.9 = (f32[128,128]{1,0:T(8,128)S(1)}, f32[128,128]{1,0:T(8,128)S(1)}, u32[]{:S(2)}, u32[]{:S(2)}) collective-permute-start(f32[128,128]{1,0:T(8,128)S(1)} %get-tuple-element.34.refs_1_), channel_id=1, source_target_pairs={{112,64},{120,72},{113,65},{121,73},{114,66},{122,74},{115,67},{12... | collective-permute-start | bytes 196616 | tf_op jit(solution)/shard_map/ppermute | solution.py:267
  41.8 1.4 %collective-permute-start.7 = (f32[128,128]{1,0:T(8,128)S(1)}, f32[128,128]{1,0:T(8,128)S(1)}, u32[]{:S(2)}, u32[]{:S(2)}) collective-permute-start(f32[128,128]{1,0:T(8,128)S(1)} %get-tuple-element.37.refs_1_), channel_id=1, source_target_pairs={{96,80},{104,88},{97,81},{105,89},{98,82},{106,90},{99,83},{107,91... | collective-permute-start | bytes 196616 | tf_op jit(solution)/shard_map/ppermute | solution.py:267
  42.5 4.6 %collective-permute-start.11 = (f32[128,128]{1,0:T(8,128)S(1)}, f32[128,128]{1,0:T(8,128)S(1)}, u32[]{:S(2)}, u32[]{:S(2)}) collective-permute-start(f32[128,128]{1,0:T(8,128)S(1)} %get-tuple-element.37.refs_1_), channel_id=1, source_target_pairs={{96,64},{104,72},{112,48},{120,56},{97,65},{105,73},{113,49},{121,... | collective-permute-start | bytes 196616 | tf_op jit(solution)/shard_map/ppermute | solution.py:267
  43.2 63.1 %collective-permute-start.34 = (bf16[3072,128]{1,0:T(8,128)(2,1)S(1)}, bf16[3072,128]{1,0:T(8,128)(2,1)S(1)}, u32[]{:S(2)}, u32[]{:S(2)}) collective-permute-start(bf16[3072,128]{1,0:T(8,128)(2,1)S(1)} %collective-permute-done.31.v1), channel_id=1, source_target_pairs={{0,2},{1,3},{2,0},{3,1},{4,6},{5,7},{6,4},{7,5},{8,10},{9,11},{10,... | collective-permute-start | bytes 2359304 | tf_op jit(solution)/shard_map/ppermute | solution.py:264
  44.5 61.9 %collective-permute-start.35 = (bf16[3072,128]{1,0:T(8,128)(2,1)S(1)}, bf16[3072,128]{1,0:T(8,128)(2,1)S(1)}, u32[]{:S(2)}, u32[]{:S(2)}) collective-permute-start(bf16[3072,128]{1,0:T(8,128)(2,1)S(1)} %collective-permute-done.31.v1), channel_id=1, source_target_pairs={{0,6},{1,7},{2,4},{3,5},{4,2},{5,3},{6,0},{7,1},{8,14},{9,15},{10,... | collective-permute-start | bytes 2359304 | tf_op jit(solution)/shard_map/ppermute | solution.py:264
  47.1 0.7 collective-permute-start.12
  47.8 0.7 collective-permute-start.10
  48.5 0.7 collective-permute-start.14
  49.2 17.1 %collective-permute-start.15 = (f32[128,128]{1,0:T(8,128)S(1)}, f32[128,128]{1,0:T(8,128)S(1)}, u32[]{:S(2)}, u32[]{:S(2)}) collective-permute-start(f32[128,128]{1,0:T(8,128)S(1)} %get-tuple-element.39.refs_1_), channel_id=1, source_target_pairs={{80,32},{88,40},{96,16},{104,24},{112,0},{120,8},{81,33},{89,41},{... | collective-permute-start | bytes 196616 | tf_op jit(solution)/shard_map/ppermute | solution.py:267
  66.2 0.7 collective-permute-start.13
  66.9 7.7 %collective-permute-start.17 = (f32[128,128]{1,0:T(8,128)S(1)}, f32[128,128]{1,0:T(8,128)S(1)}, u32[]{:S(2)}, u32[]{:S(2)}) collective-permute-start(f32[128,128]{1,0:T(8,128)S(1)} %get-tuple-element.41.refs_1_), channel_id=1, source_target_pairs={{64,32},{72,40},{80,16},{88,24},{96,0},{104,8},{65,33},{73,41},{81... | collective-permute-start | bytes 196616 | tf_op jit(solution)/shard_map/ppermute | solution.py:267
  74.6 8.6 %collective-permute-start.18 = (f32[128,128]{1,0:T(8,128)S(1)}, f32[128,128]{1,0:T(8,128)S(1)}, u32[]{:S(2)}, u32[]{:S(2)}) collective-permute-start(f32[128,128]{1,0:T(8,128)S(1)} %get-tuple-element.41.refs_1_), channel_id=1, source_target_pairs={{64,16},{72,24},{80,0},{88,8},{65,17},{73,25},{81,1},{89,9},{66,18... | collective-permute-start | bytes 196616 | tf_op jit(solution)/shard_map/ppermute | solution.py:267
  83.1 0.7 collective-permute-start.16
  83.8 7.7 %collective-permute-start.20 = (f32[128,128]{1,0:T(8,128)S(1)}, f32[128,128]{1,0:T(8,128)S(1)}, u32[]{:S(2)}, u32[]{:S(2)}) collective-permute-start(f32[128,128]{1,0:T(8,128)S(1)} %get-tuple-element.43.refs_1_), channel_id=1, source_target_pairs={{48,16},{56,24},{64,0},{72,8},{49,17},{57,25},{65,1},{73,9},{50,18... | collective-permute-start | bytes 196616 | tf_op jit(solution)/shard_map/ppermute | solution.py:267
  85.7 11.1 %collective-permute-start.21 = (f32[128,128]{1,0:T(8,128)S(1)}, f32[128,128]{1,0:T(8,128)S(1)}, u32[]{:S(2)}, u32[]{:S(2)}) collective-permute-start(f32[128,128]{1,0:T(8,128)S(1)} %get-tuple-element.43.refs_1_), channel_id=1, source_target_pairs={{48,0},{56,8},{49,1},{57,9},{50,2},{58,10},{51,3},{59,11},{52,4},{... | collective-permute-start | bytes 196616 | tf_op jit(solution)/shard_map/ppermute | solution.py:267
  87.0 11.1 %collective-permute-start.19 = (f32[128,128]{1,0:T(8,128)S(1)}, f32[128,128]{1,0:T(8,128)S(1)}, u32[]{:S(2)}, u32[]{:S(2)}) collective-permute-start(f32[128,128]{1,0:T(8,128)S(1)} %get-tuple-element.45.refs_1_), channel_id=1, source_target_pairs={{32,16},{40,24},{33,17},{41,25},{34,18},{42,26},{35,19},{43,27},{3... | collective-permute-start | bytes 196616 | tf_op jit(solution)/shard_map/ppermute | solution.py:267
  91.5 30.6 %collective-permute-start.36 = (bf16[1536,128]{1,0:T(8,128)(2,1)S(1)}, bf16[1536,128]{1,0:T(8,128)(2,1)S(1)}, u32[]{:S(2)}, u32[]{:S(2)}) collective-permute-start(bf16[1536,128]{1,0:T(8,128)(2,1)S(1)} %slice.12), channel_id=1, source_target_pairs={{0,2},{1,3},{2,0},{3,1},{4,6},{5,7},{6,4},{7,5},{8,10},{9,11},{10,... | collective-permute-start | bytes 1179656 | tf_op jit(solution)/shard_map/ppermute | solution.py:264
  96.9 6.5 %collective-permute-start.23 = (f32[128,128]{1,0:T(8,128)S(1)}, f32[128,128]{1,0:T(8,128)S(1)}, u32[]{:S(2)}, u32[]{:S(2)}) collective-permute-start(f32[128,128]{1,0:T(8,128)S(1)} %get-tuple-element.45.refs_1_), channel_id=1, source_target_pairs={{32,0},{40,8},{33,1},{41,9},{34,2},{42,10},{35,3},{43,11},{36,4},{... | collective-permute-start | bytes 196616 | tf_op jit(solution)/shard_map/ppermute | solution.py:267
  98.6 6.2 %collective-permute-start.22 = (f32[128,128]{1,0:T(8,128)S(1)}, f32[128,128]{1,0:T(8,128)S(1)}, u32[]{:S(2)}, u32[]{:S(2)}) collective-permute-start(f32[128,128]{1,0:T(8,128)S(1)} %get-tuple-element.47.refs_1_), channel_id=1, source_target_pairs={{16,0},{24,8},{17,1},{25,9},{18,2},{26,10},{19,3},{27,11},{20,4},{... | collective-permute-start | bytes 196616 | tf_op jit(solution)/shard_map/ppermute | solution.py:267
  103.4 24.3 %collective-permute-start.37 = (bf16[1536,128]{1,0:T(8,128)(2,1)S(1)}, bf16[1536,128]{1,0:T(8,128)(2,1)S(1)}, u32[]{:S(2)}, u32[]{:S(2)}) collective-permute-start(bf16[1536,128]{1,0:T(8,128)(2,1)S(1)} %slice.13), channel_id=1, source_target_pairs={{0,6},{1,7},{2,4},{3,5},{4,2},{5,3},{6,0},{7,1},{8,14},{9,15},{10,... | collective-permute-start | bytes 1179656 | tf_op jit(solution)/shard_map/ppermute | solution.py:264
  106.4 3.9 %collective-permute-start.24 = (bf16[128,128]{1,0:T(8,128)(2,1)S(1)}, bf16[128,128]{1,0:T(8,128)(2,1)S(1)}, u32[]{:S(2)}, u32[]{:S(2)}) collective-permute-start(bf16[128,128]{1,0:T(8,128)(2,1)S(1)} %get-tuple-element.48.a), channel_id=1, source_target_pairs={{0,32},{8,40},{16,48},{24,56},{32,0},{40,8},{48,16},{56,24},{64,96... | collective-permute-start | bytes 98312 | tf_op jit(solution)/shard_map/ppermute | solution.py:267
  106.4 22.5 %collective-permute-start.38 = (bf16[1536,128]{1,0:T(8,128)(2,1)S(1)}, bf16[1536,128]{1,0:T(8,128)(2,1)S(1)}, u32[]{:S(2)}, u32[]{:S(2)}) collective-permute-start(bf16[1536,128]{1,0:T(8,128)(2,1)S(1)} %slice.14), channel_id=1, source_target_pairs={{0,2},{1,3},{2,0},{3,1},{4,6},{5,7},{6,4},{7,5},{8,10},{9,11},{10,... | collective-permute-start | bytes 1179656 | tf_op jit(solution)/shard_map/ppermute | solution.py:264
  107.0 22.0 %collective-permute-start.39 = (bf16[1536,128]{1,0:T(8,128)(2,1)S(1)}, bf16[1536,128]{1,0:T(8,128)(2,1)S(1)}, u32[]{:S(2)}, u32[]{:S(2)}) collective-permute-start(bf16[1536,128]{1,0:T(8,128)(2,1)S(1)} %slice.15), channel_id=1, source_target_pairs={{0,6},{1,7},{2,4},{3,5},{4,2},{5,3},{6,0},{7,1},{8,14},{9,15},{10,... | collective-permute-start | bytes 1179656 | tf_op jit(solution)/shard_map/ppermute | solution.py:264
  110.3 5.4 %collective-permute-start.25 = (bf16[128,128]{1,0:T(8,128)(2,1)S(1)}, bf16[128,128]{1,0:T(8,128)(2,1)S(1)}, u32[]{:S(2)}, u32[]{:S(2)}) collective-permute-start(bf16[128,128]{1,0:T(8,128)(2,1)S(1)} %get-tuple-element.48.a), channel_id=1, source_target_pairs={{0,64},{8,72},{16,80},{24,88},{32,96},{40,104},{48,112},{56,120},{... | collective-permute-start | bytes 98312 | tf_op jit(solution)/shard_map/ppermute | solution.py:267
  115.7 5.1 %collective-permute-start.26 = (bf16[128,128]{1,0:T(8,128)(2,1)S(1)}, bf16[128,128]{1,0:T(8,128)(2,1)S(1)}, u32[]{:S(2)}, u32[]{:S(2)}) collective-permute-start(bf16[128,128]{1,0:T(8,128)(2,1)S(1)} %get-tuple-element.48.a), channel_id=1, source_target_pairs={{0,96},{8,104},{16,112},{24,120},{32,64},{40,72},{48,80},{56,88},{... | collective-permute-start | bytes 98312 | tf_op jit(solution)/shard_map/ppermute | solution.py:267
  120.8 1.2 collective-permute-start.30
  122.0 5.6 %collective-permute-start.28 = (bf16[4,128,128]{2,1,0:T(8,128)(2,1)S(1)}, bf16[4,128,128]{2,1,0:T(8,128)(2,1)S(1)}, u32[]{:S(2)}, u32[]{:S(2)}) collective-permute-start(bf16[4,128,128]{2,1,0:T(8,128)(2,1)S(1)} %stack4.1.same), channel_id=1, source_target_pairs={{0,16},{8,24},{16,0},{24,8},{32,48},{40,56},{48,32},{56,40},{64,80... | collective-permute-start | bytes 393224 | tf_op jit(solution)/shard_map/ppermute | solution.py:267
  122.1 5.6 %collective-permute-start.27 = (bf16[4,128,128]{2,1,0:T(8,128)(2,1)S(1)}, bf16[4,128,128]{2,1,0:T(8,128)(2,1)S(1)}, u32[]{:S(2)}, u32[]{:S(2)}) collective-permute-start(bf16[4,128,128]{2,1,0:T(8,128)(2,1)S(1)} %stack4.1.same), channel_id=1, source_target_pairs={{0,8},{8,0},{16,24},{24,16},{32,40},{40,32},{48,56},{56,48},{64,72... | collective-permute-start | bytes 393224 | tf_op jit(solution)/shard_map/ppermute | solution.py:267
  127.6 1.3 %collective-permute-start.29 = (bf16[4,128,128]{2,1,0:T(8,128)(2,1)S(1)}, bf16[4,128,128]{2,1,0:T(8,128)(2,1)S(1)}, u32[]{:S(2)}, u32[]{:S(2)}) collective-permute-start(bf16[4,128,128]{2,1,0:T(8,128)(2,1)S(1)} %collective-permute-done.28.cross), channel_id=1, source_target_pairs={{0,8},{8,0},{16,24},{24,16},{32,40},{40,32},{48,56},{56,48},{64,72... | collective-permute-start | bytes 393224 | tf_op jit(solution)/shard_map/ppermute | solution.py:267

commit v4 on v3

--- a/solution.py
+++ b/solution.py
@@ -39,7 +39,7 @@
     return pl.ds(pl.multiple_of(core * LANES, LANES), LANES)
 
 
-def setup_kernel(candidates_from, selected_from, t0, t1, t2, t3, inv, inv_from, inv_mine, inv_other, send, rhs_mine, coupling, selected, sem):
+def setup_kernel(candidates_from, selected_from, inv, inv_from, inv_mine, inv_other, rhs_mine, rhs_send, coupling, selected, sem):
     core = lax.rem(lax.axis_index("row"), 2)
     copies = [
         pltpu.make_async_copy(candidates_from, coupling, sem.at[0]),
@@ -49,9 +49,6 @@
     ]
     for copy in copies:
         copy.start()
-    for index, tile in enumerate((t0, t1, t2, t3)):
-        for half in range(2):
-            send[pl.ds((2 * index + half) * NB, NB), :] = tile[half]
     copies[0].wait()
     copies[1].wait()
     candidates, columns = coupling.shape[1], selected.shape[1]
@@ -69,17 +66,18 @@
     rhs = -(total[:NB] + total[NB : 2 * NB] + total[2 * NB :])
     left, right = rhs[:, :LANES], rhs[:, LANES:]
     rhs_mine[...] = jnp.where(core == 0, left, right)
-    send[pl.ds(CHIPS * NB, NB), :] = jnp.where(core == 0, right, left)
+    rhs_send[...] = jnp.where(core == 0, right, left)
     copies[2].wait()
     copies[3].wait()
 
 
-def setup(coupling, selected, parts, inverses, inv_from):
+def setup(coupling, selected, inverses, inv_from):
     half = pltpu.VMEM((NB, NB, LANES), F32)
+    side = pltpu.VMEM((NB, LANES), F32)
     return pl.pallas_call(
         setup_kernel,
-        out_shape=(half, half, pltpu.VMEM(((CHIPS + 1) * NB, LANES), F32), pltpu.VMEM((NB, LANES), F32)),
-        in_specs=[HBM] * 2 + [VMEM] * 4 + [HBM] * 2,
+        out_shape=(half, half, side, side),
+        in_specs=[HBM] * 4,
         out_specs=(VMEM,) * 4,
         scratch_shapes=[
             pltpu.VMEM(coupling.shape, F32),
@@ -87,8 +85,27 @@
             pltpu.SemaphoreType.DMA((4,)),
         ],
         compiler_params=pltpu.CompilerParams(vmem_limit_bytes=16 << 20),
+        cost_estimate=pl.CostEstimate(flops=100_000_000, bytes_accessed=5_000_000, transcendentals=0),
         name="setup",
-    )(hbm(coupling), hbm(selected[None, :]), *parts, hbm(inverses), inv_from)
+    )(hbm(coupling), hbm(selected[None, :]), hbm(inverses), inv_from)
+
+
+def join_kernel(t0, t1, t2, t3, rhs_send, send):
+    for index, tile in enumerate((t0, t1, t2, t3)):
+        for half in range(2):
+            send[pl.ds((2 * index + half) * NB, NB), :] = tile[half]
+    send[pl.ds(CHIPS * NB, NB), :] = rhs_send[...]
+
+
+def join(parts, rhs_send):
+    return pl.pallas_call(
+        join_kernel,
+        out_shape=pltpu.VMEM(((CHIPS + 1) * NB, LANES), F32),
+        in_specs=[VMEM] * 5,
+        out_specs=VMEM,
+        compiler_params=pltpu.CompilerParams(vmem_limit_bytes=8 << 20),
+        name="join",
+    )(*parts, rhs_send)
 
 
 def hbm(value):
@@ -277,7 +294,8 @@
     v[2], v[6] = col_flip(schur_basis, 2), col_flip(schur_basis, 6)
     split = schur_basis.shape[0] // 2
 
-    inv_mine, inv_other, sent, rhs_mine = setup(coupling, selected, parts, inverses, inv_from)
+    inv_mine, inv_other, rhs_mine, rhs_send = setup(coupling, selected, inverses, inv_from)
+    sent = join(parts, rhs_send)
     swapped = row_flip(sent, 1)
     kept = {"inv_mine": inv_mine, "inv_other": inv_other}
     state = solve_step(0, {"rhs_mine": rhs_mine, "sent": sent, "swapped": swapped, **kept})

time: 134 us -> 133 us (level)
  waiting for transfers between devices: 87.6 us -> 85.8 us
    ppermute x13, waiting for transfers between devices: 24.2 us -> 22.4 us  [col_flip(): return lax.ppermute(value, 'col', flip(CHIPS, mask))]
where the time goes in v4:
time: 133 us; the launch traced here: 131 us
  waiting for transfers between devices  85.8 us (65%)
  starting transfers between devices  34.3 us (26%)
  Pallas kernels  8.98 us (7%)
    ppermute x27, waiting for transfers between devices, row_move(): return lax.ppermute(value, 'row', pairs)  63.4 us
    ppermute x13, waiting for transfers between devices, col_flip(): return lax.ppermute(value, 'col', flip(CHIPS, mask))  22.4 us
    ppermute x13, starting transfers between devices, col_flip(): return lax.ppermute(value, 'col', flip(CHIPS, mask))  17.6 us
    ppermute x27, starting transfers between devices, row_move(): return lax.ppermute(value, 'row', pairs)  16.8 us
    pallas_call x1, Pallas kernels, back_transform(): pl.pallas_call(product_kernel, grid=(rows // BLOCK,), out_shape=(jax.Shap...  4.07 us
    pallas_call x8, Pallas kernels, solve_step(): result = call(*operands.values())  3.06 us
  transfers between devices with their start and end apart: 40, of which 17 were waited for; matrix products, arithmetic and copies ran while one was open for 1% of the time, Pallas kernels for 4%

profile of v4, /device:TPU:0, one launch (start us, length us, event | category | flops | bytes accessed | tf_op | source)
XLA Modules:
  0.0 131.2 jit_solution(13812324935018844242)
XLA Ops:
  0.6 0.1 collective-permute-start
  0.7 3.2 %collective-permute-start.31 = (bf16[3072,128]{1,0:T(8,128)(2,1)}, bf16[3072,128]{1,0:T(8,128)(2,1)S(1)}, u32[]{:S(2)}, u32[]{:S(2)}) collective-permute-start(bf16[3072,128]{1,0:T(8,128)(2,1)} %v0.1), channel_id=1, source_target_pairs={{0,1},{1,0},{2,3},{3,2},{4,5},{5,4},{6,7},{7,6},{8,9},{9,8},{10,11... | collective-permute-start | bytes 2359304 | tf_op jit(solution)/shard_map/ppermute | solution.py:281
  3.9 0.4 collective-permute-start.1
  4.3 18.7 %collective-permute-done.1 = f32[64,128]{1,0:T(8,128)S(1)} collective-permute-done((f32[64,128]{1,0:T(8,128)}, f32[64,128]{1,0:T(8,128)S(1)}, u32[]{:S(2)}, u32[]{:S(2)}) %collective-permute-start.1) | collective-permute-done | bytes 32800 | tf_op jit(solution)/shard_map/ppermute | solution.py:281
  23.1 0.8 pad_maximum_fusion.t0
  23.8 2.0 %collective-permute-start.2 = (f32[2,64,128]{2,1,0:T(8,128)S(1)}, f32[2,64,128]{2,1,0:T(8,128)S(1)}, u32[]{:S(2)}, u32[]{:S(2)}) collective-permute-start(f32[2,64,128]{2,1,0:T(8,128)S(1)} %pad_maximum_fusion.t0), channel_id=1, source_target_pairs={{0,2},{1,3},{2,0},{3,1},{4,6},{5,7},{6,4},{7,5},{8,10},{9,11},{10,... | collective-permute-start | bytes 196616 | tf_op jit(solution)/shard_map/ppermute | solution.py:281
  25.9 3.6 %collective-permute-start.3 = (f32[2,64,128]{2,1,0:T(8,128)S(1)}, f32[2,64,128]{2,1,0:T(8,128)S(1)}, u32[]{:S(2)}, u32[]{:S(2)}) collective-permute-start(f32[2,64,128]{2,1,0:T(8,128)S(1)} %pad_maximum_fusion.t0), channel_id=1, source_target_pairs={{0,4},{1,5},{2,6},{3,7},{4,0},{5,1},{6,2},{7,3},{8,12},{9,13},{10,... | collective-permute-start | bytes 196616 | tf_op jit(solution)/shard_map/ppermute | solution.py:281
  29.5 0.0 collective-permute-start.4
  29.5 0.0 collective-permute-done.inv_from
  29.5 1.8 %setup.1 = (f32[64,64,128]{2,1,0:T(8,128)S(1)}, f32[64,64,128]{2,1,0:T(8,128)S(1)}, f32[64,128]{1,0:T(8,128)S(1)}, f32[64,128]{1,0:T(8,128)S(1)}) custom-call(f32[64,2048]{1,0:T(8,128)} %candidates_from.1, s32[1,256]{1,0:T(1,128)} %bitcast.5, f32[64,64,256]{2,1,0:T(8,128)} %inv.1, f32[64,64,256]{2,1,0:T(8,128)S(1)} %collective-permute-done.inv_from), custom_call_target="tpu_custom_call" | custom-call | flops 100000000 | bytes 5000000 | tf_op jit(solution)/shard_map/setup/pallas_call | solution.py:77
  31.3 0.0 collective-permute-done.2.t1
  31.3 1.1 collective-permute-done.3.t2
  32.4 2.5 %collective-permute-done.4.t3 = f32[2,64,128]{2,1,0:T(8,128)S(1)} collective-permute-done((f32[2,64,128]{2,1,0:T(8,128)S(1)}, f32[2,64,128]{2,1,0:T(8,128)S(1)}, u32[]{:S(2)}, u32[]{:S(2)}) %collective-permute-start.4) | collective-permute-done | bytes 65568 | tf_op jit(solution)/shard_map/ppermute | solution.py:281
  35.0 0.1 collective-permute-start.5
  35.1 1.6 %collective-permute-done.5.refs_2_ = f32[576,128]{1,0:T(8,128)S(1)} collective-permute-done((f32[576,128]{1,0:T(8,128)S(1)}, f32[576,128]{1,0:T(8,128)S(1)}, u32[]{:S(2)}, u32[]{:S(2)}) %collective-permute-start.5) | collective-permute-done | bytes 294944 | tf_op jit(solution)/shard_map/ppermute | solution.py:284
  36.6 0.1 solve_step.8
  36.7 0.8 collective-permute-start.6
  37.5 0.3 copy-done
  37.8 0.9 collective-permute-start.33
  38.6 0.7 collective-permute-start.8
  39.3 0.0 collective-permute-done.6.refs_2_
  39.3 0.7 collective-permute-start.9
  40.0 0.7 collective-permute-start.7
  40.7 0.7 collective-permute-start.11
  41.4 0.0 collective-permute-done.31.v1
  41.4 1.2 collective-permute-start.34
  42.7 2.6 %collective-permute-start.35 = (bf16[3072,128]{1,0:T(8,128)(2,1)S(1)}, bf16[3072,128]{1,0:T(8,128)(2,1)S(1)}, u32[]{:S(2)}, u32[]{:S(2)}) collective-permute-start(bf16[3072,128]{1,0:T(8,128)(2,1)S(1)} %collective-permute-done.31.v1), channel_id=1, source_target_pairs={{0,6},{1,7},{2,4},{3,5},{4,2},{5,3},{6,0},{7,1},{8,14},{9,15},{10,... | collective-permute-start | bytes 2359304 | tf_op jit(solution)/shard_map/ppermute | solution.py:281
  45.3 0.0 collective-permute-done.11.refs_3_
  45.3 0.7 collective-permute-start.12
  46.0 0.7 collective-permute-start.10
  46.7 0.7 collective-permute-start.14
  47.3 1.3 collective-permute-start.15
  48.7 15.7 %collective-permute-done.15.refs_4_ = f32[128,128]{1,0:T(8,128)S(1)} collective-permute-done((f32[128,128]{1,0:T(8,128)S(1)}, f32[128,128]{1,0:T(8,128)S(1)}, u32[]{:S(2)}, u32[]{:S(2)}) %collective-permute-start.15) | collective-permute-done | bytes 65568 | tf_op jit(solution)/shard_map/ppermute | solution.py:284
  64.4 0.7 collective-permute-start.13
  65.1 1.3 collective-permute-start.17
  66.4 6.4 %collective-permute-done.17.refs_3_ = f32[128,128]{1,0:T(8,128)S(1)} collective-permute-done((f32[128,128]{1,0:T(8,128)S(1)}, f32[128,128]{1,0:T(8,128)S(1)}, u32[]{:S(2)}, u32[]{:S(2)}) %collective-permute-start.17) | collective-permute-done | bytes 65568 | tf_op jit(solution)/shard_map/ppermute | solution.py:284
  72.8 1.3 collective-permute-start.18
  74.0 0.2 solve_step.12
  74.3 7.0 %collective-permute-done.18.refs_4_ = f32[128,128]{1,0:T(8,128)S(1)} collective-permute-done((f32[128,128]{1,0:T(8,128)S(1)}, f32[128,128]{1,0:T(8,128)S(1)}, u32[]{:S(2)}, u32[]{:S(2)}) %collective-permute-start.18) | collective-permute-done | bytes 65568 | tf_op jit(solution)/shard_map/ppermute | solution.py:284
  81.3 0.7 collective-permute-start.16
  82.0 1.3 collective-permute-start.20
  83.3 0.6 solve_step.13
  83.9 1.3 collective-permute-start.21
  85.2 0.7 collective-permute-start.19
  85.9 3.7 %collective-permute-done.20.refs_3_ = f32[128,128]{1,0:T(8,128)S(1)} collective-permute-done((f32[128,128]{1,0:T(8,128)S(1)}, f32[128,128]{1,0:T(8,128)S(1)}, u32[]{:S(2)}, u32[]{:S(2)}) %collective-permute-start.20) | collective-permute-done | bytes 65568 | tf_op jit(solution)/shard_map/ppermute | solution.py:284
  89.6 0.1 collective-permute-start.36
  89.7 5.3 %collective-permute-done.21.refs_4_ = f32[128,128]{1,0:T(8,128)S(1)} collective-permute-done((f32[128,128]{1,0:T(8,128)S(1)}, f32[128,128]{1,0:T(8,128)S(1)}, u32[]{:S(2)}, u32[]{:S(2)}) %collective-permute-start.21) | collective-permute-done | bytes 65568 | tf_op jit(solution)/shard_map/ppermute | solution.py:284
  95.1 1.3 collective-permute-start.23
  96.4 0.4 solve_step.14
  96.8 1.3 collective-permute-start.22
  98.1 3.4 %collective-permute-done.23.refs_3_ = f32[128,128]{1,0:T(8,128)S(1)} collective-permute-done((f32[128,128]{1,0:T(8,128)S(1)}, f32[128,128]{1,0:T(8,128)S(1)}, u32[]{:S(2)}, u32[]{:S(2)}) %collective-permute-start.23) | collective-permute-done | bytes 65568 | tf_op jit(solution)/shard_map/ppermute | solution.py:284
  101.6 0.9 collective-permute-start.37
  102.5 0.5 collective-permute-done.22.refs_2_
  103.0 1.6 %solve_step.15 = (f32[128,128]{1,0:T(8,128)}, f32[128,128]{1,0:T(8,128)}, bf16[128,128]{1,0:T(8,128)(2,1)S(1)}, f32[64,128]{1,0:T(8,128)S(1)}, f32[64,128]{1,0:T(8,128)S(1)}) custom-call(f32[128,128]{1,0:T(8,128)S(1)} %get-tuple-element.46.refs_0_, f32[128,128]{1,0:T(8,128)S(1)} %get-tuple-element.47.refs_1_, ...), custom_call_target="tpu_custom_call" | custom-call | flops 8000000 | bytes 5000000 | tf_op jit(solution)/shard_map/solve_step/pallas_call | solution.py:209
  104.6 0.5 collective-permute-start.38
  105.2 2.1 %collective-permute-start.39 = (bf16[1536,128]{1,0:T(8,128)(2,1)S(1)}, bf16[1536,128]{1,0:T(8,128)(2,1)S(1)}, u32[]{:S(2)}, u32[]{:S(2)}) collective-permute-start(bf16[1536,128]{1,0:T(8,128)(2,1)S(1)} %slice.15), channel_id=1, source_target_pairs={{0,6},{1,7},{2,4},{3,5},{4,2},{5,3},{6,0},{7,1},{8,14},{9,15},{10,... | collective-permute-start | bytes 1179656 | tf_op jit(solution)/shard_map/ppermute | solution.py:281
  107.3 1.2 collective-permute-done.24.b
  108.5 5.4 %collective-permute-done.25.c = bf16[128,128]{1,0:T(8,128)(2,1)S(1)} collective-permute-done((bf16[128,128]{1,0:T(8,128)(2,1)S(1)}, bf16[128,128]{1,0:T(8,128)(2,1)S(1)}, u32[]{:S(2)}, u32[]{:S(2)}) %collective-permute-start.25) | collective-permute-done | bytes 32800 | tf_op jit(solution)/shard_map/ppermute | solution.py:284
  113.9 5.1 %collective-permute-done.26.d = bf16[128,128]{1,0:T(8,128)(2,1)S(1)} collective-permute-done((bf16[128,128]{1,0:T(8,128)(2,1)S(1)}, bf16[128,128]{1,0:T(8,128)(2,1)S(1)}, u32[]{:S(2)}, u32[]{:S(2)}) %collective-permute-start.26) | collective-permute-done | bytes 32800 | tf_op jit(solution)/shard_map/ppermute | solution.py:284
  119.1 1.2 collective-permute-done.30.theirs
  120.3 0.2 collective-permute-start.27
  120.4 5.4 %collective-permute-done.28.cross = bf16[4,128,128]{2,1,0:T(8,128)(2,1)S(1)} collective-permute-done((bf16[4,128,128]{2,1,0:T(8,128)(2,1)S(1)}, bf16[4,128,128]{2,1,0:T(8,128)(2,1)S(1)}, u32[]{:S(2)}, u32[]{:S(2)}) %collective-permute-start.28) | collective-permute-done | bytes 131104 | tf_op jit(solution)/shard_map/ppermute | solution.py:284
  125.8 1.3 %collective-permute-done.29.cross_swap = bf16[4,128,128]{2,1,0:T(8,128)(2,1)S(1)} collective-permute-done((bf16[4,128,128]{2,1,0:T(8,128)(2,1)S(1)}, bf16[4,128,128]{2,1,0:T(8,128)(2,1)S(1)}, u32[]{:S(2)}, u32[]{:S(2)}) %collective-permute-start.29) | collective-permute-done | bytes 131104 | tf_op jit(solution)/shard_map/ppermute | solution.py:284
  127.2 4.1 %back_transform.1 = (bf16[3072,256]{1,0:T(8,128)(2,1)}, f32[64,256]{1,0:T(8,128)}) custom-call(bf16[4,128,128]{2,1,0:T(8,128)(2,1)S(1)} %stack4.1.same, bf16[4,128,128]{2,1,0:T(8,128)(2,1)S(1)} %collective-permute-done.27.same_swap, bf16[4,128,128]{2,1,0:T(8,128)(2,1)S(1)} %collective-permute-done.28.cross, ...), custom_call_target="tpu_custom_call" | custom-call | flops 1610612736 | bytes 8000000 | tf_op jit(solution)/shard_map/back_transform/pallas_call | solution.py:263
  (35 shorter events, 0.3 us)
Async XLA Ops:
  0.6 28.8 %collective-permute-start = (f32[64,64,256]{2,1,0:T(8,128)}, f32[64,64,256]{2,1,0:T(8,128)S(1)}, u32[]{:S(2)}, u32[]{:S(2)}) collective-permute-start(f32[64,64,256]{2,1,0:T(8,128)} %inv.1), channel_id=1, source_target_pairs={{0,8},{8,0},{16,24},{24,16},{32,40},{40,32},{48,56},{56,48},{64,72... | collective-permute-start | bytes 12582920 | tf_op jit(solution)/shard_map/ppermute | solution.py:284
  0.7 40.7 %collective-permute-start.31 = (bf16[3072,128]{1,0:T(8,128)(2,1)}, bf16[3072,128]{1,0:T(8,128)(2,1)S(1)}, u32[]{:S(2)}, u32[]{:S(2)}) collective-permute-start(bf16[3072,128]{1,0:T(8,128)(2,1)} %v0.1), channel_id=1, source_target_pairs={{0,1},{1,0},{2,3},{3,2},{4,5},{5,4},{6,7},{7,6},{8,9},{9,8},{10,11... | collective-permute-start | bytes 2359304 | tf_op jit(solution)/shard_map/ppermute | solution.py:281
  3.9 19.1 %collective-permute-start.1 = (f32[64,128]{1,0:T(8,128)}, f32[64,128]{1,0:T(8,128)S(1)}, u32[]{:S(2)}, u32[]{:S(2)}) collective-permute-start(f32[64,128]{1,0:T(8,128)} %param.5), channel_id=1, source_target_pairs={{0,1},{1,0},{2,3},{3,2},{4,5},{5,4},{6,7},{7,6},{8,9},{9,8},{10,11... | collective-permute-start | bytes 98312 | tf_op jit(solution)/shard_map/ppermute | solution.py:281
  23.8 7.5 %collective-permute-start.2 = (f32[2,64,128]{2,1,0:T(8,128)S(1)}, f32[2,64,128]{2,1,0:T(8,128)S(1)}, u32[]{:S(2)}, u32[]{:S(2)}) collective-permute-start(f32[2,64,128]{2,1,0:T(8,128)S(1)} %pad_maximum_fusion.t0), channel_id=1, source_target_pairs={{0,2},{1,3},{2,0},{3,1},{4,6},{5,7},{6,4},{7,5},{8,10},{9,11},{10,... | collective-permute-start | bytes 196616 | tf_op jit(solution)/shard_map/ppermute | solution.py:281
  25.9 6.5 %collective-permute-start.3 = (f32[2,64,128]{2,1,0:T(8,128)S(1)}, f32[2,64,128]{2,1,0:T(8,128)S(1)}, u32[]{:S(2)}, u32[]{:S(2)}) collective-permute-start(f32[2,64,128]{2,1,0:T(8,128)S(1)} %pad_maximum_fusion.t0), channel_id=1, source_target_pairs={{0,4},{1,5},{2,6},{3,7},{4,0},{5,1},{6,2},{7,3},{8,12},{9,13},{10,... | collective-permute-start | bytes 196616 | tf_op jit(solution)/shard_map/ppermute | solution.py:281
  29.5 5.5 %collective-permute-start.4 = (f32[2,64,128]{2,1,0:T(8,128)S(1)}, f32[2,64,128]{2,1,0:T(8,128)S(1)}, u32[]{:S(2)}, u32[]{:S(2)}) collective-permute-start(f32[2,64,128]{2,1,0:T(8,128)S(1)} %pad_maximum_fusion.t0), channel_id=1, source_target_pairs={{0,6},{1,7},{2,4},{3,5},{4,2},{5,3},{6,0},{7,1},{8,14},{9,15},{10,... | collective-permute-start | bytes 196616 | tf_op jit(solution)/shard_map/ppermute | solution.py:281
  35.0 1.7 %collective-permute-start.5 = (f32[576,128]{1,0:T(8,128)S(1)}, f32[576,128]{1,0:T(8,128)S(1)}, u32[]{:S(2)}, u32[]{:S(2)}) collective-permute-start(f32[576,128]{1,0:T(8,128)S(1)} %join.1.refs_1_), channel_id=1, source_target_pairs={{0,8},{8,0},{16,24},{24,16},{32,40},{40,32},{48,56},{56,48},{64,72... | collective-permute-start | bytes 884744 | tf_op jit(solution)/shard_map/ppermute | solution.py:284
  36.6 1.1 copy-start
  36.7 2.6 %collective-permute-start.6 = (f32[128,128]{1,0:T(8,128)S(1)}, f32[128,128]{1,0:T(8,128)S(1)}, u32[]{:S(2)}, u32[]{:S(2)}) collective-permute-start(f32[128,128]{1,0:T(8,128)S(1)} %get-tuple-element.34.refs_1_), channel_id=1, source_target_pairs={{112,96},{120,104},{113,97},{121,105},{114,98},{122,106},{115,99},... | collective-permute-start | bytes 196616 | tf_op jit(solution)/shard_map/ppermute | solution.py:284
  37.8 46.1 %collective-permute-start.32 = (bf16[3072,128]{1,0:T(8,128)(2,1)S(1)}, bf16[3072,128]{1,0:T(8,128)(2,1)S(1)}, u32[]{:S(2)}, u32[]{:S(2)}) collective-permute-start(bf16[3072,128]{1,0:T(8,128)(2,1)S(1)} %copy-done), channel_id=1, source_target_pairs={{0,2},{1,3},{2,0},{3,1},{4,6},{5,7},{6,4},{7,5},{8,10},{9,11},{10,... | collective-permute-start | bytes 2359304 | tf_op jit(solution)/shard_map/ppermute | solution.py:281
  37.8 47.5 %collective-permute-start.33 = (bf16[3072,128]{1,0:T(8,128)(2,1)S(1)}, bf16[3072,128]{1,0:T(8,128)(2,1)S(1)}, u32[]{:S(2)}, u32[]{:S(2)}) collective-permute-start(bf16[3072,128]{1,0:T(8,128)(2,1)S(1)} %copy-done), channel_id=1, source_target_pairs={{0,6},{1,7},{2,4},{3,5},{4,2},{5,3},{6,0},{7,1},{8,14},{9,15},{10,... | collective-permute-start | bytes 2359304 | tf_op jit(solution)/shard_map/ppermute | solution.py:281
  38.6 1.4 %collective-permute-start.8 = (f32[128,128]{1,0:T(8,128)S(1)}, f32[128,128]{1,0:T(8,128)S(1)}, u32[]{:S(2)}, u32[]{:S(2)}) collective-permute-start(f32[128,128]{1,0:T(8,128)S(1)} %get-tuple-element.34.refs_1_), channel_id=1, source_target_pairs={{112,80},{120,88},{113,81},{121,89},{114,82},{122,90},{115,83},{12... | collective-permute-start | bytes 196616 | tf_op jit(solution)/shard_map/ppermute | solution.py:284
  39.3 1.4 %collective-permute-start.9 = (f32[128,128]{1,0:T(8,128)S(1)}, f32[128,128]{1,0:T(8,128)S(1)}, u32[]{:S(2)}, u32[]{:S(2)}) collective-permute-start(f32[128,128]{1,0:T(8,128)S(1)} %get-tuple-element.34.refs_1_), channel_id=1, source_target_pairs={{112,64},{120,72},{113,65},{121,73},{114,66},{122,74},{115,67},{12... | collective-permute-start | bytes 196616 | tf_op jit(solution)/shard_map/ppermute | solution.py:284
  40.0 1.4 %collective-permute-start.7 = (f32[128,128]{1,0:T(8,128)S(1)}, f32[128,128]{1,0:T(8,128)S(1)}, u32[]{:S(2)}, u32[]{:S(2)}) collective-permute-start(f32[128,128]{1,0:T(8,128)S(1)} %get-tuple-element.37.refs_1_), channel_id=1, source_target_pairs={{96,80},{104,88},{97,81},{105,89},{98,82},{106,90},{99,83},{107,91... | collective-permute-start | bytes 196616 | tf_op jit(solution)/shard_map/ppermute | solution.py:284
  40.7 4.6 %collective-permute-start.11 = (f32[128,128]{1,0:T(8,128)S(1)}, f32[128,128]{1,0:T(8,128)S(1)}, u32[]{:S(2)}, u32[]{:S(2)}) collective-permute-start(f32[128,128]{1,0:T(8,128)S(1)} %get-tuple-element.37.refs_1_), channel_id=1, source_target_pairs={{96,64},{104,72},{112,48},{120,56},{97,65},{105,73},{113,49},{121,... | collective-permute-start | bytes 196616 | tf_op jit(solution)/shard_map/ppermute | solution.py:284
  41.4 63.2 %collective-permute-start.34 = (bf16[3072,128]{1,0:T(8,128)(2,1)S(1)}, bf16[3072,128]{1,0:T(8,128)(2,1)S(1)}, u32[]{:S(2)}, u32[]{:S(2)}) collective-permute-start(bf16[3072,128]{1,0:T(8,128)(2,1)S(1)} %collective-permute-done.31.v1), channel_id=1, source_target_pairs={{0,2},{1,3},{2,0},{3,1},{4,6},{5,7},{6,4},{7,5},{8,10},{9,11},{10,... | collective-permute-start | bytes 2359304 | tf_op jit(solution)/shard_map/ppermute | solution.py:281
  42.7 61.9 %collective-permute-start.35 = (bf16[3072,128]{1,0:T(8,128)(2,1)S(1)}, bf16[3072,128]{1,0:T(8,128)(2,1)S(1)}, u32[]{:S(2)}, u32[]{:S(2)}) collective-permute-start(bf16[3072,128]{1,0:T(8,128)(2,1)S(1)} %collective-permute-done.31.v1), channel_id=1, source_target_pairs={{0,6},{1,7},{2,4},{3,5},{4,2},{5,3},{6,0},{7,1},{8,14},{9,15},{10,... | collective-permute-start | bytes 2359304 | tf_op jit(solution)/shard_map/ppermute | solution.py:281
  45.3 0.7 collective-permute-start.12
  46.0 0.7 collective-permute-start.10
  46.7 0.7 collective-permute-start.14
  47.3 17.1 %collective-permute-start.15 = (f32[128,128]{1,0:T(8,128)S(1)}, f32[128,128]{1,0:T(8,128)S(1)}, u32[]{:S(2)}, u32[]{:S(2)}) collective-permute-start(f32[128,128]{1,0:T(8,128)S(1)} %get-tuple-element.39.refs_1_), channel_id=1, source_target_pairs={{80,32},{88,40},{96,16},{104,24},{112,0},{120,8},{81,33},{89,41},{... | collective-permute-start | bytes 196616 | tf_op jit(solution)/shard_map/ppermute | solution.py:284
  64.4 0.7 collective-permute-start.13
  65.1 7.7 %collective-permute-start.17 = (f32[128,128]{1,0:T(8,128)S(1)}, f32[128,128]{1,0:T(8,128)S(1)}, u32[]{:S(2)}, u32[]{:S(2)}) collective-permute-start(f32[128,128]{1,0:T(8,128)S(1)} %get-tuple-element.41.refs_1_), channel_id=1, source_target_pairs={{64,32},{72,40},{80,16},{88,24},{96,0},{104,8},{65,33},{73,41},{81... | collective-permute-start | bytes 196616 | tf_op jit(solution)/shard_map/ppermute | solution.py:284
  72.8 8.6 %collective-permute-start.18 = (f32[128,128]{1,0:T(8,128)S(1)}, f32[128,128]{1,0:T(8,128)S(1)}, u32[]{:S(2)}, u32[]{:S(2)}) collective-permute-start(f32[128,128]{1,0:T(8,128)S(1)} %get-tuple-element.41.refs_1_), channel_id=1, source_target_pairs={{64,16},{72,24},{80,0},{88,8},{65,17},{73,25},{81,1},{89,9},{66,18... | collective-permute-start | bytes 196616 | tf_op jit(solution)/shard_map/ppermute | solution.py:284
  81.3 0.7 collective-permute-start.16
  82.0 7.7 %collective-permute-start.20 = (f32[128,128]{1,0:T(8,128)S(1)}, f32[128,128]{1,0:T(8,128)S(1)}, u32[]{:S(2)}, u32[]{:S(2)}) collective-permute-start(f32[128,128]{1,0:T(8,128)S(1)} %get-tuple-element.43.refs_1_), channel_id=1, source_target_pairs={{48,16},{56,24},{64,0},{72,8},{49,17},{57,25},{65,1},{73,9},{50,18... | collective-permute-start | bytes 196616 | tf_op jit(solution)/shard_map/ppermute | solution.py:284
  83.9 11.1 %collective-permute-start.21 = (f32[128,128]{1,0:T(8,128)S(1)}, f32[128,128]{1,0:T(8,128)S(1)}, u32[]{:S(2)}, u32[]{:S(2)}) collective-permute-start(f32[128,128]{1,0:T(8,128)S(1)} %get-tuple-element.43.refs_1_), channel_id=1, source_target_pairs={{48,0},{56,8},{49,1},{57,9},{50,2},{58,10},{51,3},{59,11},{52,4},{... | collective-permute-start | bytes 196616 | tf_op jit(solution)/shard_map/ppermute | solution.py:284
  85.2 11.1 %collective-permute-start.19 = (f32[128,128]{1,0:T(8,128)S(1)}, f32[128,128]{1,0:T(8,128)S(1)}, u32[]{:S(2)}, u32[]{:S(2)}) collective-permute-start(f32[128,128]{1,0:T(8,128)S(1)} %get-tuple-element.45.refs_1_), channel_id=1, source_target_pairs={{32,16},{40,24},{33,17},{41,25},{34,18},{42,26},{35,19},{43,27},{3... | collective-permute-start | bytes 196616 | tf_op jit(solution)/shard_map/ppermute | solution.py:284
  89.6 30.6 %collective-permute-start.36 = (bf16[1536,128]{1,0:T(8,128)(2,1)S(1)}, bf16[1536,128]{1,0:T(8,128)(2,1)S(1)}, u32[]{:S(2)}, u32[]{:S(2)}) collective-permute-start(bf16[1536,128]{1,0:T(8,128)(2,1)S(1)} %slice.12), channel_id=1, source_target_pairs={{0,2},{1,3},{2,0},{3,1},{4,6},{5,7},{6,4},{7,5},{8,10},{9,11},{10,... | collective-permute-start | bytes 1179656 | tf_op jit(solution)/shard_map/ppermute | solution.py:281
  95.1 6.5 %collective-permute-start.23 = (f32[128,128]{1,0:T(8,128)S(1)}, f32[128,128]{1,0:T(8,128)S(1)}, u32[]{:S(2)}, u32[]{:S(2)}) collective-permute-start(f32[128,128]{1,0:T(8,128)S(1)} %get-tuple-element.45.refs_1_), channel_id=1, source_target_pairs={{32,0},{40,8},{33,1},{41,9},{34,2},{42,10},{35,3},{43,11},{36,4},{... | collective-permute-start | bytes 196616 | tf_op jit(solution)/shard_map/ppermute | solution.py:284
  96.8 6.2 %collective-permute-start.22 = (f32[128,128]{1,0:T(8,128)S(1)}, f32[128,128]{1,0:T(8,128)S(1)}, u32[]{:S(2)}, u32[]{:S(2)}) collective-permute-start(f32[128,128]{1,0:T(8,128)S(1)} %get-tuple-element.47.refs_1_), channel_id=1, source_target_pairs={{16,0},{24,8},{17,1},{25,9},{18,2},{26,10},{19,3},{27,11},{20,4},{... | collective-permute-start | bytes 196616 | tf_op jit(solution)/shard_map/ppermute | solution.py:284
  101.6 24.3 %collective-permute-start.37 = (bf16[1536,128]{1,0:T(8,128)(2,1)S(1)}, bf16[1536,128]{1,0:T(8,128)(2,1)S(1)}, u32[]{:S(2)}, u32[]{:S(2)}) collective-permute-start(bf16[1536,128]{1,0:T(8,128)(2,1)S(1)} %slice.13), channel_id=1, source_target_pairs={{0,6},{1,7},{2,4},{3,5},{4,2},{5,3},{6,0},{7,1},{8,14},{9,15},{10,... | collective-permute-start | bytes 1179656 | tf_op jit(solution)/shard_map/ppermute | solution.py:281
  104.6 3.9 %collective-permute-start.24 = (bf16[128,128]{1,0:T(8,128)(2,1)S(1)}, bf16[128,128]{1,0:T(8,128)(2,1)S(1)}, u32[]{:S(2)}, u32[]{:S(2)}) collective-permute-start(bf16[128,128]{1,0:T(8,128)(2,1)S(1)} %get-tuple-element.48.a), channel_id=1, source_target_pairs={{0,32},{8,40},{16,48},{24,56},{32,0},{40,8},{48,16},{56,24},{64,96... | collective-permute-start | bytes 98312 | tf_op jit(solution)/shard_map/ppermute | solution.py:284
  104.6 22.5 %collective-permute-start.38 = (bf16[1536,128]{1,0:T(8,128)(2,1)S(1)}, bf16[1536,128]{1,0:T(8,128)(2,1)S(1)}, u32[]{:S(2)}, u32[]{:S(2)}) collective-permute-start(bf16[1536,128]{1,0:T(8,128)(2,1)S(1)} %slice.14), channel_id=1, source_target_pairs={{0,2},{1,3},{2,0},{3,1},{4,6},{5,7},{6,4},{7,5},{8,10},{9,11},{10,... | collective-permute-start | bytes 1179656 | tf_op jit(solution)/shard_map/ppermute | solution.py:281
  105.2 22.0 %collective-permute-start.39 = (bf16[1536,128]{1,0:T(8,128)(2,1)S(1)}, bf16[1536,128]{1,0:T(8,128)(2,1)S(1)}, u32[]{:S(2)}, u32[]{:S(2)}) collective-permute-start(bf16[1536,128]{1,0:T(8,128)(2,1)S(1)} %slice.15), channel_id=1, source_target_pairs={{0,6},{1,7},{2,4},{3,5},{4,2},{5,3},{6,0},{7,1},{8,14},{9,15},{10,... | collective-permute-start | bytes 1179656 | tf_op jit(solution)/shard_map/ppermute | solution.py:281
  108.5 5.4 %collective-permute-start.25 = (bf16[128,128]{1,0:T(8,128)(2,1)S(1)}, bf16[128,128]{1,0:T(8,128)(2,1)S(1)}, u32[]{:S(2)}, u32[]{:S(2)}) collective-permute-start(bf16[128,128]{1,0:T(8,128)(2,1)S(1)} %get-tuple-element.48.a), channel_id=1, source_target_pairs={{0,64},{8,72},{16,80},{24,88},{32,96},{40,104},{48,112},{56,120},{... | collective-permute-start | bytes 98312 | tf_op jit(solution)/shard_map/ppermute | solution.py:284
  113.9 5.1 %collective-permute-start.26 = (bf16[128,128]{1,0:T(8,128)(2,1)S(1)}, bf16[128,128]{1,0:T(8,128)(2,1)S(1)}, u32[]{:S(2)}, u32[]{:S(2)}) collective-permute-start(bf16[128,128]{1,0:T(8,128)(2,1)S(1)} %get-tuple-element.48.a), channel_id=1, source_target_pairs={{0,96},{8,104},{16,112},{24,120},{32,64},{40,72},{48,80},{56,88},{... | collective-permute-start | bytes 98312 | tf_op jit(solution)/shard_map/ppermute | solution.py:284
  119.0 1.2 collective-permute-start.30
  120.2 5.6 %collective-permute-start.28 = (bf16[4,128,128]{2,1,0:T(8,128)(2,1)S(1)}, bf16[4,128,128]{2,1,0:T(8,128)(2,1)S(1)}, u32[]{:S(2)}, u32[]{:S(2)}) collective-permute-start(bf16[4,128,128]{2,1,0:T(8,128)(2,1)S(1)} %stack4.1.same), channel_id=1, source_target_pairs={{0,16},{8,24},{16,0},{24,8},{32,48},{40,56},{48,32},{56,40},{64,80... | collective-permute-start | bytes 393224 | tf_op jit(solution)/shard_map/ppermute | solution.py:284
  120.3 5.6 %collective-permute-start.27 = (bf16[4,128,128]{2,1,0:T(8,128)(2,1)S(1)}, bf16[4,128,128]{2,1,0:T(8,128)(2,1)S(1)}, u32[]{:S(2)}, u32[]{:S(2)}) collective-permute-start(bf16[4,128,128]{2,1,0:T(8,128)(2,1)S(1)} %stack4.1.same), channel_id=1, source_target_pairs={{0,8},{8,0},{16,24},{24,16},{32,40},{40,32},{48,56},{56,48},{64,72... | collective-permute-start | bytes 393224 | tf_op jit(solution)/shard_map/ppermute | solution.py:284
  125.8 1.3 %collective-permute-start.29 = (bf16[4,128,128]{2,1,0:T(8,128)(2,1)S(1)}, bf16[4,128,128]{2,1,0:T(8,128)(2,1)S(1)}, u32[]{:S(2)}, u32[]{:S(2)}) collective-permute-start(bf16[4,128,128]{2,1,0:T(8,128)(2,1)S(1)} %collective-permute-done.28.cross), channel_id=1, source_target_pairs={{0,8},{8,0},{16,24},{24,16},{32,40},{40,32},{48,56},{56,48},{64,72... | collective-permute-start | bytes 393224 | tf_op jit(solution)/shard_map/ppermute | solution.py:284

commit v5 on v4

--- a/solution.py
+++ b/solution.py
@@ -12,7 +12,6 @@
 LANES = 128
 PAIR = 2 * NB
 CHIPS = 8
-HIGHEST = lax.Precision.HIGHEST
 F32 = jnp.float32
 BF16 = jnp.bfloat16
 
@@ -117,46 +116,73 @@
     return jnp.concatenate(parts, axis=0)
 
 
+def halves_of(value):
+    high = value.astype(BF16)
+    return high, (value - high.astype(F32)).astype(BF16)
+
+
 def step_kernel(step, names, *refs):
     ref = dict(zip(names, refs))
     row, col = lax.axis_index("row"), lax.axis_index("col")
     me, core = row // 2, lax.rem(row, 2)
     chip = CHIPS - 1 - step
     active = me == chip
-    inv_mine, inv_other, pend, x = ref["inv_mine"], ref["inv_other"], ref["pend"], ref["x"]
+    inv_mine, inv_other, pend, x, send = ref["inv_mine"], ref["inv_other"], ref["pend"], ref["x"], ref["send"]
     tiles = ref["tiles"] if step else ref["tiles_out"]
+    own = pl.ds(pl.multiple_of(core * NB, NB), NB)
+    others = pl.ds(pl.multiple_of((1 - core) * NB, NB), NB)
 
     def tile(source):
         return tiles[lax.bitwise_xor(col, source)]
 
-    def product(source, value):
-        return jnp.dot(tile(source), value, precision=HIGHEST, preferred_element_type=F32)
+    def product(*terms):
+        lhs = jnp.concatenate([tile(source) for source, _ in terms], axis=1)
+        rhs = jnp.concatenate([value[...] for _, value in terms], axis=0)
+        both = jnp.dot(lhs, rhs, preferred_element_type=F32)
+        return both[:PAIR] + both[PAIR:]
 
     if step == 0:
-        mine = pl.ds(pl.multiple_of(core * NB, NB), NB)
-        theirs = pl.ds(pl.multiple_of((1 - core) * NB, NB), NB)
         for index in range(CHIPS):
-            tiles[index, mine, :] = ref["sent"][pl.ds(index * NB, NB), :]
-            tiles[index, theirs, :] = ref["swapped"][pl.ds(index * NB, NB), :]
-        pend[mine, :] = ref["rhs_mine"][...]
-        pend[theirs, :] = ref["swapped"][pl.ds(CHIPS * NB, NB), :]
+            for rows, name in ((own, "sent"), (others, "swapped")):
+                high, low = halves_of(ref[name][pl.ds(index * NB, NB), :])
+                tiles[index, rows, :] = high
+                first = core if name == "sent" else 1 - core
+                tiles[index, pl.ds(pl.multiple_of(PAIR + first * NB, NB), NB), :] = low
+        pend[own, :] = ref["rhs_mine"][...]
+        pend[others, :] = ref["swapped"][pl.ds(CHIPS * NB, NB), :]
     else:
         pend[...] = ref["pend_in"][...]
 
     @pl.when(active)
     def _():
         if step:
-            total = pend[...] - product(chip + 1, ref["near"][...])
+            near = ref["near"]
+            low = jnp.concatenate([near[PAIR:, :], jnp.zeros((NB, LANES), BF16)], axis=0)
+            terms = [(chip + 1, near[:PAIR, :]), (chip + 1, low)]
             if step > 1:
-                total -= product(chip + 2, ref["far2"][...])
-            pend[...] = total
+                terms.append((chip + 2, ref["far2"]))
+            pend[...] -= product(*terms)
 
         def solve(odd, even):
             x_odd = apply_inverse(odd, pend[NB:, :])
             x[NB:, :] = x_odd
-            padded = jnp.concatenate([jnp.zeros_like(x_odd), x_odd], axis=0)
-            within = jnp.dot(tile(me)[:NB, :], padded, precision=HIGHEST, preferred_element_type=F32)
-            x[:NB, :] = apply_inverse(even, pend[:NB, :] - within)
+            high, low = halves_of(x_odd)
+            send[NB:, :] = high
+            parts = jnp.concatenate([high, low], axis=1)
+            padded = jnp.concatenate([jnp.zeros_like(parts), parts], axis=0)
+            diagonal = tile(me)
+            lhs = jnp.concatenate([diagonal[:NB, :], diagonal[PAIR : PAIR + NB, :]], axis=0)
+            both = jnp.dot(lhs, padded, preferred_element_type=F32)
+            within = both[:NB, :LANES] + (both[:NB, LANES:] + both[NB:, :LANES])
+            x_even = apply_inverse(even, pend[:NB, :] - within)
+            x[:NB, :] = x_even
+            high_even, low_even = halves_of(x_even)
+            send[:NB, :] = high_even
+            if step < CHIPS - 1:
+                ahead = ref["ahead"]
+                ahead[:NB, :] = high_even
+                ahead[NB:PAIR, :] = high
+                ahead[PAIR:, :] = low_even
 
         @pl.when(core == 1)
         def _():
@@ -169,39 +195,46 @@
     @pl.when(jnp.logical_not(active))
     def _():
         x[...] = ref["x_in"][...] if step else jnp.zeros_like(x)
+        send[...] = ref["send_in"][...] if step else jnp.zeros_like(send)
+        if step < CHIPS - 1:
+            ref["ahead"][...] = jnp.zeros_like(ref["ahead"])
         if step > 1:
             from2, from3 = 2 * chip + 2 - me, 2 * chip + 1 - me
 
             @pl.when(jnp.logical_and(me < chip, from2 < CHIPS))
             def _():
-                pend[...] -= product(from2, ref["far2"][...])
+                pend[...] -= product((from2, ref["far2"]))
 
             if "far3" in ref:
 
                 @pl.when(jnp.logical_and(me < chip, from3 < CHIPS))
                 def _():
-                    pend[...] -= product(from3, ref["far3"][...])
+                    pend[...] -= product((from3, ref["far3"]))
 
     if step == CHIPS - 1:
-        ref["factor"][...] = x[...].astype(BF16)
-        ref["mine"][...] = x[pl.ds(pl.multiple_of(core * NB, NB), NB), :]
-        ref["theirs"][...] = x[pl.ds(pl.multiple_of((1 - core) * NB, NB), NB), :]
+        ref["mine"][...] = x[own, :]
+        ref["theirs"][...] = x[others, :]
 
 
 def solve_step(step, operands):
     block = pltpu.VMEM((PAIR, LANES), F32)
-    outs = {"pend": block, "x": block}
+    outs = {"send": pltpu.VMEM((PAIR, LANES), BF16)}
+    scratch = {}
+    if step == CHIPS - 1:
+        outs["mine"] = outs["theirs"] = pltpu.VMEM((NB, LANES), F32)
+        scratch["pend"] = scratch["x"] = block
+    else:
+        outs["pend"] = outs["x"] = block
+        outs["ahead"] = pltpu.VMEM((PAIR + NB, LANES), BF16)
     if step == 0:
-        outs["tiles_out"] = pltpu.VMEM((CHIPS, PAIR, LANES), F32)
-    if step == CHIPS - 1:
-        outs["factor"] = pltpu.VMEM((PAIR, LANES), BF16)
-        outs["mine"] = outs["theirs"] = pltpu.VMEM((NB, LANES), F32)
-    names = list(operands) + list(outs)
+        outs["tiles_out"] = pltpu.VMEM((CHIPS, 2 * PAIR, LANES), BF16)
+    names = list(operands) + list(outs) + list(scratch)
     call = pl.pallas_call(
         functools.partial(step_kernel, step, names),
         out_shape=tuple(outs.values()),
         in_specs=[VMEM] * len(operands),
         out_specs=(VMEM,) * len(outs),
+        scratch_shapes=tuple(scratch.values()),
         compiler_params=pltpu.CompilerParams(vmem_limit_bytes=16 << 20),
         cost_estimate=pl.CostEstimate(flops=8_000_000, bytes_accessed=5_000_000, transcendentals=0),
         name="solve_step",
@@ -210,37 +243,42 @@
     return dict(zip(outs, result))
 
 
-BLOCK = 512
-
-
-def stack_kernel(a, b, c, d, out):
-    for index, part in enumerate((a, b, c, d)):
-        out[index] = part[...]
-
-
-def stack4(*parts):
+BLOCK = 1536
+
+
+def stack_kernel(*refs):
+    parts, out = refs[:-1], refs[-1]
+    size = out.shape[0] // len(parts)
+    for index, part in enumerate(parts):
+        out[pl.ds(index * size, size)] = part[...].reshape((size,) + out.shape[1:])
+
+
+def stack(*parts):
+    block = parts[0].shape[-2:]
+    blocks = sum(part.size for part in parts) // (block[0] * block[1])
     return pl.pallas_call(
         stack_kernel,
-        out_shape=jax.ShapeDtypeStruct((4,) + parts[0].shape, parts[0].dtype),
-        in_specs=[VMEM] * 4,
+        out_shape=pltpu.VMEM((blocks,) + block, parts[0].dtype),
+        in_specs=[VMEM] * len(parts),
         out_specs=VMEM,
         compiler_params=pltpu.CompilerParams(vmem_limit_bytes=8 << 20),
-        name="stack4",
+        name="stack",
     )(*parts)
 
 
-def product_kernel(same, same_swap, cross, cross_swap, mine, theirs, v0, v1, v2, v3, a4, b4, a5, b5, v6, v7, out, slab, x_all):
+def product_kernel(pair, far1, far2, far3, pair_swap, far_swap, mine, theirs, v0, v1, v2, v3, a4, b4, a5, b5, v6, v7, out, slab, x_all):
     row, col = lax.axis_index("row"), lax.axis_index("col")
     core, xlo, y = lax.rem(row, 2), lax.rem(row // 2, 2), row // 4
 
     @pl.when(pl.program_id(0) == 0)
     def _():
-        for mask in range(4):
-            source = 2 * lax.bitwise_xor(y, mask) + xlo
-            for index, left, right in ((source, same, same_swap), (lax.bitwise_xor(source, 1), cross, cross_swap)):
+        for mask, left in enumerate((pair, far1, far2, far3)):
+            for cross in range(2):
+                index = lax.bitwise_xor(2 * lax.bitwise_xor(y, mask) + xlo, cross)
                 slot = pl.ds(pl.multiple_of(lax.bitwise_xor(col, index) * PAIR, PAIR), PAIR)
-                x_all[slot, core_lanes(core)] = left[mask]
-                x_all[slot, core_lanes(1 - core)] = right[mask]
+                x_all[slot, core_lanes(core)] = left[cross]
+                right = far_swap[2 * mask - 2 + cross] if mask else pair_swap[cross]
+                x_all[slot, core_lanes(1 - core)] = right
         slab[:, core_lanes(core)] = mine[...]
         slab[:, core_lanes(1 - core)] = theirs[...]
 
@@ -267,7 +305,7 @@
             jax.ShapeDtypeStruct((rows, 2 * LANES), BF16),
             jax.ShapeDtypeStruct((NB, 2 * LANES), F32),
         ),
-        in_specs=[VMEM] * 16,
+        in_specs=[VMEM] * 18,
         out_specs=(pl.BlockSpec((BLOCK, 2 * LANES), lambda i: (i, 0)), VMEM),
         scratch_shapes=[pltpu.VMEM((CHIPS * PAIR, 2 * LANES), BF16)],
         compiler_params=pltpu.CompilerParams(vmem_limit_bytes=24 << 20),
@@ -286,7 +324,7 @@
     def row_flip(value, mask):
         return row_move(value, flip(2 * CHIPS, mask))
 
-    t0 = jnp.stack([schur_rows, col_flip(schur_rows, 1)])
+    t0 = stack(schur_rows, col_flip(schur_rows, 1))
     parts = [t0] + [col_flip(t0, mask) for mask in (2, 4, 6)]
     inv_from = row_flip(inverses, 1)
 
@@ -303,11 +341,12 @@
     late = {}
     for step in range(1, CHIPS):
         near, far2, far3 = moves(step - 1)
-        operands = {"pend_in": state["pend"], "x_in": state["x"], "near": row_move(state["x"], near)}
+        operands = {"pend_in": state["pend"], "x_in": state["x"], "send_in": state["send"]}
+        operands["near"] = row_move(state["ahead"], near)
         operands.update(late)
-        late = {name: row_move(state["x"], pairs) for name, pairs in (("far2", far2), ("far3", far3)) if pairs}
+        late = {name: row_move(state["send"], pairs) for name, pairs in (("far2", far2), ("far3", far3)) if pairs}
         state = solve_step(step, {**operands, **kept})
-        if step == 2:
+        if step == 1:
             v[1], _ = lax.optimization_barrier((v[1], state["x"]))
             v[3], v[7] = col_flip(v[1], 2), col_flip(v[1], 6)
         if step == 3:
@@ -317,10 +356,10 @@
             v[3], v[7], _ = lax.optimization_barrier((v[3], v[7], state["x"]))
             a5, b5 = col_flip(v[7][:split], 2), col_flip(v[3][split:], 6)
 
-    factor = state["factor"]
-    same = stack4(factor, *[row_flip(factor, 4 * mask) for mask in (1, 2, 3)])
-    cross = row_flip(same, 2)
-    factors = (same, row_flip(same, 1), cross, row_flip(cross, 1))
+    factor = state["send"]
+    pair = stack(factor, row_flip(factor, 2))
+    far = [row_flip(pair, 4 * mask) for mask in (1, 2, 3)]
+    factors = (pair, *far, row_flip(pair, 1), row_flip(stack(*far), 1))
     slabs = (state["mine"], row_flip(state["theirs"], 1))
     return back_transform(factors, slabs, (v[0], v[1], v[2], v[3], a4, b4, a5, b5, v[6], v[7]))
 

time: 133 us -> 147 us (1.11)
  waiting for transfers between devices: 85.8 us -> 100 us
  starting transfers between devices: 34.3 us -> 36.4 us
  Pallas kernels: 8.98 us -> 6.95 us
    ppermute x27, waiting for transfers between devices: 63.4 us -> 72 us  [row_move(): return lax.ppermute(value, 'row', pairs)]
    ppermute x13, waiting for transfers between devices: 22.4 us -> 28.2 us  [col_flip(): return lax.ppermute(value, 'col', flip(CHIPS, mask))]
    ppermute x27, starting transfers between devices: 16.8 us -> 19.1 us  [row_move(): return lax.ppermute(value, 'row', pairs)]
  transfers between devices with their start and end apart: 40 -> 40, of which waited for: 17 -> 19; matrix products, arithmetic and copies ran while one was open for 1% -> 0% of each run, Pallas kernels for 4% -> 3%
where the time goes in v5:
time: 147 us; the launch traced here: 146 us
  waiting for transfers between devices  100 us (68%)
  starting transfers between devices  36.4 us (25%)
  Pallas kernels  6.95 us (5%)
    ppermute x27, waiting for transfers between devices, row_move(): return lax.ppermute(value, 'row', pairs)  72 us
    ppermute x13, waiting for transfers between devices, col_flip(): return lax.ppermute(value, 'col', flip(CHIPS, mask))  28.2 us
    ppermute x27, starting transfers between devices, row_move(): return lax.ppermute(value, 'row', pairs)  19.1 us
    ppermute x13, starting transfers between devices, col_flip(): return lax.ppermute(value, 'col', flip(CHIPS, mask))  17.2 us
    pallas_call x1, Pallas kernels, back_transform(): pl.pallas_call(product_kernel, grid=(rows // BLOCK,), out_shape=(jax.Shap...  3 us
  transfers between devices with their start and end apart: 40, of which 19 were waited for; matrix products, arithmetic and copies ran while one was open for 0% of the time, Pallas kernels for 3%

profile of v5, /device:TPU:0, one launch (start us, length us, event | category | flops | bytes accessed | tf_op | source)
XLA Modules:
  0.0 145.7 jit_solution(5901170656120105388)
XLA Ops:
  0.6 0.1 collective-permute-start
  0.7 3.2 %collective-permute-start.31 = (bf16[3072,128]{1,0:T(8,128)(2,1)}, bf16[3072,128]{1,0:T(8,128)(2,1)S(1)}, u32[]{:S(2)}, u32[]{:S(2)}) collective-permute-start(bf16[3072,128]{1,0:T(8,128)(2,1)} %v0.1), channel_id=1, source_target_pairs={{0,1},{1,0},{2,3},{3,2},{4,5},{5,4},{6,7},{7,6},{8,9},{9,8},{10,11... | collective-permute-start | bytes 2359304 | tf_op jit(solution)/shard_map/ppermute | solution.py:319
  3.9 0.4 collective-permute-start.1
  4.3 18.7 %collective-permute-done.1.refs_1_ = f32[64,128]{1,0:T(8,128)S(1)} collective-permute-done((f32[64,128]{1,0:T(8,128)}, f32[64,128]{1,0:T(8,128)S(1)}, u32[]{:S(2)}, u32[]{:S(2)}) %collective-permute-start.1) | collective-permute-done | bytes 32800 | tf_op jit(solution)/shard_map/ppermute | solution.py:319
  23.1 0.8 copy-done.1
  23.8 2.0 %collective-permute-start.2 = (f32[2,64,128]{2,1,0:T(8,128)S(1)}, f32[2,64,128]{2,1,0:T(8,128)S(1)}, u32[]{:S(2)}, u32[]{:S(2)}) collective-permute-start(f32[2,64,128]{2,1,0:T(8,128)S(1)} %stack.3.t0), channel_id=1, source_target_pairs={{0,2},{1,3},{2,0},{3,1},{4,6},{5,7},{6,4},{7,5},{8,10},{9,11},{10,... | collective-permute-start | bytes 196616 | tf_op jit(solution)/shard_map/ppermute | solution.py:319
  25.9 3.6 %collective-permute-start.3 = (f32[2,64,128]{2,1,0:T(8,128)S(1)}, f32[2,64,128]{2,1,0:T(8,128)S(1)}, u32[]{:S(2)}, u32[]{:S(2)}) collective-permute-start(f32[2,64,128]{2,1,0:T(8,128)S(1)} %stack.3.t0), channel_id=1, source_target_pairs={{0,4},{1,5},{2,6},{3,7},{4,0},{5,1},{6,2},{7,3},{8,12},{9,13},{10,... | collective-permute-start | bytes 196616 | tf_op jit(solution)/shard_map/ppermute | solution.py:319
  29.5 1.8 %setup.1 = (f32[64,64,128]{2,1,0:T(8,128)S(1)}, f32[64,64,128]{2,1,0:T(8,128)S(1)}, f32[64,128]{1,0:T(8,128)S(1)}, f32[64,128]{1,0:T(8,128)S(1)}) custom-call(f32[64,2048]{1,0:T(8,128)} %candidates_from.1, s32[1,256]{1,0:T(1,128)} %bitcast.1, f32[64,64,256]{2,1,0:T(8,128)} %inv.1, f32[64,64,256]{2,1,0:T(8,128)S(1)} %collective-permute-done.inv_from), custom_call_target="tpu_custom_call" | custom-call | flops 100000000 | bytes 5000000 | tf_op jit(solution)/shard_map/setup/pallas_call | solution.py:76
  31.3 1.1 collective-permute-done.3.t2
  32.4 2.5 %collective-permute-done.4.t3 = f32[2,64,128]{2,1,0:T(8,128)S(1)} collective-permute-done((f32[2,64,128]{2,1,0:T(8,128)S(1)}, f32[2,64,128]{2,1,0:T(8,128)S(1)}, u32[]{:S(2)}, u32[]{:S(2)}) %collective-permute-start.4) | collective-permute-done | bytes 65568 | tf_op jit(solution)/shard_map/ppermute | solution.py:319
  35.0 0.1 collective-permute-start.5
  35.1 1.6 %collective-permute-done.5.refs_2_ = f32[576,128]{1,0:T(8,128)S(1)} collective-permute-done((f32[576,128]{1,0:T(8,128)S(1)}, f32[576,128]{1,0:T(8,128)S(1)}, u32[]{:S(2)}, u32[]{:S(2)}) %collective-permute-start.5) | collective-permute-done | bytes 294944 | tf_op jit(solution)/shard_map/ppermute | solution.py:322
  36.6 0.1 solve_step.8
  36.7 0.8 collective-permute-start.6
  37.5 0.2 copy-done
  37.8 0.0 collective-permute-start.32
  37.8 0.9 collective-permute-start.33
  38.7 1.2 collective-permute-start.34
  39.9 2.6 %collective-permute-start.35 = (bf16[3072,128]{1,0:T(8,128)(2,1)S(1)}, bf16[3072,128]{1,0:T(8,128)(2,1)S(1)}, u32[]{:S(2)}, u32[]{:S(2)}) collective-permute-start(bf16[3072,128]{1,0:T(8,128)(2,1)S(1)} %collective-permute-done.31.v1), channel_id=1, source_target_pairs={{0,6},{1,7},{2,4},{3,5},{4,2},{5,3},{6,0},{7,1},{8,14},{9,15},{10,... | collective-permute-start | bytes 2359304 | tf_op jit(solution)/shard_map/ppermute | solution.py:319
  42.5 0.7 collective-permute-start.8
  43.2 0.7 collective-permute-start.9
  43.9 0.7 collective-permute-start.11
  44.6 0.7 collective-permute-start.7
  45.3 0.7 collective-permute-start.12
  46.0 0.7 collective-permute-start.14
  46.7 0.7 collective-permute-start.10
  47.4 1.3 collective-permute-start.15
  48.7 18.3 %collective-permute-done.15.refs_5_ = bf16[128,128]{1,0:T(8,128)(2,1)S(1)} collective-permute-done((bf16[128,128]{1,0:T(8,128)(2,1)S(1)}, bf16[128,128]{1,0:T(8,128)(2,1)S(1)}, u32[]{:S(2)}, u32[]{:S(2)}) %collective-permute-start.15) | collective-permute-done | bytes 32800 | tf_op jit(solution)/shard_map/ppermute | solution.py:322
  67.0 1.3 collective-permute-start.17
  68.3 6.8 %collective-permute-done.17.refs_4_ = bf16[128,128]{1,0:T(8,128)(2,1)S(1)} collective-permute-done((bf16[128,128]{1,0:T(8,128)(2,1)S(1)}, bf16[128,128]{1,0:T(8,128)(2,1)S(1)}, u32[]{:S(2)}, u32[]{:S(2)}) %collective-permute-start.17) | collective-permute-done | bytes 32800 | tf_op jit(solution)/shard_map/ppermute | solution.py:322
  75.1 0.7 collective-permute-start.13
  75.8 1.3 collective-permute-start.18
  77.1 0.2 solve_step.12
  77.3 8.5 %collective-permute-done.18.refs_5_ = bf16[128,128]{1,0:T(8,128)(2,1)S(1)} collective-permute-done((bf16[128,128]{1,0:T(8,128)(2,1)S(1)}, bf16[128,128]{1,0:T(8,128)(2,1)S(1)}, u32[]{:S(2)}, u32[]{:S(2)}) %collective-permute-start.18) | collective-permute-done | bytes 32800 | tf_op jit(solution)/shard_map/ppermute | solution.py:322
  85.7 1.3 collective-permute-start.20
  87.0 6.8 %collective-permute-done.20.refs_4_ = bf16[128,128]{1,0:T(8,128)(2,1)S(1)} collective-permute-done((bf16[128,128]{1,0:T(8,128)(2,1)S(1)}, bf16[128,128]{1,0:T(8,128)(2,1)S(1)}, u32[]{:S(2)}, u32[]{:S(2)}) %collective-permute-start.20) | collective-permute-done | bytes 32800 | tf_op jit(solution)/shard_map/ppermute | solution.py:322
  93.9 0.7 collective-permute-start.16
  94.5 1.3 collective-permute-start.21
  95.8 0.5 solve_step.13
  96.4 7.5 %collective-permute-done.21.refs_5_ = bf16[128,128]{1,0:T(8,128)(2,1)S(1)} collective-permute-done((bf16[128,128]{1,0:T(8,128)(2,1)S(1)}, bf16[128,128]{1,0:T(8,128)(2,1)S(1)}, u32[]{:S(2)}, u32[]{:S(2)}) %collective-permute-start.21) | collective-permute-done | bytes 32800 | tf_op jit(solution)/shard_map/ppermute | solution.py:322
  103.9 0.7 collective-permute-start.19
  104.6 1.3 collective-permute-start.23
  105.9 0.3 solve_step.14
  106.2 4.2 %collective-permute-done.23.refs_4_ = bf16[128,128]{1,0:T(8,128)(2,1)S(1)} collective-permute-done((bf16[128,128]{1,0:T(8,128)(2,1)S(1)}, bf16[128,128]{1,0:T(8,128)(2,1)S(1)}, u32[]{:S(2)}, u32[]{:S(2)}) %collective-permute-start.23) | collective-permute-done | bytes 32800 | tf_op jit(solution)/shard_map/ppermute | solution.py:322
  110.4 1.3 collective-permute-start.22
  111.7 4.7 %collective-permute-done.22.refs_3_ = bf16[192,128]{1,0:T(8,128)(2,1)S(1)} collective-permute-done((bf16[192,128]{1,0:T(8,128)(2,1)S(1)}, bf16[192,128]{1,0:T(8,128)(2,1)S(1)}, u32[]{:S(2)}, u32[]{:S(2)}) %collective-permute-start.22) | collective-permute-done | bytes 49184 | tf_op jit(solution)/shard_map/ppermute | solution.py:322
  116.4 0.9 solve_step.15
  117.2 0.1 collective-permute-start.24
  117.3 3.9 %collective-permute-done.24.refs_1_ = bf16[128,128]{1,0:T(8,128)(2,1)S(1)} collective-permute-done((bf16[128,128]{1,0:T(8,128)(2,1)S(1)}, bf16[128,128]{1,0:T(8,128)(2,1)S(1)}, u32[]{:S(2)}, u32[]{:S(2)}) %collective-permute-start.24) | collective-permute-done | bytes 32800 | tf_op jit(solution)/shard_map/ppermute | solution.py:322
  121.2 0.1 collective-permute-start.30
  121.4 0.1 collective-permute-start.36
  121.5 1.5 collective-permute-start.37
  123.1 0.8 collective-permute-start.38
  123.9 1.6 %collective-permute-done.25.refs_0_.far1 = bf16[2,128,128]{2,1,0:T(8,128)(2,1)S(1)} collective-permute-done((bf16[2,128,128]{2,1,0:T(8,128)(2,1)S(1)}, bf16[2,128,128]{2,1,0:T(8,128)(2,1)S(1)}, u32[]{:S(2)}, u32[]{:S(2)}) %collective-permute-start.25) | collective-permute-done | bytes 65568 | tf_op jit(solution)/shard_map/ppermute | solution.py:322
  125.5 0.9 collective-permute-start.39
  126.4 2.3 %collective-permute-done.26.refs_1_.far2 = bf16[2,128,128]{2,1,0:T(8,128)(2,1)S(1)} collective-permute-done((bf16[2,128,128]{2,1,0:T(8,128)(2,1)S(1)}, bf16[2,128,128]{2,1,0:T(8,128)(2,1)S(1)}, u32[]{:S(2)}, u32[]{:S(2)}) %collective-permute-start.26) | collective-permute-done | bytes 65568 | tf_op jit(solution)/shard_map/ppermute | solution.py:322
  128.7 2.2 %collective-permute-start.27 = (bf16[2,128,128]{2,1,0:T(8,128)(2,1)S(1)}, bf16[2,128,128]{2,1,0:T(8,128)(2,1)S(1)}, u32[]{:S(2)}, u32[]{:S(2)}) collective-permute-start(bf16[2,128,128]{2,1,0:T(8,128)(2,1)S(1)} %stack.4.pair), channel_id=1, source_target_pairs={{0,96},{8,104},{16,112},{24,120},{32,64},{40,72},{48,80},{56,88},{... | collective-permute-start | bytes 196616 | tf_op jit(solution)/shard_map/ppermute | solution.py:322
  131.0 3.2 %collective-permute-done.27.refs_2_.far3 = bf16[2,128,128]{2,1,0:T(8,128)(2,1)S(1)} collective-permute-done((bf16[2,128,128]{2,1,0:T(8,128)(2,1)S(1)}, bf16[2,128,128]{2,1,0:T(8,128)(2,1)S(1)}, u32[]{:S(2)}, u32[]{:S(2)}) %collective-permute-start.27) | collective-permute-done | bytes 65568 | tf_op jit(solution)/shard_map/ppermute | solution.py:322
  134.2 1.2 collective-permute-done.28.pair_swap
  135.5 0.2 collective-permute-start.29
  135.6 1.3 collective-permute-done.29.far_swap
  136.9 4.5 %collective-permute-done.38.a5 = bf16[1536,128]{1,0:T(8,128)(2,1)S(1)} collective-permute-done((bf16[1536,128]{1,0:T(8,128)(2,1)S(1)}, bf16[1536,128]{1,0:T(8,128)(2,1)S(1)}, u32[]{:S(2)}, u32[]{:S(2)}) %collective-permute-start.38) | collective-permute-done | bytes 393248 | tf_op jit(solution)/shard_map/ppermute | solution.py:319
  141.4 1.3 collective-permute-done.39.b5
  142.7 3.0 %back_transform.1 = (bf16[3072,256]{1,0:T(8,128)(2,1)}, f32[64,256]{1,0:T(8,128)}) custom-call(bf16[2,128,128]{2,1,0:T(8,128)(2,1)S(1)} %stack.4.pair, bf16[2,128,128]{2,1,0:T(8,128)(2,1)S(1)} %collective-permute-done.25.refs_0_.far1, bf16[2,128,128]{2,1,0:T(8,128)(2,1)S(1)} %collective-permute-done.26.refs_1_.far2, ...), custom_call_target="tpu_custom_call" | custom-call | flops 1610612736 | bytes 8000000 | tf_op jit(solution)/shard_map/back_transform/pallas_call | solution.py:301
  (38 shorter events, 0.3 us)
Async XLA Ops:
  0.6 28.8 %collective-permute-start = (f32[64,64,256]{2,1,0:T(8,128)}, f32[64,64,256]{2,1,0:T(8,128)S(1)}, u32[]{:S(2)}, u32[]{:S(2)}) collective-permute-start(f32[64,64,256]{2,1,0:T(8,128)} %inv.1), channel_id=1, source_target_pairs={{0,8},{8,0},{16,24},{24,16},{32,40},{40,32},{48,56},{56,48},{64,72... | collective-permute-start | bytes 12582920 | tf_op jit(solution)/shard_map/ppermute | solution.py:322
  0.7 37.9 %collective-permute-start.31 = (bf16[3072,128]{1,0:T(8,128)(2,1)}, bf16[3072,128]{1,0:T(8,128)(2,1)S(1)}, u32[]{:S(2)}, u32[]{:S(2)}) collective-permute-start(bf16[3072,128]{1,0:T(8,128)(2,1)} %v0.1), channel_id=1, source_target_pairs={{0,1},{1,0},{2,3},{3,2},{4,5},{5,4},{6,7},{7,6},{8,9},{9,8},{10,11... | collective-permute-start | bytes 2359304 | tf_op jit(solution)/shard_map/ppermute | solution.py:319
  3.9 19.1 %collective-permute-start.1 = (f32[64,128]{1,0:T(8,128)}, f32[64,128]{1,0:T(8,128)S(1)}, u32[]{:S(2)}, u32[]{:S(2)}) collective-permute-start(f32[64,128]{1,0:T(8,128)} %refs_0_.1), channel_id=1, source_target_pairs={{0,1},{1,0},{2,3},{3,2},{4,5},{5,4},{6,7},{7,6},{8,9},{9,8},{10,11... | collective-permute-start | bytes 98312 | tf_op jit(solution)/shard_map/ppermute | solution.py:319
  23.1 0.8 copy-start.1
  23.8 7.5 %collective-permute-start.2 = (f32[2,64,128]{2,1,0:T(8,128)S(1)}, f32[2,64,128]{2,1,0:T(8,128)S(1)}, u32[]{:S(2)}, u32[]{:S(2)}) collective-permute-start(f32[2,64,128]{2,1,0:T(8,128)S(1)} %stack.3.t0), channel_id=1, source_target_pairs={{0,2},{1,3},{2,0},{3,1},{4,6},{5,7},{6,4},{7,5},{8,10},{9,11},{10,... | collective-permute-start | bytes 196616 | tf_op jit(solution)/shard_map/ppermute | solution.py:319
  25.9 6.5 %collective-permute-start.3 = (f32[2,64,128]{2,1,0:T(8,128)S(1)}, f32[2,64,128]{2,1,0:T(8,128)S(1)}, u32[]{:S(2)}, u32[]{:S(2)}) collective-permute-start(f32[2,64,128]{2,1,0:T(8,128)S(1)} %stack.3.t0), channel_id=1, source_target_pairs={{0,4},{1,5},{2,6},{3,7},{4,0},{5,1},{6,2},{7,3},{8,12},{9,13},{10,... | collective-permute-start | bytes 196616 | tf_op jit(solution)/shard_map/ppermute | solution.py:319
  29.5 5.5 %collective-permute-start.4 = (f32[2,64,128]{2,1,0:T(8,128)S(1)}, f32[2,64,128]{2,1,0:T(8,128)S(1)}, u32[]{:S(2)}, u32[]{:S(2)}) collective-permute-start(f32[2,64,128]{2,1,0:T(8,128)S(1)} %stack.3.t0), channel_id=1, source_target_pairs={{0,6},{1,7},{2,4},{3,5},{4,2},{5,3},{6,0},{7,1},{8,14},{9,15},{10,... | collective-permute-start | bytes 196616 | tf_op jit(solution)/shard_map/ppermute | solution.py:319
  35.0 1.7 %collective-permute-start.5 = (f32[576,128]{1,0:T(8,128)S(1)}, f32[576,128]{1,0:T(8,128)S(1)}, u32[]{:S(2)}, u32[]{:S(2)}) collective-permute-start(f32[576,128]{1,0:T(8,128)S(1)} %join.1.refs_1_), channel_id=1, source_target_pairs={{0,8},{8,0},{16,24},{24,16},{32,40},{40,32},{48,56},{56,48},{64,72... | collective-permute-start | bytes 884744 | tf_op jit(solution)/shard_map/ppermute | solution.py:322
  36.6 1.1 copy-start
  36.7 1.9 %collective-permute-start.6 = (bf16[192,128]{1,0:T(8,128)(2,1)S(1)}, bf16[192,128]{1,0:T(8,128)(2,1)S(1)}, u32[]{:S(2)}, u32[]{:S(2)}) collective-permute-start(bf16[192,128]{1,0:T(8,128)(2,1)S(1)} %get-tuple-element.50), channel_id=1, source_target_pairs={{112,96},{120,104},{113,97},{121,105},{114,98},{122,106},{115,99},... | collective-permute-start | bytes 147464 | tf_op jit(solution)/shard_map/ppermute | solution.py:322
  37.8 83.5 %collective-permute-start.32 = (bf16[3072,128]{1,0:T(8,128)(2,1)S(1)}, bf16[3072,128]{1,0:T(8,128)(2,1)S(1)}, u32[]{:S(2)}, u32[]{:S(2)}) collective-permute-start(bf16[3072,128]{1,0:T(8,128)(2,1)S(1)} %copy-done), channel_id=1, source_target_pairs={{0,2},{1,3},{2,0},{3,1},{4,6},{5,7},{6,4},{7,5},{8,10},{9,11},{10,... | collective-permute-start | bytes 2359304 | tf_op jit(solution)/shard_map/ppermute | solution.py:319
  37.8 83.6 %collective-permute-start.33 = (bf16[3072,128]{1,0:T(8,128)(2,1)S(1)}, bf16[3072,128]{1,0:T(8,128)(2,1)S(1)}, u32[]{:S(2)}, u32[]{:S(2)}) collective-permute-start(bf16[3072,128]{1,0:T(8,128)(2,1)S(1)} %copy-done), channel_id=1, source_target_pairs={{0,6},{1,7},{2,4},{3,5},{4,2},{5,3},{6,0},{7,1},{8,14},{9,15},{10,... | collective-permute-start | bytes 2359304 | tf_op jit(solution)/shard_map/ppermute | solution.py:319
  38.7 82.8 %collective-permute-start.34 = (bf16[3072,128]{1,0:T(8,128)(2,1)S(1)}, bf16[3072,128]{1,0:T(8,128)(2,1)S(1)}, u32[]{:S(2)}, u32[]{:S(2)}) collective-permute-start(bf16[3072,128]{1,0:T(8,128)(2,1)S(1)} %collective-permute-done.31.v1), channel_id=1, source_target_pairs={{0,2},{1,3},{2,0},{3,1},{4,6},{5,7},{6,4},{7,5},{8,10},{9,11},{10,... | collective-permute-start | bytes 2359304 | tf_op jit(solution)/shard_map/ppermute | solution.py:319
  39.9 83.1 %collective-permute-start.35 = (bf16[3072,128]{1,0:T(8,128)(2,1)S(1)}, bf16[3072,128]{1,0:T(8,128)(2,1)S(1)}, u32[]{:S(2)}, u32[]{:S(2)}) collective-permute-start(bf16[3072,128]{1,0:T(8,128)(2,1)S(1)} %collective-permute-done.31.v1), channel_id=1, source_target_pairs={{0,6},{1,7},{2,4},{3,5},{4,2},{5,3},{6,0},{7,1},{8,14},{9,15},{10,... | collective-permute-start | bytes 2359304 | tf_op jit(solution)/shard_map/ppermute | solution.py:319
  42.5 0.7 collective-permute-start.8
  43.2 0.7 collective-permute-start.9
  43.9 0.7 collective-permute-start.11
  44.6 0.7 collective-permute-start.7
  45.3 0.7 collective-permute-start.12
  46.0 0.7 collective-permute-start.14
  46.7 0.7 collective-permute-start.10
  47.4 19.6 %collective-permute-start.15 = (bf16[128,128]{1,0:T(8,128)(2,1)S(1)}, bf16[128,128]{1,0:T(8,128)(2,1)S(1)}, u32[]{:S(2)}, u32[]{:S(2)}) collective-permute-start(bf16[128,128]{1,0:T(8,128)(2,1)S(1)} %get-tuple-element.58.refs_2_), channel_id=1, source_target_pairs={{80,32},{88,40},{96,16},{104,24},{112,0},{120,8},{81,33},{89,41},{... | collective-permute-start | bytes 98312 | tf_op jit(solution)/shard_map/ppermute | solution.py:322
  67.0 8.1 %collective-permute-start.17 = (bf16[128,128]{1,0:T(8,128)(2,1)S(1)}, bf16[128,128]{1,0:T(8,128)(2,1)S(1)}, u32[]{:S(2)}, u32[]{:S(2)}) collective-permute-start(bf16[128,128]{1,0:T(8,128)(2,1)S(1)} %get-tuple-element.62.refs_2_), channel_id=1, source_target_pairs={{64,32},{72,40},{80,16},{88,24},{96,0},{104,8},{65,33},{73,41},{81... | collective-permute-start | bytes 98312 | tf_op jit(solution)/shard_map/ppermute | solution.py:322
  75.1 0.7 collective-permute-start.13
  75.8 10.0 %collective-permute-start.18 = (bf16[128,128]{1,0:T(8,128)(2,1)S(1)}, bf16[128,128]{1,0:T(8,128)(2,1)S(1)}, u32[]{:S(2)}, u32[]{:S(2)}) collective-permute-start(bf16[128,128]{1,0:T(8,128)(2,1)S(1)} %get-tuple-element.62.refs_2_), channel_id=1, source_target_pairs={{64,16},{72,24},{80,0},{88,8},{65,17},{73,25},{81,1},{89,9},{66,18... | collective-permute-start | bytes 98312 | tf_op jit(solution)/shard_map/ppermute | solution.py:322
  85.7 8.1 %collective-permute-start.20 = (bf16[128,128]{1,0:T(8,128)(2,1)S(1)}, bf16[128,128]{1,0:T(8,128)(2,1)S(1)}, u32[]{:S(2)}, u32[]{:S(2)}) collective-permute-start(bf16[128,128]{1,0:T(8,128)(2,1)S(1)} %get-tuple-element.66.refs_2_), channel_id=1, source_target_pairs={{48,16},{56,24},{64,0},{72,8},{49,17},{57,25},{65,1},{73,9},{50,18... | collective-permute-start | bytes 98312 | tf_op jit(solution)/shard_map/ppermute | solution.py:322
  93.9 0.7 collective-permute-start.16
  94.5 9.4 %collective-permute-start.21 = (bf16[128,128]{1,0:T(8,128)(2,1)S(1)}, bf16[128,128]{1,0:T(8,128)(2,1)S(1)}, u32[]{:S(2)}, u32[]{:S(2)}) collective-permute-start(bf16[128,128]{1,0:T(8,128)(2,1)S(1)} %get-tuple-element.66.refs_2_), channel_id=1, source_target_pairs={{48,0},{56,8},{49,1},{57,9},{50,2},{58,10},{51,3},{59,11},{52,4},{... | collective-permute-start | bytes 98312 | tf_op jit(solution)/shard_map/ppermute | solution.py:322
  103.9 0.7 collective-permute-start.19
  104.6 5.8 %collective-permute-start.23 = (bf16[128,128]{1,0:T(8,128)(2,1)S(1)}, bf16[128,128]{1,0:T(8,128)(2,1)S(1)}, u32[]{:S(2)}, u32[]{:S(2)}) collective-permute-start(bf16[128,128]{1,0:T(8,128)(2,1)S(1)} %get-tuple-element.70.refs_2_), channel_id=1, source_target_pairs={{32,0},{40,8},{33,1},{41,9},{34,2},{42,10},{35,3},{43,11},{36,4},{... | collective-permute-start | bytes 98312 | tf_op jit(solution)/shard_map/ppermute | solution.py:322
  110.4 6.0 %collective-permute-start.22 = (bf16[192,128]{1,0:T(8,128)(2,1)S(1)}, bf16[192,128]{1,0:T(8,128)(2,1)S(1)}, u32[]{:S(2)}, u32[]{:S(2)}) collective-permute-start(bf16[192,128]{1,0:T(8,128)(2,1)S(1)} %get-tuple-element.75), channel_id=1, source_target_pairs={{16,0},{24,8},{17,1},{25,9},{18,2},{26,10},{19,3},{27,11},{20,4},{... | collective-permute-start | bytes 147464 | tf_op jit(solution)/shard_map/ppermute | solution.py:322
  117.2 4.0 %collective-permute-start.24 = (bf16[128,128]{1,0:T(8,128)(2,1)S(1)}, bf16[128,128]{1,0:T(8,128)(2,1)S(1)}, u32[]{:S(2)}, u32[]{:S(2)}) collective-permute-start(bf16[128,128]{1,0:T(8,128)(2,1)S(1)} %get-tuple-element.76.refs_0_), channel_id=1, source_target_pairs={{0,16},{8,24},{16,0},{24,8},{32,48},{40,56},{48,32},{56,40},{64,80... | collective-permute-start | bytes 98312 | tf_op jit(solution)/shard_map/ppermute | solution.py:322
  121.2 4.3 %collective-permute-start.25 = (bf16[2,128,128]{2,1,0:T(8,128)(2,1)S(1)}, bf16[2,128,128]{2,1,0:T(8,128)(2,1)S(1)}, u32[]{:S(2)}, u32[]{:S(2)}) collective-permute-start(bf16[2,128,128]{2,1,0:T(8,128)(2,1)S(1)} %stack.4.pair), channel_id=1, source_target_pairs={{0,32},{8,40},{16,48},{24,56},{32,0},{40,8},{48,16},{56,24},{64,96... | collective-permute-start | bytes 196616 | tf_op jit(solution)/shard_map/ppermute | solution.py:322
  121.2 1.8 %collective-permute-start.30 = (f32[64,128]{1,0:T(8,128)S(1)}, f32[64,128]{1,0:T(8,128)S(1)}, u32[]{:S(2)}, u32[]{:S(2)}) collective-permute-start(f32[64,128]{1,0:T(8,128)S(1)} %get-tuple-element.78), channel_id=1, source_target_pairs={{0,8},{8,0},{16,24},{24,16},{32,40},{40,32},{48,56},{56,48},{64,72... | collective-permute-start | bytes 98312 | tf_op jit(solution)/shard_map/ppermute | solution.py:322
  121.4 14.3 %collective-permute-start.36 = (bf16[1536,128]{1,0:T(8,128)(2,1)S(1)}, bf16[1536,128]{1,0:T(8,128)(2,1)S(1)}, u32[]{:S(2)}, u32[]{:S(2)}) collective-permute-start(bf16[1536,128]{1,0:T(8,128)(2,1)S(1)} %slice.12), channel_id=1, source_target_pairs={{0,2},{1,3},{2,0},{3,1},{4,6},{5,7},{6,4},{7,5},{8,10},{9,11},{10,... | collective-permute-start | bytes 1179656 | tf_op jit(solution)/shard_map/ppermute | solution.py:319
  121.5 14.1 %collective-permute-start.37 = (bf16[1536,128]{1,0:T(8,128)(2,1)S(1)}, bf16[1536,128]{1,0:T(8,128)(2,1)S(1)}, u32[]{:S(2)}, u32[]{:S(2)}) collective-permute-start(bf16[1536,128]{1,0:T(8,128)(2,1)S(1)} %slice.13), channel_id=1, source_target_pairs={{0,6},{1,7},{2,4},{3,5},{4,2},{5,3},{6,0},{7,1},{8,14},{9,15},{10,... | collective-permute-start | bytes 1179656 | tf_op jit(solution)/shard_map/ppermute | solution.py:319
  123.0 5.8 %collective-permute-start.26 = (bf16[2,128,128]{2,1,0:T(8,128)(2,1)S(1)}, bf16[2,128,128]{2,1,0:T(8,128)(2,1)S(1)}, u32[]{:S(2)}, u32[]{:S(2)}) collective-permute-start(bf16[2,128,128]{2,1,0:T(8,128)(2,1)S(1)} %stack.4.pair), channel_id=1, source_target_pairs={{0,64},{8,72},{16,80},{24,88},{32,96},{40,104},{48,112},{56,120},{... | collective-permute-start | bytes 196616 | tf_op jit(solution)/shard_map/ppermute | solution.py:322
  123.1 18.3 %collective-permute-start.38 = (bf16[1536,128]{1,0:T(8,128)(2,1)S(1)}, bf16[1536,128]{1,0:T(8,128)(2,1)S(1)}, u32[]{:S(2)}, u32[]{:S(2)}) collective-permute-start(bf16[1536,128]{1,0:T(8,128)(2,1)S(1)} %slice.14), channel_id=1, source_target_pairs={{0,2},{1,3},{2,0},{3,1},{4,6},{5,7},{6,4},{7,5},{8,10},{9,11},{10,... | collective-permute-start | bytes 1179656 | tf_op jit(solution)/shard_map/ppermute | solution.py:319
  125.5 17.3 %collective-permute-start.39 = (bf16[1536,128]{1,0:T(8,128)(2,1)S(1)}, bf16[1536,128]{1,0:T(8,128)(2,1)S(1)}, u32[]{:S(2)}, u32[]{:S(2)}) collective-permute-start(bf16[1536,128]{1,0:T(8,128)(2,1)S(1)} %slice.15), channel_id=1, source_target_pairs={{0,6},{1,7},{2,4},{3,5},{4,2},{5,3},{6,0},{7,1},{8,14},{9,15},{10,... | collective-permute-start | bytes 1179656 | tf_op jit(solution)/shard_map/ppermute | solution.py:319
  128.7 5.5 %collective-permute-start.27 = (bf16[2,128,128]{2,1,0:T(8,128)(2,1)S(1)}, bf16[2,128,128]{2,1,0:T(8,128)(2,1)S(1)}, u32[]{:S(2)}, u32[]{:S(2)}) collective-permute-start(bf16[2,128,128]{2,1,0:T(8,128)(2,1)S(1)} %stack.4.pair), channel_id=1, source_target_pairs={{0,96},{8,104},{16,112},{24,120},{32,64},{40,72},{48,80},{56,88},{... | collective-permute-start | bytes 196616 | tf_op jit(solution)/shard_map/ppermute | solution.py:322
  134.2 1.3 collective-permute-start.28
  135.5 1.4 collective-permute-start.29

commit v6 on v5

--- a/solution.py
+++ b/solution.py
@@ -11,6 +11,7 @@
 NB = 64
 LANES = 128
 PAIR = 2 * NB
+PLAIN_HOPS = 3
 CHIPS = 8
 F32 = jnp.float32
 BF16 = jnp.bfloat16
@@ -157,8 +158,10 @@
     def _():
         if step:
             near = ref["near"]
-            low = jnp.concatenate([near[PAIR:, :], jnp.zeros((NB, LANES), BF16)], axis=0)
-            terms = [(chip + 1, near[:PAIR, :]), (chip + 1, low)]
+            terms = [(chip + 1, near[:PAIR, :])]
+            if step > PLAIN_HOPS:
+                low = jnp.concatenate([near[PAIR:, :], jnp.zeros((NB, LANES), BF16)], axis=0)
+                terms.append((chip + 1, low))
             if step > 1:
                 terms.append((chip + 2, ref["far2"]))
             pend[...] -= product(*terms)
@@ -178,7 +181,7 @@
             x[:NB, :] = x_even
             high_even, low_even = halves_of(x_even)
             send[:NB, :] = high_even
-            if step < CHIPS - 1:
+            if PLAIN_HOPS <= step < CHIPS - 1:
                 ahead = ref["ahead"]
                 ahead[:NB, :] = high_even
                 ahead[NB:PAIR, :] = high
@@ -196,7 +199,7 @@
     def _():
         x[...] = ref["x_in"][...] if step else jnp.zeros_like(x)
         send[...] = ref["send_in"][...] if step else jnp.zeros_like(send)
-        if step < CHIPS - 1:
+        if PLAIN_HOPS <= step < CHIPS - 1:
             ref["ahead"][...] = jnp.zeros_like(ref["ahead"])
         if step > 1:
             from2, from3 = 2 * chip + 2 - me, 2 * chip + 1 - me
@@ -225,7 +228,8 @@
         scratch["pend"] = scratch["x"] = block
     else:
         outs["pend"] = outs["x"] = block
-        outs["ahead"] = pltpu.VMEM((PAIR + NB, LANES), BF16)
+        if step >= PLAIN_HOPS:
+            outs["ahead"] = pltpu.VMEM((PAIR + NB, LANES), BF16)
     if step == 0:
         outs["tiles_out"] = pltpu.VMEM((CHIPS, 2 * PAIR, LANES), BF16)
     names = list(operands) + list(outs) + list(scratch)
@@ -342,7 +346,7 @@
     for step in range(1, CHIPS):
         near, far2, far3 = moves(step - 1)
         operands = {"pend_in": state["pend"], "x_in": state["x"], "send_in": state["send"]}
-        operands["near"] = row_move(state["ahead"], near)
+        operands["near"] = row_move(state["ahead" if step > PLAIN_HOPS else "send"], near)
         operands.update(late)
         late = {name: row_move(state["send"], pairs) for name, pairs in (("far2", far2), ("far3", far3)) if pairs}
         state = solve_step(step, {**operands, **kept})

time: 147 us -> 143 us (0.973)
  waiting for transfers between devices: 100 us -> 97.2 us
    ppermute x27, waiting for transfers between devices: 72 us -> 69.5 us  [row_move(): return lax.ppermute(value, 'row', pairs)]
where the time goes in v6:
time: 143 us; the launch traced here: 142 us
  waiting for transfers between devices  97.2 us (68%)
  starting transfers between devices  36.1 us (25%)
  Pallas kernels  6.93 us (5%)
    ppermute x27, waiting for transfers between devices, row_move(): return lax.ppermute(value, 'row', pairs)  69.5 us
    ppermute x13, waiting for transfers between devices, col_flip(): return lax.ppermute(value, 'col', flip(CHIPS, mask))  27.7 us
    ppermute x27, starting transfers between devices, row_move(): return lax.ppermute(value, 'row', pairs)  18.6 us
    ppermute x13, starting transfers between devices, col_flip(): return lax.ppermute(value, 'col', flip(CHIPS, mask))  17.4 us
    pallas_call x1, Pallas kernels, back_transform(): pl.pallas_call(product_kernel, grid=(rows // BLOCK,), out_shape=(jax.Shap...  2.99 us
  transfers between devices with their start and end apart: 40, of which 19 were waited for; matrix products, arithmetic and copies ran while one was open for 0% of the time, Pallas kernels for 3%

profile of v6, /device:TPU:0, one launch (start us, length us, event | category | flops | bytes accessed | tf_op | source)
XLA Modules:
  0.0 142.4 jit_solution(16723844178965300304)
XLA Ops:
  0.6 0.1 collective-permute-start
  0.7 3.2 %collective-permute-start.31 = (bf16[3072,128]{1,0:T(8,128)(2,1)}, bf16[3072,128]{1,0:T(8,128)(2,1)S(1)}, u32[]{:S(2)}, u32[]{:S(2)}) collective-permute-start(bf16[3072,128]{1,0:T(8,128)(2,1)} %v0.1), channel_id=1, source_target_pairs={{0,1},{1,0},{2,3},{3,2},{4,5},{5,4},{6,7},{7,6},{8,9},{9,8},{10,11... | collective-permute-start | bytes 2359304 | tf_op jit(solution)/shard_map/ppermute | solution.py:323
  3.9 0.4 collective-permute-start.1
  4.3 18.7 %collective-permute-done.1.refs_1_ = f32[64,128]{1,0:T(8,128)S(1)} collective-permute-done((f32[64,128]{1,0:T(8,128)}, f32[64,128]{1,0:T(8,128)S(1)}, u32[]{:S(2)}, u32[]{:S(2)}) %collective-permute-start.1) | collective-permute-done | bytes 32800 | tf_op jit(solution)/shard_map/ppermute | solution.py:323
  23.1 0.8 copy-done.1
  23.8 2.0 %collective-permute-start.2 = (f32[2,64,128]{2,1,0:T(8,128)S(1)}, f32[2,64,128]{2,1,0:T(8,128)S(1)}, u32[]{:S(2)}, u32[]{:S(2)}) collective-permute-start(f32[2,64,128]{2,1,0:T(8,128)S(1)} %stack.3.t0), channel_id=1, source_target_pairs={{0,2},{1,3},{2,0},{3,1},{4,6},{5,7},{6,4},{7,5},{8,10},{9,11},{10,... | collective-permute-start | bytes 196616 | tf_op jit(solution)/shard_map/ppermute | solution.py:323
  25.9 3.6 %collective-permute-start.3 = (f32[2,64,128]{2,1,0:T(8,128)S(1)}, f32[2,64,128]{2,1,0:T(8,128)S(1)}, u32[]{:S(2)}, u32[]{:S(2)}) collective-permute-start(f32[2,64,128]{2,1,0:T(8,128)S(1)} %stack.3.t0), channel_id=1, source_target_pairs={{0,4},{1,5},{2,6},{3,7},{4,0},{5,1},{6,2},{7,3},{8,12},{9,13},{10,... | collective-permute-start | bytes 196616 | tf_op jit(solution)/shard_map/ppermute | solution.py:323
  29.5 1.8 %setup.1 = (f32[64,64,128]{2,1,0:T(8,128)S(1)}, f32[64,64,128]{2,1,0:T(8,128)S(1)}, f32[64,128]{1,0:T(8,128)S(1)}, f32[64,128]{1,0:T(8,128)S(1)}) custom-call(f32[64,2048]{1,0:T(8,128)} %candidates_from.1, s32[1,256]{1,0:T(1,128)} %bitcast.1, f32[64,64,256]{2,1,0:T(8,128)} %inv.1, f32[64,64,256]{2,1,0:T(8,128)S(1)} %collective-permute-done.inv_from), custom_call_target="tpu_custom_call" | custom-call | flops 100000000 | bytes 5000000 | tf_op jit(solution)/shard_map/setup/pallas_call | solution.py:77
  31.3 1.1 collective-permute-done.3.t2
  32.4 2.5 %collective-permute-done.4.t3 = f32[2,64,128]{2,1,0:T(8,128)S(1)} collective-permute-done((f32[2,64,128]{2,1,0:T(8,128)S(1)}, f32[2,64,128]{2,1,0:T(8,128)S(1)}, u32[]{:S(2)}, u32[]{:S(2)}) %collective-permute-start.4) | collective-permute-done | bytes 65568 | tf_op jit(solution)/shard_map/ppermute | solution.py:323
  35.0 0.1 collective-permute-start.5
  35.1 1.6 %collective-permute-done.5.refs_2_ = f32[576,128]{1,0:T(8,128)S(1)} collective-permute-done((f32[576,128]{1,0:T(8,128)S(1)}, f32[576,128]{1,0:T(8,128)S(1)}, u32[]{:S(2)}, u32[]{:S(2)}) %collective-permute-start.5) | collective-permute-done | bytes 294944 | tf_op jit(solution)/shard_map/ppermute | solution.py:326
  36.6 0.1 solve_step.8
  36.7 0.8 collective-permute-start.6
  37.5 0.2 copy-done
  37.8 0.0 collective-permute-start.32
  37.8 0.9 collective-permute-start.33
  38.7 1.2 collective-permute-start.34
  39.9 2.6 %collective-permute-start.35 = (bf16[3072,128]{1,0:T(8,128)(2,1)S(1)}, bf16[3072,128]{1,0:T(8,128)(2,1)S(1)}, u32[]{:S(2)}, u32[]{:S(2)}) collective-permute-start(bf16[3072,128]{1,0:T(8,128)(2,1)S(1)} %collective-permute-done.31.v1), channel_id=1, source_target_pairs={{0,6},{1,7},{2,4},{3,5},{4,2},{5,3},{6,0},{7,1},{8,14},{9,15},{10,... | collective-permute-start | bytes 2359304 | tf_op jit(solution)/shard_map/ppermute | solution.py:323
  42.5 0.7 collective-permute-start.8
  43.2 0.7 collective-permute-start.9
  43.9 0.7 collective-permute-start.7
  44.6 0.7 collective-permute-start.11
  45.3 0.7 collective-permute-start.12
  46.0 0.7 collective-permute-start.10
  46.7 0.7 collective-permute-start.14
  47.3 1.3 collective-permute-start.15
  48.7 18.2 %collective-permute-done.15.refs_5_ = bf16[128,128]{1,0:T(8,128)(2,1)S(1)} collective-permute-done((bf16[128,128]{1,0:T(8,128)(2,1)S(1)}, bf16[128,128]{1,0:T(8,128)(2,1)S(1)}, u32[]{:S(2)}, u32[]{:S(2)}) %collective-permute-start.15) | collective-permute-done | bytes 32800 | tf_op jit(solution)/shard_map/ppermute | solution.py:326
  67.0 1.3 collective-permute-start.17
  68.2 6.0 %collective-permute-done.17.refs_4_ = bf16[128,128]{1,0:T(8,128)(2,1)S(1)} collective-permute-done((bf16[128,128]{1,0:T(8,128)(2,1)S(1)}, bf16[128,128]{1,0:T(8,128)(2,1)S(1)}, u32[]{:S(2)}, u32[]{:S(2)}) %collective-permute-start.17) | collective-permute-done | bytes 32800 | tf_op jit(solution)/shard_map/ppermute | solution.py:326
  74.3 0.7 collective-permute-start.13
  75.0 1.3 collective-permute-start.18
  76.3 0.2 solve_step.12
  76.4 6.7 %collective-permute-done.18.refs_5_ = bf16[128,128]{1,0:T(8,128)(2,1)S(1)} collective-permute-done((bf16[128,128]{1,0:T(8,128)(2,1)S(1)}, bf16[128,128]{1,0:T(8,128)(2,1)S(1)}, u32[]{:S(2)}, u32[]{:S(2)}) %collective-permute-start.18) | collective-permute-done | bytes 32800 | tf_op jit(solution)/shard_map/ppermute | solution.py:326
  83.2 1.3 collective-permute-start.20
  84.5 6.6 %collective-permute-done.20.refs_4_ = bf16[128,128]{1,0:T(8,128)(2,1)S(1)} collective-permute-done((bf16[128,128]{1,0:T(8,128)(2,1)S(1)}, bf16[128,128]{1,0:T(8,128)(2,1)S(1)}, u32[]{:S(2)}, u32[]{:S(2)}) %collective-permute-start.20) | collective-permute-done | bytes 32800 | tf_op jit(solution)/shard_map/ppermute | solution.py:326
  91.0 0.7 collective-permute-start.16
  91.7 1.3 collective-permute-start.21
  93.0 0.5 solve_step.13
  93.5 7.0 %collective-permute-done.21.refs_5_ = bf16[128,128]{1,0:T(8,128)(2,1)S(1)} collective-permute-done((bf16[128,128]{1,0:T(8,128)(2,1)S(1)}, bf16[128,128]{1,0:T(8,128)(2,1)S(1)}, u32[]{:S(2)}, u32[]{:S(2)}) %collective-permute-start.21) | collective-permute-done | bytes 32800 | tf_op jit(solution)/shard_map/ppermute | solution.py:326
  100.5 0.7 collective-permute-start.19
  101.2 1.3 collective-permute-start.23
  102.5 0.3 solve_step.14
  102.8 4.2 %collective-permute-done.23.refs_4_ = bf16[128,128]{1,0:T(8,128)(2,1)S(1)} collective-permute-done((bf16[128,128]{1,0:T(8,128)(2,1)S(1)}, bf16[128,128]{1,0:T(8,128)(2,1)S(1)}, u32[]{:S(2)}, u32[]{:S(2)}) %collective-permute-start.23) | collective-permute-done | bytes 32800 | tf_op jit(solution)/shard_map/ppermute | solution.py:326
  107.0 1.3 collective-permute-start.22
  108.3 4.7 %collective-permute-done.22.refs_3_ = bf16[192,128]{1,0:T(8,128)(2,1)S(1)} collective-permute-done((bf16[192,128]{1,0:T(8,128)(2,1)S(1)}, bf16[192,128]{1,0:T(8,128)(2,1)S(1)}, u32[]{:S(2)}, u32[]{:S(2)}) %collective-permute-start.22) | collective-permute-done | bytes 49184 | tf_op jit(solution)/shard_map/ppermute | solution.py:326
  113.0 0.9 solve_step.15
  113.8 0.1 collective-permute-start.24
  113.9 3.9 %collective-permute-done.24.refs_1_ = bf16[128,128]{1,0:T(8,128)(2,1)S(1)} collective-permute-done((bf16[128,128]{1,0:T(8,128)(2,1)S(1)}, bf16[128,128]{1,0:T(8,128)(2,1)S(1)}, u32[]{:S(2)}, u32[]{:S(2)}) %collective-permute-start.24) | collective-permute-done | bytes 32800 | tf_op jit(solution)/shard_map/ppermute | solution.py:326
  117.9 0.1 collective-permute-start.30
  118.0 0.3 collective-permute-start.36
  118.3 1.8 %collective-permute-start.37 = (bf16[1536,128]{1,0:T(8,128)(2,1)S(1)}, bf16[1536,128]{1,0:T(8,128)(2,1)S(1)}, u32[]{:S(2)}, u32[]{:S(2)}) collective-permute-start(bf16[1536,128]{1,0:T(8,128)(2,1)S(1)} %slice.13), channel_id=1, source_target_pairs={{0,6},{1,7},{2,4},{3,5},{4,2},{5,3},{6,0},{7,1},{8,14},{9,15},{10,... | collective-permute-start | bytes 1179656 | tf_op jit(solution)/shard_map/ppermute | solution.py:323
  120.2 0.5 collective-permute-start.38
  120.7 1.4 %collective-permute-done.25.refs_0_.far1 = bf16[2,128,128]{2,1,0:T(8,128)(2,1)S(1)} collective-permute-done((bf16[2,128,128]{2,1,0:T(8,128)(2,1)S(1)}, bf16[2,128,128]{2,1,0:T(8,128)(2,1)S(1)}, u32[]{:S(2)}, u32[]{:S(2)}) %collective-permute-start.25) | collective-permute-done | bytes 65568 | tf_op jit(solution)/shard_map/ppermute | solution.py:326
  122.1 0.9 collective-permute-start.39
  123.0 2.9 %collective-permute-done.26.refs_1_.far2 = bf16[2,128,128]{2,1,0:T(8,128)(2,1)S(1)} collective-permute-done((bf16[2,128,128]{2,1,0:T(8,128)(2,1)S(1)}, bf16[2,128,128]{2,1,0:T(8,128)(2,1)S(1)}, u32[]{:S(2)}, u32[]{:S(2)}) %collective-permute-start.26) | collective-permute-done | bytes 65568 | tf_op jit(solution)/shard_map/ppermute | solution.py:326
  125.9 1.7 %collective-permute-start.27 = (bf16[2,128,128]{2,1,0:T(8,128)(2,1)S(1)}, bf16[2,128,128]{2,1,0:T(8,128)(2,1)S(1)}, u32[]{:S(2)}, u32[]{:S(2)}) collective-permute-start(bf16[2,128,128]{2,1,0:T(8,128)(2,1)S(1)} %stack.4.pair), channel_id=1, source_target_pairs={{0,96},{8,104},{16,112},{24,120},{32,64},{40,72},{48,80},{56,88},{... | collective-permute-start | bytes 196616 | tf_op jit(solution)/shard_map/ppermute | solution.py:326
  127.6 3.7 %collective-permute-done.27.refs_2_.far3 = bf16[2,128,128]{2,1,0:T(8,128)(2,1)S(1)} collective-permute-done((bf16[2,128,128]{2,1,0:T(8,128)(2,1)S(1)}, bf16[2,128,128]{2,1,0:T(8,128)(2,1)S(1)}, u32[]{:S(2)}, u32[]{:S(2)}) %collective-permute-start.27) | collective-permute-done | bytes 65568 | tf_op jit(solution)/shard_map/ppermute | solution.py:326
  131.4 1.2 collective-permute-done.28.pair_swap
  132.6 0.2 collective-permute-start.29
  132.8 1.3 collective-permute-done.29.far_swap
  134.1 4.0 %collective-permute-done.38.a5 = bf16[1536,128]{1,0:T(8,128)(2,1)S(1)} collective-permute-done((bf16[1536,128]{1,0:T(8,128)(2,1)S(1)}, bf16[1536,128]{1,0:T(8,128)(2,1)S(1)}, u32[]{:S(2)}, u32[]{:S(2)}) %collective-permute-start.38) | collective-permute-done | bytes 393248 | tf_op jit(solution)/shard_map/ppermute | solution.py:323
  138.0 1.3 collective-permute-done.39.b5
  139.4 3.0 %back_transform.1 = (bf16[3072,256]{1,0:T(8,128)(2,1)}, f32[64,256]{1,0:T(8,128)}) custom-call(bf16[2,128,128]{2,1,0:T(8,128)(2,1)S(1)} %stack.4.pair, bf16[2,128,128]{2,1,0:T(8,128)(2,1)S(1)} %collective-permute-done.25.refs_0_.far1, bf16[2,128,128]{2,1,0:T(8,128)(2,1)S(1)} %collective-permute-done.26.refs_1_.far2, ...), custom_call_target="tpu_custom_call" | custom-call | flops 1610612736 | bytes 8000000 | tf_op jit(solution)/shard_map/back_transform/pallas_call | solution.py:305
  (38 shorter events, 0.3 us)
Async XLA Ops:
  0.6 28.8 %collective-permute-start = (f32[64,64,256]{2,1,0:T(8,128)}, f32[64,64,256]{2,1,0:T(8,128)S(1)}, u32[]{:S(2)}, u32[]{:S(2)}) collective-permute-start(f32[64,64,256]{2,1,0:T(8,128)} %inv.1), channel_id=1, source_target_pairs={{0,8},{8,0},{16,24},{24,16},{32,40},{40,32},{48,56},{56,48},{64,72... | collective-permute-start | bytes 12582920 | tf_op jit(solution)/shard_map/ppermute | solution.py:326
  0.7 37.9 %collective-permute-start.31 = (bf16[3072,128]{1,0:T(8,128)(2,1)}, bf16[3072,128]{1,0:T(8,128)(2,1)S(1)}, u32[]{:S(2)}, u32[]{:S(2)}) collective-permute-start(bf16[3072,128]{1,0:T(8,128)(2,1)} %v0.1), channel_id=1, source_target_pairs={{0,1},{1,0},{2,3},{3,2},{4,5},{5,4},{6,7},{7,6},{8,9},{9,8},{10,11... | collective-permute-start | bytes 2359304 | tf_op jit(solution)/shard_map/ppermute | solution.py:323
  3.9 19.1 %collective-permute-start.1 = (f32[64,128]{1,0:T(8,128)}, f32[64,128]{1,0:T(8,128)S(1)}, u32[]{:S(2)}, u32[]{:S(2)}) collective-permute-start(f32[64,128]{1,0:T(8,128)} %refs_0_.1), channel_id=1, source_target_pairs={{0,1},{1,0},{2,3},{3,2},{4,5},{5,4},{6,7},{7,6},{8,9},{9,8},{10,11... | collective-permute-start | bytes 98312 | tf_op jit(solution)/shard_map/ppermute | solution.py:323
  23.1 0.8 copy-start.1
  23.8 7.5 %collective-permute-start.2 = (f32[2,64,128]{2,1,0:T(8,128)S(1)}, f32[2,64,128]{2,1,0:T(8,128)S(1)}, u32[]{:S(2)}, u32[]{:S(2)}) collective-permute-start(f32[2,64,128]{2,1,0:T(8,128)S(1)} %stack.3.t0), channel_id=1, source_target_pairs={{0,2},{1,3},{2,0},{3,1},{4,6},{5,7},{6,4},{7,5},{8,10},{9,11},{10,... | collective-permute-start | bytes 196616 | tf_op jit(solution)/shard_map/ppermute | solution.py:323
  25.9 6.5 %collective-permute-start.3 = (f32[2,64,128]{2,1,0:T(8,128)S(1)}, f32[2,64,128]{2,1,0:T(8,128)S(1)}, u32[]{:S(2)}, u32[]{:S(2)}) collective-permute-start(f32[2,64,128]{2,1,0:T(8,128)S(1)} %stack.3.t0), channel_id=1, source_target_pairs={{0,4},{1,5},{2,6},{3,7},{4,0},{5,1},{6,2},{7,3},{8,12},{9,13},{10,... | collective-permute-start | bytes 196616 | tf_op jit(solution)/shard_map/ppermute | solution.py:323
  29.5 5.5 %collective-permute-start.4 = (f32[2,64,128]{2,1,0:T(8,128)S(1)}, f32[2,64,128]{2,1,0:T(8,128)S(1)}, u32[]{:S(2)}, u32[]{:S(2)}) collective-permute-start(f32[2,64,128]{2,1,0:T(8,128)S(1)} %stack.3.t0), channel_id=1, source_target_pairs={{0,6},{1,7},{2,4},{3,5},{4,2},{5,3},{6,0},{7,1},{8,14},{9,15},{10,... | collective-permute-start | bytes 196616 | tf_op jit(solution)/shard_map/ppermute | solution.py:323
  35.0 1.7 %collective-permute-start.5 = (f32[576,128]{1,0:T(8,128)S(1)}, f32[576,128]{1,0:T(8,128)S(1)}, u32[]{:S(2)}, u32[]{:S(2)}) collective-permute-start(f32[576,128]{1,0:T(8,128)S(1)} %join.1.refs_1_), channel_id=1, source_target_pairs={{0,8},{8,0},{16,24},{24,16},{32,40},{40,32},{48,56},{56,48},{64,72... | collective-permute-start | bytes 884744 | tf_op jit(solution)/shard_map/ppermute | solution.py:326
  36.6 1.1 copy-start
  36.7 1.9 %collective-permute-start.6 = (bf16[128,128]{1,0:T(8,128)(2,1)S(1)}, bf16[128,128]{1,0:T(8,128)(2,1)S(1)}, u32[]{:S(2)}, u32[]{:S(2)}) collective-permute-start(bf16[128,128]{1,0:T(8,128)(2,1)S(1)} %get-tuple-element.46.refs_2_), channel_id=1, source_target_pairs={{112,96},{120,104},{113,97},{121,105},{114,98},{122,106},{115,99},... | collective-permute-start | bytes 98312 | tf_op jit(solution)/shard_map/ppermute | solution.py:326
  37.8 80.1 %collective-permute-start.32 = (bf16[3072,128]{1,0:T(8,128)(2,1)S(1)}, bf16[3072,128]{1,0:T(8,128)(2,1)S(1)}, u32[]{:S(2)}, u32[]{:S(2)}) collective-permute-start(bf16[3072,128]{1,0:T(8,128)(2,1)S(1)} %copy-done), channel_id=1, source_target_pairs={{0,2},{1,3},{2,0},{3,1},{4,6},{5,7},{6,4},{7,5},{8,10},{9,11},{10,... | collective-permute-start | bytes 2359304 | tf_op jit(solution)/shard_map/ppermute | solution.py:323
  37.8 80.2 %collective-permute-start.33 = (bf16[3072,128]{1,0:T(8,128)(2,1)S(1)}, bf16[3072,128]{1,0:T(8,128)(2,1)S(1)}, u32[]{:S(2)}, u32[]{:S(2)}) collective-permute-start(bf16[3072,128]{1,0:T(8,128)(2,1)S(1)} %copy-done), channel_id=1, source_target_pairs={{0,6},{1,7},{2,4},{3,5},{4,2},{5,3},{6,0},{7,1},{8,14},{9,15},{10,... | collective-permute-start | bytes 2359304 | tf_op jit(solution)/shard_map/ppermute | solution.py:323
  38.7 79.7 %collective-permute-start.34 = (bf16[3072,128]{1,0:T(8,128)(2,1)S(1)}, bf16[3072,128]{1,0:T(8,128)(2,1)S(1)}, u32[]{:S(2)}, u32[]{:S(2)}) collective-permute-start(bf16[3072,128]{1,0:T(8,128)(2,1)S(1)} %collective-permute-done.31.v1), channel_id=1, source_target_pairs={{0,2},{1,3},{2,0},{3,1},{4,6},{5,7},{6,4},{7,5},{8,10},{9,11},{10,... | collective-permute-start | bytes 2359304 | tf_op jit(solution)/shard_map/ppermute | solution.py:323
  39.9 80.2 %collective-permute-start.35 = (bf16[3072,128]{1,0:T(8,128)(2,1)S(1)}, bf16[3072,128]{1,0:T(8,128)(2,1)S(1)}, u32[]{:S(2)}, u32[]{:S(2)}) collective-permute-start(bf16[3072,128]{1,0:T(8,128)(2,1)S(1)} %collective-permute-done.31.v1), channel_id=1, source_target_pairs={{0,6},{1,7},{2,4},{3,5},{4,2},{5,3},{6,0},{7,1},{8,14},{9,15},{10,... | collective-permute-start | bytes 2359304 | tf_op jit(solution)/shard_map/ppermute | solution.py:323
  42.5 0.7 collective-permute-start.8
  43.2 0.7 collective-permute-start.9
  43.9 0.7 collective-permute-start.7
  44.6 0.7 collective-permute-start.11
  45.3 0.7 collective-permute-start.12
  46.0 0.7 collective-permute-start.10
  46.7 0.7 collective-permute-start.14
  47.3 19.6 %collective-permute-start.15 = (bf16[128,128]{1,0:T(8,128)(2,1)S(1)}, bf16[128,128]{1,0:T(8,128)(2,1)S(1)}, u32[]{:S(2)}, u32[]{:S(2)}) collective-permute-start(bf16[128,128]{1,0:T(8,128)(2,1)S(1)} %get-tuple-element.53.refs_2_), channel_id=1, source_target_pairs={{80,32},{88,40},{96,16},{104,24},{112,0},{120,8},{81,33},{89,41},{... | collective-permute-start | bytes 98312 | tf_op jit(solution)/shard_map/ppermute | solution.py:326
  67.0 7.3 %collective-permute-start.17 = (bf16[128,128]{1,0:T(8,128)(2,1)S(1)}, bf16[128,128]{1,0:T(8,128)(2,1)S(1)}, u32[]{:S(2)}, u32[]{:S(2)}) collective-permute-start(bf16[128,128]{1,0:T(8,128)(2,1)S(1)} %get-tuple-element.56.refs_2_), channel_id=1, source_target_pairs={{64,32},{72,40},{80,16},{88,24},{96,0},{104,8},{65,33},{73,41},{81... | collective-permute-start | bytes 98312 | tf_op jit(solution)/shard_map/ppermute | solution.py:326
  74.3 0.7 collective-permute-start.13
  75.0 8.2 %collective-permute-start.18 = (bf16[128,128]{1,0:T(8,128)(2,1)S(1)}, bf16[128,128]{1,0:T(8,128)(2,1)S(1)}, u32[]{:S(2)}, u32[]{:S(2)}) collective-permute-start(bf16[128,128]{1,0:T(8,128)(2,1)S(1)} %get-tuple-element.56.refs_2_), channel_id=1, source_target_pairs={{64,16},{72,24},{80,0},{88,8},{65,17},{73,25},{81,1},{89,9},{66,18... | collective-permute-start | bytes 98312 | tf_op jit(solution)/shard_map/ppermute | solution.py:326
  83.2 7.9 %collective-permute-start.20 = (bf16[128,128]{1,0:T(8,128)(2,1)S(1)}, bf16[128,128]{1,0:T(8,128)(2,1)S(1)}, u32[]{:S(2)}, u32[]{:S(2)}) collective-permute-start(bf16[128,128]{1,0:T(8,128)(2,1)S(1)} %get-tuple-element.60.refs_2_), channel_id=1, source_target_pairs={{48,16},{56,24},{64,0},{72,8},{49,17},{57,25},{65,1},{73,9},{50,18... | collective-permute-start | bytes 98312 | tf_op jit(solution)/shard_map/ppermute | solution.py:326
  91.0 0.7 collective-permute-start.16
  91.7 8.8 %collective-permute-start.21 = (bf16[128,128]{1,0:T(8,128)(2,1)S(1)}, bf16[128,128]{1,0:T(8,128)(2,1)S(1)}, u32[]{:S(2)}, u32[]{:S(2)}) collective-permute-start(bf16[128,128]{1,0:T(8,128)(2,1)S(1)} %get-tuple-element.60.refs_2_), channel_id=1, source_target_pairs={{48,0},{56,8},{49,1},{57,9},{50,2},{58,10},{51,3},{59,11},{52,4},{... | collective-permute-start | bytes 98312 | tf_op jit(solution)/shard_map/ppermute | solution.py:326
  100.5 0.7 collective-permute-start.19
  101.2 5.8 %collective-permute-start.23 = (bf16[128,128]{1,0:T(8,128)(2,1)S(1)}, bf16[128,128]{1,0:T(8,128)(2,1)S(1)}, u32[]{:S(2)}, u32[]{:S(2)}) collective-permute-start(bf16[128,128]{1,0:T(8,128)(2,1)S(1)} %get-tuple-element.64.refs_2_), channel_id=1, source_target_pairs={{32,0},{40,8},{33,1},{41,9},{34,2},{42,10},{35,3},{43,11},{36,4},{... | collective-permute-start | bytes 98312 | tf_op jit(solution)/shard_map/ppermute | solution.py:326
  107.0 6.0 %collective-permute-start.22 = (bf16[192,128]{1,0:T(8,128)(2,1)S(1)}, bf16[192,128]{1,0:T(8,128)(2,1)S(1)}, u32[]{:S(2)}, u32[]{:S(2)}) collective-permute-start(bf16[192,128]{1,0:T(8,128)(2,1)S(1)} %get-tuple-element.69), channel_id=1, source_target_pairs={{16,0},{24,8},{17,1},{25,9},{18,2},{26,10},{19,3},{27,11},{20,4},{... | collective-permute-start | bytes 147464 | tf_op jit(solution)/shard_map/ppermute | solution.py:326
  113.8 4.0 %collective-permute-start.24 = (bf16[128,128]{1,0:T(8,128)(2,1)S(1)}, bf16[128,128]{1,0:T(8,128)(2,1)S(1)}, u32[]{:S(2)}, u32[]{:S(2)}) collective-permute-start(bf16[128,128]{1,0:T(8,128)(2,1)S(1)} %get-tuple-element.70.refs_0_), channel_id=1, source_target_pairs={{0,16},{8,24},{16,0},{24,8},{32,48},{40,56},{48,32},{56,40},{64,80... | collective-permute-start | bytes 98312 | tf_op jit(solution)/shard_map/ppermute | solution.py:326
  117.8 4.3 %collective-permute-start.25 = (bf16[2,128,128]{2,1,0:T(8,128)(2,1)S(1)}, bf16[2,128,128]{2,1,0:T(8,128)(2,1)S(1)}, u32[]{:S(2)}, u32[]{:S(2)}) collective-permute-start(bf16[2,128,128]{2,1,0:T(8,128)(2,1)S(1)} %stack.4.pair), channel_id=1, source_target_pairs={{0,32},{8,40},{16,48},{24,56},{32,0},{40,8},{48,16},{56,24},{64,96... | collective-permute-start | bytes 196616 | tf_op jit(solution)/shard_map/ppermute | solution.py:326
  117.9 2.3 %collective-permute-start.30 = (f32[64,128]{1,0:T(8,128)S(1)}, f32[64,128]{1,0:T(8,128)S(1)}, u32[]{:S(2)}, u32[]{:S(2)}) collective-permute-start(f32[64,128]{1,0:T(8,128)S(1)} %get-tuple-element.72), channel_id=1, source_target_pairs={{0,8},{8,0},{16,24},{24,16},{32,40},{40,32},{48,56},{56,48},{64,72... | collective-permute-start | bytes 98312 | tf_op jit(solution)/shard_map/ppermute | solution.py:326
  118.0 14.8 %collective-permute-start.36 = (bf16[1536,128]{1,0:T(8,128)(2,1)S(1)}, bf16[1536,128]{1,0:T(8,128)(2,1)S(1)}, u32[]{:S(2)}, u32[]{:S(2)}) collective-permute-start(bf16[1536,128]{1,0:T(8,128)(2,1)S(1)} %slice.12), channel_id=1, source_target_pairs={{0,2},{1,3},{2,0},{3,1},{4,6},{5,7},{6,4},{7,5},{8,10},{9,11},{10,... | collective-permute-start | bytes 1179656 | tf_op jit(solution)/shard_map/ppermute | solution.py:323
  118.3 14.4 %collective-permute-start.37 = (bf16[1536,128]{1,0:T(8,128)(2,1)S(1)}, bf16[1536,128]{1,0:T(8,128)(2,1)S(1)}, u32[]{:S(2)}, u32[]{:S(2)}) collective-permute-start(bf16[1536,128]{1,0:T(8,128)(2,1)S(1)} %slice.13), channel_id=1, source_target_pairs={{0,6},{1,7},{2,4},{3,5},{4,2},{5,3},{6,0},{7,1},{8,14},{9,15},{10,... | collective-permute-start | bytes 1179656 | tf_op jit(solution)/shard_map/ppermute | solution.py:323
  120.1 5.8 %collective-permute-start.26 = (bf16[2,128,128]{2,1,0:T(8,128)(2,1)S(1)}, bf16[2,128,128]{2,1,0:T(8,128)(2,1)S(1)}, u32[]{:S(2)}, u32[]{:S(2)}) collective-permute-start(bf16[2,128,128]{2,1,0:T(8,128)(2,1)S(1)} %stack.4.pair), channel_id=1, source_target_pairs={{0,64},{8,72},{16,80},{24,88},{32,96},{40,104},{48,112},{56,120},{... | collective-permute-start | bytes 196616 | tf_op jit(solution)/shard_map/ppermute | solution.py:326
  120.2 17.8 %collective-permute-start.38 = (bf16[1536,128]{1,0:T(8,128)(2,1)S(1)}, bf16[1536,128]{1,0:T(8,128)(2,1)S(1)}, u32[]{:S(2)}, u32[]{:S(2)}) collective-permute-start(bf16[1536,128]{1,0:T(8,128)(2,1)S(1)} %slice.14), channel_id=1, source_target_pairs={{0,2},{1,3},{2,0},{3,1},{4,6},{5,7},{6,4},{7,5},{8,10},{9,11},{10,... | collective-permute-start | bytes 1179656 | tf_op jit(solution)/shard_map/ppermute | solution.py:323
  122.1 17.3 %collective-permute-start.39 = (bf16[1536,128]{1,0:T(8,128)(2,1)S(1)}, bf16[1536,128]{1,0:T(8,128)(2,1)S(1)}, u32[]{:S(2)}, u32[]{:S(2)}) collective-permute-start(bf16[1536,128]{1,0:T(8,128)(2,1)S(1)} %slice.15), channel_id=1, source_target_pairs={{0,6},{1,7},{2,4},{3,5},{4,2},{5,3},{6,0},{7,1},{8,14},{9,15},{10,... | collective-permute-start | bytes 1179656 | tf_op jit(solution)/shard_map/ppermute | solution.py:323
  125.9 5.5 %collective-permute-start.27 = (bf16[2,128,128]{2,1,0:T(8,128)(2,1)S(1)}, bf16[2,128,128]{2,1,0:T(8,128)(2,1)S(1)}, u32[]{:S(2)}, u32[]{:S(2)}) collective-permute-start(bf16[2,128,128]{2,1,0:T(8,128)(2,1)S(1)} %stack.4.pair), channel_id=1, source_target_pairs={{0,96},{8,104},{16,112},{24,120},{32,64},{40,72},{48,80},{56,88},{... | collective-permute-start | bytes 196616 | tf_op jit(solution)/shard_map/ppermute | solution.py:326
  131.4 1.3 collective-permute-start.28
  132.6 1.4 %collective-permute-start.29 = (bf16[6,128,128]{2,1,0:T(8,128)(2,1)S(1)}, bf16[6,128,128]{2,1,0:T(8,128)(2,1)S(1)}, u32[]{:S(2)}, u32[]{:S(2)}) collective-permute-start(bf16[6,128,128]{2,1,0:T(8,128)(2,1)S(1)} %stack.5), channel_id=1, source_target_pairs={{0,8},{8,0},{16,24},{24,16},{32,40},{40,32},{48,56},{56,48},{64,72... | collective-permute-start | bytes 589832 | tf_op jit(solution)/shard_map/ppermute | solution.py:326
